TPU v7x, 32 devices: a whole 2x2x4 slice. The times are simulated.
32 devices in a mesh: dp: 8 (over z, y), ctx: 4 (over x, core).
Axes of the slice: x: 2, y: 2, z: 4, core: 2. Of those that a mesh axis runs over, the one named last changes fastest.
Arguments:
- layer_input: bfloat16 [16, 1024, 1600], P('dp', 'ctx'), may hold values from -6 to 6
- grad_out: bfloat16 [16, 1024, 1600], P('dp', 'ctx'), may hold values from -6 to 6
- segment_ids: int32 [16, 1024], P('dp'), may hold values from 0 to 7, as said below
- qkv_weight: bfloat16 [1600, 4800], P('ctx', 'dp'), may hold values from -0.15625 to 0.15625
- q_bias: bfloat16 [1600], P('dp'), may hold values from -1.796875 to 1.796875
- v_bias: bfloat16 [1600], P('dp'), may hold values from -1.796875 to 1.796875
- out_weight: bfloat16 [1600, 1600], P('ctx', 'dp'), may hold values from -0.875 to 0.875
- out_bias: bfloat16 [1600], P('dp'), may hold values from -1.796875 to 1.796875
- fc_weight: bfloat16 [1600, 6400], P('ctx', 'dp'), may hold values from -0.15625 to 0.15625
- fc_bias: bfloat16 [6400], P('dp'), may hold values from -1.796875 to 1.796875
- proj_weight: bfloat16 [6400, 1600], P('ctx', 'dp'), may hold values from -0.078125 to 0.078125
- proj_bias: bfloat16 [1600], P('dp'), may hold values from -1.796875 to 1.796875
- ln1_gain: bfloat16 [1600], P('dp'), may hold values from 0.5 to 1.5
- ln1_bias: bfloat16 [1600], P('dp'), may hold values from -1.796875 to 1.796875
- ln2_gain: bfloat16 [1600], P('dp'), may hold values from 0.5 to 1.5
- ln2_bias: bfloat16 [1600], P('dp'), may hold values from -1.796875 to 1.796875
Outputs:
- output: bfloat16 [16, 1024, 1600], P('dp', 'ctx')
- input_grad: float32 [16, 1024, 1600], P('dp', 'ctx')
- qkv_weight_grad: float32 [1600, 4800], P('ctx', 'dp')
- q_bias_grad: float32 [1600], P('dp')
- v_bias_grad: float32 [1600], P('dp')
- out_weight_grad: float32 [1600, 1600], P('ctx', 'dp')
- out_bias_grad: float32 [1600], P('dp')
- fc_weight_grad: float32 [1600, 6400], P('ctx', 'dp')
- fc_bias_grad: float32 [6400], P('dp')
- proj_weight_grad: float32 [6400, 1600], P('ctx', 'dp')
- proj_bias_grad: float32 [1600], P('dp')
- ln1_gain_grad: float32 [1600], P('dp')
- ln1_bias_grad: float32 [1600], P('dp')
- ln2_gain_grad: float32 [1600], P('dp')
- ln2_bias_grad: float32 [1600], P('dp')
Inputs may be any that keep to these rules, and one draw needn't show every extreme that they name: `segment_ids`: ids start at 0 in every sequence, never fall along it, and rise by at most one from one position to the next.
All inputs are finite; a program needn't handle non-finite values.
Results may differ from a plain program's by a relative error of at most 0.012.
Values may be sent and summed in bfloat16 or wider, within the bound.
A program may use at most 384 MiB of HBM per device.

v0:
```python
import jax
import jax.numpy as jnp
from jax import lax
from jax.sharding import PartitionSpec as P

HEADS = 25
HEAD_DIM = 64
FF = 6400
MB = 2


EPS = 1e-05
NEG_FILL = -1e30


def layer_norm(values, gain, shift):
    center = values - jnp.mean(values, axis=-1, keepdims=True)
    factor = lax.rsqrt(jnp.mean(center * center, axis=-1, keepdims=True) + EPS)
    return center * factor * gain + shift


def gelu_tanh(values):
    return (
        0.5
        * values
        * (1.0 + jnp.tanh(0.7978845608028654 * (values + 0.044715 * values * values * values)))
    )


def gather_weights(qkv_weight, out_weight, fc_weight, proj_weight, vectors):
    rows_all = (
        lax.all_gather(qkv_weight, "ctx", axis=0, tiled=True),
        lax.all_gather(out_weight, "ctx", axis=0, tiled=True),
        lax.all_gather(fc_weight, "ctx", axis=0, tiled=True),
        lax.all_gather(proj_weight, "ctx", axis=0, tiled=True),
    )
    return (
        lax.all_gather(rows_all[0], "dp", axis=1, tiled=True),
        lax.all_gather(rows_all[1], "dp", axis=1, tiled=True),
        lax.all_gather(rows_all[2], "dp", axis=1, tiled=True),
        lax.all_gather(rows_all[3], "dp", axis=1, tiled=True),
        lax.all_gather(vectors[0], "dp", axis=0, tiled=True),
        lax.all_gather(vectors[1], "dp", axis=0, tiled=True),
        lax.all_gather(vectors[2], "dp", axis=0, tiled=True),
        lax.all_gather(vectors[3], "dp", axis=0, tiled=True),
        lax.all_gather(vectors[4], "dp", axis=0, tiled=True),
        lax.all_gather(vectors[5], "dp", axis=0, tiled=True),
        lax.all_gather(vectors[6], "dp", axis=0, tiled=True),
        lax.all_gather(vectors[7], "dp", axis=0, tiled=True),
        lax.all_gather(vectors[8], "dp", axis=0, tiled=True),
    )


def gather_pairs(key_rows, value_rows):
    return (
        lax.all_gather(key_rows, "ctx", axis=1, tiled=True),
        lax.all_gather(value_rows, "ctx", axis=1, tiled=True),
    )


def key_slice(full_rows, first_key, block_len):
    piece = lax.dynamic_slice_in_dim(full_rows, first_key, block_len, 1)
    return piece.reshape(piece.shape[0], block_len, HEADS, HEAD_DIM)


def block_scores(queries, key_block, first_key, query_pos, query_seg, segments):
    block_len = key_block.shape[1]
    scores = (
        jnp.einsum("schd,skhd->shck", queries, key_block, preferred_element_type=jnp.float32)
        * 0.125
    )
    key_pos = first_key + jnp.arange(block_len, dtype=jnp.int32)
    key_seg = lax.dynamic_slice_in_dim(segments, first_key, block_len, 1)
    allowed = (key_pos[None, None, :] <= query_pos[None, :, None]) & (
        key_seg[:, None, :] == query_seg[:, :, None]
    )
    return (scores, allowed[:, None, :, :])


def block_length():
    return 256


def attend(queries, key_full, value_full, query_pos, query_seg, segments):
    seq_group, row_count, head_count, head_size = queries.shape
    length = key_full.shape[1]
    block_len = block_length()

    def stats_step(block_index, carry):
        running_max, running_sum = carry
        first_key = block_index * block_len
        scores, allowed = block_scores(
            queries,
            key_slice(key_full, first_key, block_len),
            first_key,
            query_pos,
            query_seg,
            segments,
        )
        masked = jnp.where(allowed, scores, NEG_FILL)
        new_max = jnp.maximum(running_max, jnp.max(masked, axis=-1))
        weights_now = jnp.where(allowed, jnp.exp(masked - new_max[..., None]), 0.0)
        return (
            new_max,
            running_sum * jnp.exp(running_max - new_max) + jnp.sum(weights_now, axis=-1),
        )

    start_max = jnp.full((seq_group, head_count, row_count), NEG_FILL, jnp.float32)
    running_max, running_sum = lax.fori_loop(
        0, length // block_len, stats_step, (start_max, jnp.zeros_like(start_max))
    )
    log_total = running_max + jnp.log(running_sum)

    def output_step(block_index, summed):
        first_key = block_index * block_len
        scores, allowed = block_scores(
            queries,
            key_slice(key_full, first_key, block_len),
            first_key,
            query_pos,
            query_seg,
            segments,
        )
        attn_weights = jnp.where(allowed, jnp.exp(scores - log_total[..., None]), 0.0).astype(
            jnp.bfloat16
        )
        return summed + jnp.einsum(
            "shck,skhd->schd",
            attn_weights,
            key_slice(value_full, first_key, block_len),
            preferred_element_type=jnp.float32,
        )

    summed = lax.fori_loop(
        0,
        length // block_len,
        output_step,
        jnp.zeros((seq_group, row_count, head_count, head_size), jnp.float32),
    )
    return (summed, log_total)


def attend_back(
    queries, key_full, value_full, attended_grad, log_total, query_pos, query_seg, segments
):
    seq_group, row_count, head_count, head_size = queries.shape
    length = key_full.shape[1]
    block_len = block_length()

    def delta_step(block_index, row_delta):
        first_key = block_index * block_len
        scores, allowed = block_scores(
            queries,
            key_slice(key_full, first_key, block_len),
            first_key,
            query_pos,
            query_seg,
            segments,
        )
        attn_weights = jnp.where(allowed, jnp.exp(scores - log_total[..., None]), 0.0)
        pushed = jnp.einsum(
            "schd,skhd->shck",
            attended_grad,
            key_slice(value_full, first_key, block_len),
            preferred_element_type=jnp.float32,
        )
        return row_delta + jnp.sum(attn_weights * pushed, axis=-1)

    row_delta = lax.fori_loop(
        0,
        length // block_len,
        delta_step,
        jnp.zeros((seq_group, head_count, row_count), jnp.float32),
    )

    def grad_step(block_index, carry):
        query_grad, key_grad, value_grad = carry
        first_key = block_index * block_len
        key_block = key_slice(key_full, first_key, block_len)
        scores, allowed = block_scores(
            queries, key_block, first_key, query_pos, query_seg, segments
        )
        attn_weights = jnp.where(allowed, jnp.exp(scores - log_total[..., None]), 0.0)
        pushed = jnp.einsum(
            "schd,skhd->shck",
            attended_grad,
            key_slice(value_full, first_key, block_len),
            preferred_element_type=jnp.float32,
        )
        score_grad = (attn_weights * (pushed - row_delta[..., None])).astype(jnp.bfloat16)
        query_grad = query_grad + 0.125 * jnp.einsum(
            "shck,skhd->schd", score_grad, key_block, preferred_element_type=jnp.float32
        )
        key_piece = 0.125 * jnp.einsum(
            "shck,schd->skhd", score_grad, queries, preferred_element_type=jnp.float32
        )
        value_piece = jnp.einsum(
            "shck,schd->skhd",
            attn_weights.astype(jnp.bfloat16),
            attended_grad,
            preferred_element_type=jnp.float32,
        )
        key_grad = lax.dynamic_update_slice_in_dim(
            key_grad, key_piece.reshape(seq_group, block_len, head_count * head_size), first_key, 1
        )
        value_grad = lax.dynamic_update_slice_in_dim(
            value_grad,
            value_piece.reshape(seq_group, block_len, head_count * head_size),
            first_key,
            1,
        )
        return (query_grad, key_grad, value_grad)

    full_zero = jnp.zeros((seq_group, length, head_count * head_size), jnp.float32)
    start_carry = (
        jnp.zeros((seq_group, row_count, head_count, head_size), jnp.float32),
        full_zero,
        full_zero,
    )
    return lax.fori_loop(0, length // block_len, grad_step, start_carry)


def on_device(
    layer_input,
    grad_out,
    segment_ids,
    qkv_weight,
    q_bias,
    v_bias,
    out_weight,
    out_bias,
    fc_weight,
    fc_bias,
    proj_weight,
    proj_bias,
    ln1_gain,
    ln1_bias,
    ln2_gain,
    ln2_bias,
):
    vectors = (q_bias, v_bias, out_bias, fc_bias, proj_bias, ln1_gain, ln1_bias, ln2_gain, ln2_bias)
    seq_local, row_count, model_width = layer_input.shape
    seq_group = seq_local // MB
    token_count = seq_group * row_count
    ctx_count = lax.axis_size("ctx")
    ctx_index = lax.axis_index("ctx")
    query_pos = ctx_index * row_count + jnp.arange(row_count, dtype=jnp.int32)
    bf16 = jnp.bfloat16
    f32 = jnp.float32
    width_part = model_width // ctx_count
    hidden_part = FF // ctx_count
    matrix_grads = [
        jnp.zeros((width_part, 3 * model_width), f32),
        jnp.zeros((width_part, model_width), f32),
        jnp.zeros((width_part, FF), f32),
        jnp.zeros((hidden_part, model_width), f32),
    ]
    vector_grads = [
        jnp.zeros((model_width,), f32),
        jnp.zeros((model_width,), f32),
        jnp.zeros((model_width,), f32),
        jnp.zeros((FF,), f32),
        jnp.zeros((model_width,), f32),
        jnp.zeros((model_width,), f32),
        jnp.zeros((model_width,), f32),
        jnp.zeros((model_width,), f32),
        jnp.zeros((model_width,), f32),
    ]
    outputs = []
    input_grads = []
    for micro_step in range(MB):
        first_seq = micro_step * seq_group
        values = (
            layer_input[first_seq : first_seq + seq_group]
            .astype(f32)
            .reshape(token_count, model_width)
        )
        segments = segment_ids[first_seq : first_seq + seq_group]
        query_seg = lax.dynamic_slice_in_dim(segments, ctx_index * row_count, row_count, 1)
        gathered = gather_weights(qkv_weight, out_weight, fc_weight, proj_weight, vectors)
        gain_one = gathered[9].astype(f32)
        shift_one = gathered[10].astype(f32)
        gain_two = gathered[11].astype(f32)
        shift_two = gathered[12].astype(f32)
        normed1 = layer_norm(values, gain_one, shift_one).astype(bf16)
        joined_bias = jnp.concatenate(
            [gathered[4].astype(f32), jnp.zeros((model_width,), f32), gathered[5].astype(f32)]
        )
        projected = (
            jnp.dot(normed1, gathered[0], preferred_element_type=f32) + joined_bias
        ).astype(bf16)
        queries = projected[:, :model_width].reshape(seq_group, row_count, HEADS, HEAD_DIM)
        key_rows = projected[:, model_width : 2 * model_width].reshape(
            seq_group, row_count, model_width
        )
        value_rows = projected[:, 2 * model_width :].reshape(seq_group, row_count, model_width)
        key_full, value_full = gather_pairs(key_rows, value_rows)
        attended_full, log_total = attend(
            queries, key_full, value_full, query_pos, query_seg, segments
        )
        attended = attended_full.astype(bf16).reshape(token_count, model_width)
        hidden = (
            values
            + jnp.dot(attended, gathered[1], preferred_element_type=f32)
            + gathered[6].astype(f32)
        )
        normed2 = layer_norm(hidden, gain_two, shift_two).astype(bf16)
        inner = jnp.dot(normed2, gathered[2], preferred_element_type=f32) + gathered[7].astype(f32)
        activated = gelu_tanh(inner).astype(bf16)
        result = (
            hidden
            + jnp.dot(activated, gathered[3], preferred_element_type=f32)
            + gathered[8].astype(f32)
        )
        outputs.append(result.astype(bf16).reshape(seq_group, row_count, model_width))
        gathered = gather_weights(qkv_weight, out_weight, fc_weight, proj_weight, vectors)
        key_full, value_full = gather_pairs(key_rows, value_rows)
        cotangent = (
            grad_out[first_seq : first_seq + seq_group]
            .astype(f32)
            .reshape(token_count, model_width)
        )
        mlp_grad = cotangent.astype(bf16)
        vector_grads[4] = vector_grads[4] + jnp.sum(mlp_grad, axis=0, dtype=f32)
        act_grad = jnp.einsum("nd,fd->nf", mlp_grad, gathered[3], preferred_element_type=f32)
        gelu_value, gelu_pull = jax.vjp(gelu_tanh, inner)
        inner_grad = gelu_pull(act_grad)[0].astype(bf16)
        vector_grads[3] = vector_grads[3] + jnp.sum(inner_grad, axis=0, dtype=f32)
        normed2_grad = jnp.einsum("nf,df->nd", inner_grad, gathered[2], preferred_element_type=f32)
        norm_value, norm_pull = jax.vjp(layer_norm, hidden, gain_two, shift_two)
        hidden_ln, gain_two_grad, shift_two_grad = norm_pull(normed2_grad)
        vector_grads[7] = vector_grads[7] + gain_two_grad
        vector_grads[8] = vector_grads[8] + shift_two_grad
        hidden_grad = cotangent + hidden_ln
        branch_grad = hidden_grad.astype(bf16)
        vector_grads[2] = vector_grads[2] + jnp.sum(branch_grad, axis=0, dtype=f32)
        attended_grad = jnp.einsum(
            "nd,ed->ne", branch_grad, gathered[1], preferred_element_type=f32
        ).astype(bf16)
        attended_grad = attended_grad.reshape(seq_group, row_count, HEADS, HEAD_DIM)
        query_grad, key_grad, value_grad = attend_back(
            queries, key_full, value_full, attended_grad, log_total, query_pos, query_seg, segments
        )
        key_local, value_local = (
            lax.psum_scatter(key_grad, "ctx", scatter_dimension=1, tiled=True),
            lax.psum_scatter(value_grad, "ctx", scatter_dimension=1, tiled=True),
        )
        projected_grad = jnp.concatenate(
            [
                query_grad.reshape(token_count, model_width),
                key_local.reshape(token_count, model_width),
                value_local.reshape(token_count, model_width),
            ],
            axis=1,
        ).astype(bf16)
        vector_grads[0] = vector_grads[0] + jnp.sum(
            projected_grad[:, :model_width], axis=0, dtype=f32
        )
        vector_grads[1] = vector_grads[1] + jnp.sum(
            projected_grad[:, 2 * model_width :], axis=0, dtype=f32
        )
        normed1_grad = jnp.einsum(
            "ne,de->nd", projected_grad, gathered[0], preferred_element_type=f32
        )
        first_value, first_pull = jax.vjp(layer_norm, values, gain_one, shift_one)
        values_ln, gain_one_grad, shift_one_grad = first_pull(normed1_grad)
        vector_grads[5] = vector_grads[5] + gain_one_grad
        vector_grads[6] = vector_grads[6] + shift_one_grad
        input_grads.append((hidden_grad + values_ln).reshape(seq_group, row_count, model_width))
        left_slices = (
            lax.all_to_all(normed1, "ctx", split_axis=1, concat_axis=0, tiled=True),
            lax.all_to_all(attended, "ctx", split_axis=1, concat_axis=0, tiled=True),
            lax.all_to_all(normed2, "ctx", split_axis=1, concat_axis=0, tiled=True),
            lax.all_to_all(activated, "ctx", split_axis=1, concat_axis=0, tiled=True),
        )
        right_full = (
            lax.all_gather(projected_grad, "ctx", axis=0, tiled=True),
            lax.all_gather(branch_grad, "ctx", axis=0, tiled=True),
            lax.all_gather(inner_grad, "ctx", axis=0, tiled=True),
            lax.all_gather(mlp_grad, "ctx", axis=0, tiled=True),
        )
        matrix_grads[0] = matrix_grads[0] + jnp.einsum(
            "nd,ne->de", left_slices[0], right_full[0], preferred_element_type=f32
        )
        matrix_grads[1] = matrix_grads[1] + jnp.einsum(
            "nd,ne->de", left_slices[1], right_full[1], preferred_element_type=f32
        )
        matrix_grads[2] = matrix_grads[2] + jnp.einsum(
            "nd,ne->de", left_slices[2], right_full[2], preferred_element_type=f32
        )
        matrix_grads[3] = matrix_grads[3] + jnp.einsum(
            "nd,ne->de", left_slices[3], right_full[3], preferred_element_type=f32
        )
    column_sums = (
        lax.psum_scatter(matrix_grads[0], "dp", scatter_dimension=1, tiled=True),
        lax.psum_scatter(matrix_grads[1], "dp", scatter_dimension=1, tiled=True),
        lax.psum_scatter(matrix_grads[2], "dp", scatter_dimension=1, tiled=True),
        lax.psum_scatter(matrix_grads[3], "dp", scatter_dimension=1, tiled=True),
        lax.psum_scatter(vector_grads[0], "dp", scatter_dimension=0, tiled=True),
        lax.psum_scatter(vector_grads[1], "dp", scatter_dimension=0, tiled=True),
        lax.psum_scatter(vector_grads[2], "dp", scatter_dimension=0, tiled=True),
        lax.psum_scatter(vector_grads[3], "dp", scatter_dimension=0, tiled=True),
        lax.psum_scatter(vector_grads[4], "dp", scatter_dimension=0, tiled=True),
        lax.psum_scatter(vector_grads[5], "dp", scatter_dimension=0, tiled=True),
        lax.psum_scatter(vector_grads[6], "dp", scatter_dimension=0, tiled=True),
        lax.psum_scatter(vector_grads[7], "dp", scatter_dimension=0, tiled=True),
        lax.psum_scatter(vector_grads[8], "dp", scatter_dimension=0, tiled=True),
    )
    vector_sums = lax.psum(
        (
            column_sums[4],
            column_sums[5],
            column_sums[6],
            column_sums[7],
            column_sums[8],
            column_sums[9],
            column_sums[10],
            column_sums[11],
            column_sums[12],
        ),
        "ctx",
    )
    output = jnp.concatenate(outputs, axis=0)
    input_grad = jnp.concatenate(input_grads, axis=0)
    return (
        output,
        input_grad,
        column_sums[0],
        vector_sums[0],
        vector_sums[1],
        column_sums[1],
        vector_sums[2],
        column_sums[2],
        vector_sums[3],
        column_sums[3],
        vector_sums[4],
        vector_sums[5],
        vector_sums[6],
        vector_sums[7],
        vector_sums[8],
    )


def solution(mesh):
    placed = (
        P("dp", "ctx", None),
        P("dp", "ctx", None),
        P("dp", None),
        P("ctx", "dp"),
        P("dp"),
        P("dp"),
        P("ctx", "dp"),
        P("dp"),
        P("ctx", "dp"),
        P("dp"),
        P("ctx", "dp"),
        P("dp"),
        P("dp"),
        P("dp"),
        P("dp"),
        P("dp"),
    )
    return jax.shard_map(
        on_device,
        mesh=mesh,
        in_specs=placed,
        out_specs=(
            P("dp", "ctx", None),
            P("dp", "ctx", None),
            P("ctx", "dp"),
            P("dp"),
            P("dp"),
            P("ctx", "dp"),
            P("dp"),
            P("ctx", "dp"),
            P("dp"),
            P("ctx", "dp"),
            P("dp"),
            P("dp"),
            P("dp"),
            P("dp"),
            P("dp"),
        ),
        check_vma=False,
    )
```

profile of v0, /device:TPU:0, one launch (start us, length us, event | category | flops | bytes accessed | tf_op | source)
XLA Modules:
  0.0 3017.8 jit_solution(4523406349992921891)
XLA Ops:
  8.1 26.5 all-gather.27.cloned.1.call-done
  44.2 39.8 %all-reduce.21 = (bf16[1600]{0:T(1024)(128)(2,1)S(1)}, bf16[1600]{0:T(1024)(128)(2,1)S(1)}, bf16[1600]{0:T(1024)(128)(2,1)S(1)}, bf16[1600]{0:T(1024)(128)(2,1)S...) all-reduce(bf16[1600]{0:T(1024)(128)(2,1)S(1)} %dynamic-update-slic, ...), channel_id=1, replica_groups=mesh['dp'=8,'ctx'=4] {'dp'}, use_global_device_ids=true, to_apply=%add.2 | all-reduce | flops 19200 | bytes 76800
  85.5 172.1 %all-gather.29.cloned.1.call-done = bf16[1600,4800]{0,1:T(8,128)(2,1)} async-done(((bf16[1600,600]{0,1:T(8,128)(2,1)}), bf16[1600,4800]{0,1:T(8,128)(2,1)}) %all-gather.29.cloned.1.call-update) | async-done | bytes 15360016 | tf_op jit(solution)/shard_map/all_gather | solution.py:38
  298.6 13.0 all-gather.63.cloned.1.call-done
  322.0 21.3 all-gather.57.cloned.1.call-done
  343.3 45.1 %while.126 = (s32[]{:T(128)}, f32[1,25,256]{2,1,0:T(8,128)S(1)}, f32[1,25,256]{2,1,0:T(8,128)S(1)}, s32[1,1024]{1,0:T(1,128)S(1)}, s32[1,256]{1,0:T(1,128)S(1)},...) while((s32[]{:T(128)}, f32[1,25,256]{2,1,0:T(8,128)S(1)}, ...), condition=%wide.region_15.16_spmd.clone, body=%wide.region_12.15_spmd.clone.sunk | while | flops 223051520 | bytes 16921788 | solution.py:109
  388.4 25.2 while.127
  416.2 44.4 %while.124 = (s32[]{:T(128)}, f32[1,25,256]{2,1,0:T(8,128)S(1)}, f32[1,25,256]{2,1,0:T(8,128)S(1)}, s32[1,1024]{1,0:T(1,128)S(1)}, s32[1,256]{1,0:T(1,128)S(1)},...) while((s32[]{:T(128)}, f32[1,25,256]{2,1,0:T(8,128)S(1)}, ...), condition=%wide.region_5.6_spmd.clone, body=%wide.region_2.5_spmd.clone.sunk | while | flops 223051520 | bytes 16921788 | solution.py:109
  460.7 25.5 while.125
  488.6 38.5 %all-gather.31.cloned.1.call-done = bf16[1600,1600]{0,1:T(8,128)(2,1)} async-done(((bf16[1600,200]{0,1:T(8,128)(2,1)}), bf16[1600,1600]{0,1:T(8,128)(2,1)}) %all-gather.31.cloned.1.call-update) | async-done | bytes 5120016 | tf_op jit(solution)/shard_map/all_gather | solution.py:39
  536.7 398.5 %all-gather.35.cloned.1.call-done = bf16[1600,6400]{0,1:T(8,128)(2,1)} async-done(((bf16[1600,800]{0,1:T(8,128)(2,1)}), bf16[1600,6400]{0,1:T(8,128)(2,1)}) %all-gather.35.cloned.1.call-update) | async-done | bytes 20480016 | tf_op jit(solution)/shard_map/all_gather | solution.py:40
  935.2 13.3 multiply_convert_fusion
  948.5 380.8 %all-gather.37.cloned.1.call-done = bf16[6400,1600]{0,1:T(8,128)(2,1)} async-done(((bf16[6400,200]{0,1:T(8,128)(2,1)}), bf16[6400,1600]{0,1:T(8,128)(2,1)}) %all-gather.37.cloned.1.call-update) | async-done | bytes 20480016 | tf_op jit(solution)/shard_map/all_gather | solution.py:41
  1329.3 18.6 convert_reduce_fusion
  1347.9 14.3 fusion.156
  1362.2 13.4 multiply_convert_fusion.1
  1375.6 18.6 convert_reduce_fusion.1
  1394.2 17.9 multiply_reduce_fusion.1
  1423.7 28.7 while.128
  1459.5 74.3 %while.129 = (s32[]{:T(128)}, f32[1,256,25,64]{1,3,2,0:T(8,128)}, f32[1,1024,1600]{1,2,0:T(8,128)}, f32[1,1024,1600]{1,2,0:T(8,128)}, bf16[1,1024,1600]{1,2,0:T(...) while((s32[]{:T(128)}, f32[1,256,25,64]{1,3,2,0:T(8,128)}, ...), condition=%wide.region_26.27_spmd.clone, body=%wide.region_25.26_spmd.clone.sunk | while | flops 1066795520 | bytes 55168264 | solution.py:220
  1540.6 29.4 while.130
  1577.1 74.6 %while.131 = (s32[]{:T(128)}, f32[1,256,25,64]{1,3,2,0:T(8,128)}, f32[1,1024,1600]{1,2,0:T(8,128)}, f32[1,1024,1600]{1,2,0:T(8,128)}, bf16[1,1024,1600]{1,2,0:T(...) while((s32[]{:T(128)}, f32[1,256,25,64]{1,3,2,0:T(8,128)}, ...), condition=%wide.region_37.38_spmd.clone, body=%wide.region_36.37_spmd.clone.sunk | while | flops 1066795520 | bytes 55168264 | solution.py:220
  1662.0 57.4 %reduce-scatter.23.cloned.1.call-done = f32[1,256,1600]{1,2,0:T(8,128)} async-done(((f32[1,1024,1600]{1,2,0:T(8,128)}), f32[1,256,1600]{1,2,0:T(8,128)}) %reduce-scatter.23.cloned.1.call-update) | async-done | bytes 1638416 | tf_op jit(solution)/shard_map/reduce_scatter | solution.py:346
  1721.9 60.2 %reduce-scatter.21.cloned.1.call-done = f32[1,256,1600]{1,2,0:T(8,128)} async-done(((f32[1,1024,1600]{1,2,0:T(8,128)}), f32[1,256,1600]{1,2,0:T(8,128)}) %reduce-scatter.21.cloned.1.call-update) | async-done | bytes 1638416 | tf_op jit(solution)/shard_map/reduce_scatter | solution.py:345
  1789.5 24.7 all_to_all.146
  1835.6 17.5 all-gather.45.cloned.1.call-done
  1863.6 23.5 all_to_all.147
  1892.0 19.8 all-to-all-done.5
  1917.2 13.8 fusion.143
  1931.0 14.2 multiply_reduce_fusion.6
  1957.2 13.2 fusion.159
  1970.4 73.5 %all-gather.49.cloned.1.call-done = bf16[1024,6400]{1,0:T(8,128)(2,1)} async-done(((bf16[256,6400]{1,0:T(8,128)(2,1)}), bf16[1024,6400]{1,0:T(8,128)(2,1)}) %all-gather.49.cloned.1.call-update) | async-done | bytes 13107216 | tf_op jit(solution)/shard_map/all_gather | solution.py:379
  2043.9 14.3 convolution_add_fusion.2
  2058.2 12.6 copy.137
  2073.4 23.5 all_to_all.148
  2101.9 19.6 all-to-all-done.1
  2130.7 12.4 fusion.157
  2143.1 57.0 %all-gather.41.cloned.1.call-done = bf16[1024,4800]{0,1:T(8,128)(2,1)} async-done(((bf16[256,4800]{0,1:T(8,128)(2,1)}), bf16[1024,4800]{0,1:T(8,128)(2,1)}) %all-gather.41.cloned.1.call-update) | async-done | bytes 9830416 | tf_op jit(solution)/shard_map/all_gather | solution.py:377
  2200.1 13.4 convolution_add_fusion.4
  2239.1 50.3 %all-to-all-done.6 = bf16[256,4,1600]{0,2,1:T(8,128)(2,1)} async-done(((bf16[256,4,1600]{0,2,1:T(8,128)(2,1)}), bf16[256,4,1600]{0,2,1:T(8,128)(2,1)}, u32[]{:S(2)}, u32[]{:S(2)}) %all-to-all-start.6) | async-done | bytes 3276832 | tf_op jit(solution)/shard_map/all_to_all | solution.py:374
  2299.9 32.7 %all-to-all-done.7 = bf16[256,4,1600]{0,2,1:T(8,128)(2,1)} async-done(((bf16[256,4,1600]{0,2,1:T(8,128)(2,1)}), bf16[256,4,1600]{0,2,1:T(8,128)(2,1)}, u32[]{:S(2)}, u32[]{:S(2)}) %all-to-all-start.7) | async-done | bytes 3276832 | tf_op jit(solution)/shard_map/all_to_all | solution.py:374
  2338.0 11.0 fusion.105
  2349.0 12.6 convolution_add_fusion.3
  2392.8 43.3 %all-reduce.24.cloned.1.call-done = (f32[1600]{0:T(1024)}, f32[1600]{0:T(1024)}, f32[1600]{0:T(1024)}, f32[6400]{0:T(1024)}, f32[1600]{0:T(1024)}, /*index=5*/f3...) async-done(((f32[1600]{0:T(1024)}, f32[1600]{0:T(1024)}, f32[1600]{0:T(1024)}, f32[6400]{0:T(1024)}, f32[1600]{0:T(1024)}, /*index=5*/f32[1600]{0:T(1024)}, ...) | async-done | bytes 76816
  2443.0 11.1 all-reduce.20
  2454.1 199.9 %reduce-scatter.29.cloned.1.call-done = f32[800,400]{1,0:T(8,128)} async-done(((f32[6400,400]{1,0:T(8,128)}), f32[800,400]{1,0:T(8,128)}) %reduce-scatter.29.cloned.1.call-update) | async-done | bytes 1280016
  2657.1 168.8 %reduce-scatter.25.cloned.1.call-done = f32[600,400]{1,0:T(8,128)} async-done(((f32[4800,400]{1,0:T(8,128)}), f32[600,400]{1,0:T(8,128)}) %reduce-scatter.25.cloned.1.call-update) | async-done | bytes 960016
  2828.5 182.3 %reduce-scatter.31.cloned.1.call-done = f32[1600,200]{0,1:T(8,128)} async-done(((f32[1600,1600]{0,1:T(8,128)}), f32[1600,200]{0,1:T(8,128)}) %reduce-scatter.31.cloned.1.call-update) | async-done | bytes 1280016
  (653 shorter events, 627.7 us)
Async XLA Ops:
  7.2 27.4 all-gather.27.cloned.1.call-start
  8.0 35.0 %copy-start.77 = (bf16[200]{0:T(256)(128)(2,1)S(1)}, bf16[200]{0:T(256)(128)(2,1)}, u32[]{:S(2)}) copy-start(bf16[200]{0:T(256)(128)(2,1)} %param.39) | copy-start | bytes 1204
  8.0 35.3 %copy-start.78 = (bf16[200]{0:T(256)(128)(2,1)S(1)}, bf16[200]{0:T(256)(128)(2,1)}, u32[]{:S(2)}) copy-start(bf16[200]{0:T(256)(128)(2,1)} %param.46) | copy-start | bytes 1204
  8.0 35.5 %copy-start.79 = (bf16[200]{0:T(256)(128)(2,1)S(1)}, bf16[200]{0:T(256)(128)(2,1)}, u32[]{:S(2)}) copy-start(bf16[200]{0:T(256)(128)(2,1)} %param.47) | copy-start | bytes 1204
  8.0 35.8 %copy-start.80 = (bf16[200]{0:T(256)(128)(2,1)S(1)}, bf16[200]{0:T(256)(128)(2,1)}, u32[]{:S(2)}) copy-start(bf16[200]{0:T(256)(128)(2,1)} %param.43) | copy-start | bytes 1204
  8.0 36.0 %copy-start.71 = (bf16[800]{0:T(1024)(128)(2,1)S(1)}, bf16[800]{0:T(1024)(128)(2,1)}, u32[]{:S(2)}) copy-start(bf16[800]{0:T(1024)(128)(2,1)} %param.41) | copy-start | bytes 4804
  8.0 76.7 %copy-start.4 = (bf16[2,256,1600]{1,2,0:T(8,128)(2,1)S(1)}, bf16[2,256,1600]{1,2,0:T(8,128)(2,1)}, u32[]{:S(2)}) copy-start(bf16[2,256,1600]{1,2,0:T(8,128)(2,1)} %param.32) | copy-start | bytes 4915204
  8.0 249.6 %all-gather.29.cloned.1.call-start = ((), (), s32[]{:S(2)}) async-start(), calls=%async_computation.17 | async-start | bytes 17971200 | tf_op jit(solution)/shard_map/all_gather | solution.py:38
  38.7 254.6 %all-gather.33.cloned.1.call-start = ((), (), s32[]{:S(2)}) async-start(), calls=%async_computation.19 | async-start | bytes 3584000 | tf_op jit(solution)/shard_map/all_gather | solution.py:34
  39.4 272.2 %all-gather.63.cloned.1.call-start = ((), (), s32[]{:S(2)}) async-start(), calls=%async_computation.38 | async-start | bytes 3328000 | tf_op jit(solution)/shard_map/all_gather | solution.py:35
  40.0 303.3 %all-gather.57.cloned.1.call-start = ((), (), s32[]{:S(2)}) async-start(), calls=%async_computation.35 | async-start | bytes 4096000 | tf_op jit(solution)/shard_map/all_gather | solution.py:56
  84.1 186.3 %copy-start.34 = (f32[1600]{0:T(1024)}, f32[1600]{0:T(1024)S(1)}, u32[]{:S(2)}) copy-start(f32[1600]{0:T(1024)S(1)} %convert_element_type.183) | copy-start | bytes 19204
  85.0 183.0 %copy-start.44 = (f32[256]{0:T(256)}, f32[256]{0:T(256)S(1)}, u32[]{:S(2)}) copy-start(f32[256]{0:T(256)S(1)} %get-tuple-element.2003) | copy-start | bytes 3076
  85.0 185.4 %copy-start.46 = (f32[256]{0:T(256)}, f32[256]{0:T(256)S(1)}, u32[]{:S(2)}) copy-start(f32[256]{0:T(256)S(1)} %get-tuple-element.2004) | copy-start | bytes 3076
  85.5 182.5 %copy-start.62 = (f32[256]{0:T(256)}, f32[256]{0:T(256)S(1)}, u32[]{:S(2)}) copy-start(f32[256]{0:T(256)S(1)} %get-tuple-element.1730) | copy-start | bytes 3076
  85.5 184.9 %copy-start.60 = (f32[256]{0:T(256)}, f32[256]{0:T(256)S(1)}, u32[]{:S(2)}) copy-start(f32[256]{0:T(256)S(1)} %get-tuple-element.1729) | copy-start | bytes 3076
  85.5 182.5 %copy-start.52 = (f32[256]{0:T(256)}, f32[256]{0:T(256)S(1)}, u32[]{:S(2)}) copy-start(f32[256]{0:T(256)S(1)} %fusion.139) | copy-start | bytes 3076
  269.5 118.9 %all-gather.55.cloned.1.call-start = ((), (), s32[]{:S(2)}) async-start(), calls=%async_computation.34 | async-start | bytes 4096000 | tf_op jit(solution)/shard_map/all_gather | solution.py:57
  270.1 146.1 %all-gather.53.cloned.1.call-start = ((), (), s32[]{:S(2)}) async-start(), calls=%async_computation.33 | async-start | bytes 4096000 | tf_op jit(solution)/shard_map/all_gather | solution.py:56
  282.5 178.2 %all-gather.51.cloned.1.call-start = ((), (), s32[]{:S(2)}) async-start(), calls=%async_computation.32 | async-start | bytes 4096000 | tf_op jit(solution)/shard_map/all_gather | solution.py:57
  283.2 243.9 %all-gather.31.cloned.1.call-start = ((), (), s32[]{:S(2)}) async-start(), calls=%async_computation.18 | async-start | bytes 5990400 | tf_op jit(solution)/shard_map/all_gather | solution.py:39
  293.2 642.0 %all-gather.35.cloned.1.call-start = ((), (), s32[]{:S(2)}) async-start(), calls=%async_computation.20 | async-start | bytes 23961600 | tf_op jit(solution)/shard_map/all_gather | solution.py:40
  298.6 1030.7 %all-gather.37.cloned.1.call-start = ((), (), s32[]{:S(2)}) async-start(), calls=%async_computation.21 | async-start | bytes 23040000 | tf_op jit(solution)/shard_map/all_gather | solution.py:41
  321.5 1333.6 %reduce-scatter.19.cloned.1.call-start = ((), (), s32[]{:S(2)}) async-start(), calls=%async_computation.23 | async-start | bytes 8192000 | tf_op jit(solution)/shard_map/reduce_scatter | solution.py:346
  531.6 880.5 %copy-start.6 = (f32[256,1600]{0,1:T(8,128)}, f32[256,1600]{0,1:T(8,128)S(1)}, u32[]{:S(2)}) copy-start(f32[256,1600]{0,1:T(8,128)S(1)} %get-tuple-element.1992) | copy-start | bytes 4915204
  935.2 394.1 %copy-start.14 = (bf16[2,256,1600]{1,2,0:T(8,128)(2,1)S(1)}, bf16[2,256,1600]{1,2,0:T(8,128)(2,1)}, u32[]{:S(2)}) copy-start(bf16[2,256,1600]{1,2,0:T(8,128)(2,1)} %param.33) | copy-start | bytes 4915204
  1533.8 123.1 %reduce-scatter.17.cloned.1.call-start = ((), (), s32[]{:S(2)}) async-start(), calls=%async_computation.22 | async-start | bytes 8192000 | tf_op jit(solution)/shard_map/reduce_scatter | solution.py:345
  1570.0 149.3 %reduce-scatter.23.cloned.1.call-start = ((), (), s32[]{:S(2)}) async-start(), calls=%async_computation.25 | async-start | bytes 8192000 | tf_op jit(solution)/shard_map/reduce_scatter | solution.py:346
  1651.8 130.3 %reduce-scatter.21.cloned.1.call-start = ((), (), s32[]{:S(2)}) async-start(), calls=%async_computation.24 | async-start | bytes 8192000 | tf_op jit(solution)/shard_map/reduce_scatter | solution.py:345
  1652.4 177.4 %all-gather.43.cloned.1.call-start = ((), (), s32[]{:S(2)}) async-start(), calls=%async_computation.28 | async-start | bytes 4096000 | tf_op jit(solution)/shard_map/all_gather | solution.py:378
  1653.0 200.2 %all-gather.45.cloned.1.call-start = ((), (), s32[]{:S(2)}) async-start(), calls=%async_computation.29 | async-start | bytes 4096000 | tf_op jit(solution)/shard_map/all_gather | solution.py:378
  1653.6 303.7 %all-gather.47.cloned.1.call-start = ((), (), s32[]{:S(2)}) async-start(), calls=%async_computation.30 | async-start | bytes 16384000 | tf_op jit(solution)/shard_map/all_gather | solution.py:379
  1654.1 389.8 %all-gather.49.cloned.1.call-start = ((), (), s32[]{:S(2)}) async-start(), calls=%async_computation.31 | async-start | bytes 16384000 | tf_op jit(solution)/shard_map/all_gather | solution.py:379
  1654.9 475.8 %all-gather.39.cloned.1.call-start = ((), (), s32[]{:S(2)}) async-start(), calls=%async_computation.26 | async-start | bytes 12288000 | tf_op jit(solution)/shard_map/all_gather | solution.py:377
  1661.2 538.9 %all-gather.41.cloned.1.call-start = ((), (), s32[]{:S(2)}) async-start(), calls=%async_computation.27 | async-start | bytes 12288000 | tf_op jit(solution)/shard_map/all_gather | solution.py:377
  1787.4 550.6 %all-gather.59.cloned.1.call-start = ((), (), s32[]{:S(2)}) async-start(), calls=%async_computation.36 | async-start | bytes 4096000 | tf_op jit(solution)/shard_map/all_gather | solution.py:380
  1788.8 560.2 %all-gather.61.cloned.1.call-start = ((), (), s32[]{:S(2)}) async-start(), calls=%async_computation.37 | async-start | bytes 4096000 | tf_op jit(solution)/shard_map/all_gather | solution.py:380
  1814.2 15.5 all-to-all-start.3
  1817.7 567.4 %reduce-scatter.27.cloned.1.call-start = ((), (), s32[]{:S(2)}) async-start(), calls=%async_computation.40 | async-start | bytes 3686400
  1887.2 24.7 all-to-all-start.5
  1890.8 545.3 %all-reduce.24.cloned.1.call-start = ((), (), s32[]{:S(2)}) async-start(), calls=%async_computation.43 | async-start | bytes 188416
  1950.7 703.3 %reduce-scatter.29.cloned.1.call-start = ((), (), s32[]{:S(2)}) async-start(), calls=%async_computation.41 | async-start | bytes 14745600
  1957.2 86.7 %copy-start.26 = (bf16[4,50,8,256]{3,2,0,1:T(8,128)(2,1)S(1)}, bf16[4,50,8,256]{3,2,0,1:T(8,128)(2,1)}, u32[]{:S(2)}) copy-start(bf16[4,50,8,256]{3,2,0,1:T(8,128)(2,1)} %copy.144) | copy-start | bytes 2457604
  2096.9 24.6 all-to-all-start.1
  2100.4 725.5 %reduce-scatter.25.cloned.1.call-start = ((), (), s32[]{:S(2)}) async-start(), calls=%async_computation.39 | async-start | bytes 11059200
  2228.8 60.6 %all-to-all-start.6 = ((bf16[256,4,1600]{0,2,1:T(8,128)(2,1)}), bf16[256,4,1600]{0,2,1:T(8,128)(2,1)}, u32[]{:S(2)}, u32[]{:S(2)}) async-start(bf16[256,4,1600]{0,2,1:T(8,128)(2,1)} %bitcast.646), calls=%async_computation.10 | async-start | bytes 6553600 | tf_op jit(solution)/shard_map/all_to_all | solution.py:374
  2289.5 43.1 %all-to-all-start.7 = ((bf16[256,4,1600]{0,2,1:T(8,128)(2,1)}), bf16[256,4,1600]{0,2,1:T(8,128)(2,1)}, u32[]{:S(2)}, u32[]{:S(2)}) async-start(bf16[256,4,1600]{0,2,1:T(8,128)(2,1)} %bitcast.645), calls=%async_computation.11 | async-start | bytes 6553600 | tf_op jit(solution)/shard_map/all_to_all | solution.py:374
  2294.2 716.6 %reduce-scatter.31.cloned.1.call-start = ((), (), s32[]{:S(2)}) async-start(), calls=%async_computation.42 | async-start | bytes 11980800
  (72 other events, 767.4 us)
Sparse Core Ops, SparseCore 0:
  9.6 24.9 all-gather.26
  38.8 218.8 all-gather.28
  259.2 25.1 all-gather.32
  285.8 25.7 all-gather.62
  313.6 29.6 all-gather.56
  345.3 29.6 all-gather.54
  376.6 29.6 all-gather.52
  407.8 29.6 all-gather.50
  439.8 87.2 all-gather.30
  529.0 406.1 all-gather.34
  936.7 392.5 all-gather.36
  1533.9 60.0 reduce-scatter.18
  1596.7 60.1 reduce-scatter.16
  1659.3 60.0 reduce-scatter.22
  1721.9 60.1 reduce-scatter.20
  1783.5 38.4 all-gather.42
  1823.4 29.6 all-gather.44
  1854.6 102.6 all-gather.46
  1958.8 85.0 all-gather.48
  2045.3 85.3 all-gather.38
  2132.2 67.7 all-gather.40
  2201.6 29.6 all-gather.58
  2232.9 47.3 all-gather.60
  2283.8 76.1 reduce-scatter.26
  2365.0 70.9 all-reduce.23
  2440.0 213.9 reduce-scatter.28
  2657.9 167.8 reduce-scatter.24
  2830.4 180.3 reduce-scatter.30
where the time goes:
time: 3030 us; the launch traced here: 3020 us
  waiting for transfers between devices  2070 us (68%)
  matrix products  505 us (17%)
  local copies, waits for them, and re-layouts  185 us (6%)
  blocking collectives  131 us (4%)
  other arithmetic  85.6 us (3%)
    unnamed x33, waiting for transfers between devices  601 us
    all_gather x1, waiting for transfers between devices, gather_weights(): lax.all_gather(rows_all[2], 'dp', axis=1, tiled=True)  399 us
    all_gather x1, waiting for transfers between devices, gather_weights(): lax.all_gather(rows_all[3], 'dp', axis=1, tiled=True)  381 us
    all_gather x1, waiting for transfers between devices, gather_weights(): lax.all_gather(rows_all[0], 'dp', axis=1, tiled=True)  172 us
    dot_general x24, matrix products, block_scores(): jnp.einsum('schd,skhd->shck', queries, key_block, preferred_element_type=...  86.7 us
    all_to_all x2, waiting for transfers between devices, on_device(): lax.all_to_all(activated, 'ctx', split_axis=1, concat_axis=0, tiled=True)  83 us
    all_gather x2, waiting for transfers between devices, on_device(): lax.all_gather(inner_grad, 'ctx', axis=0, tiled=True)  79.9 us
    all_gather x2, waiting for transfers between devices, on_device(): lax.all_gather(projected_grad, 'ctx', axis=0, tiled=True)  66.1 us
  transfers between devices with their start and end apart: 33, of which 23 were waited for; matrix products, arithmetic and copies ran while one was open for 19% of the time, Pallas kernels for 0%

commit v1 on v0

v1 whole, which is shorter than its diff:
```python
import functools

import jax
import jax.numpy as jnp
from jax import lax
from jax.experimental import pallas as pl
from jax.experimental.pallas import tpu as pltpu
from jax.sharding import PartitionSpec as P

HEADS = 25
HEAD_DIM = 64
LANES = 128
EPS = 1e-05
NEG_FILL = -1e30
GELU_C = 0.7978845608028654
GELU_A = 0.044715

bf16 = jnp.bfloat16
f32 = jnp.float32
VMEM_LIMIT = 58 * 1024 * 1024


def layer_norm(values, gain, shift):
    center = values - jnp.mean(values, axis=-1, keepdims=True)
    factor = lax.rsqrt(jnp.mean(center * center, axis=-1, keepdims=True) + EPS)
    return center * factor * gain + shift


def dot_nn(a, b):
    return lax.dot_general(a, b, (((1,), (0,)), ((), ())), preferred_element_type=f32)


def dot_nt(a, b):
    return lax.dot_general(a, b, (((1,), (1,)), ((), ())), preferred_element_type=f32)


def dot_tn(a, b):
    return lax.dot_general(a, b, (((0,), (0,)), ((), ())), preferred_element_type=f32)


def params(n_axes=1):
    return pltpu.CompilerParams(
        dimension_semantics=("arbitrary",) * n_axes, vmem_limit_bytes=VMEM_LIMIT
    )


def cost(flops, read, transcendentals=0):
    return pl.CostEstimate(
        flops=int(flops), bytes_accessed=int(read), transcendentals=int(transcendentals)
    )


def qkv_project(normed, weight, bias):
    tokens, width = normed.shape
    parts, _, n = weight.shape

    def kernel(x_ref, w_ref, b_ref, *out_refs):
        part = pl.program_id(0)
        y = (dot_nn(x_ref[...], w_ref[0]) + b_ref[0]).astype(bf16)
        for d in range(parts):

            @pl.when(part == d)
            def _():
                first, last = d * n, (d + 1) * n
                for g in range(3):
                    lo, hi = max(first, g * width), min(last, (g + 1) * width)
                    if lo < hi:
                        out_refs[g][:, lo - g * width : hi - g * width] = y[
                            :, lo - first : hi - first
                        ]

    whole = pl.BlockSpec((tokens, width), lambda d: (0, 0))
    return pl.pallas_call(
        kernel,
        grid=(parts,),
        in_specs=[
            whole,
            pl.BlockSpec((1, width, n), lambda d: (d, 0, 0)),
            pl.BlockSpec((1, 1, n), lambda d: (d, 0, 0)),
        ],
        out_specs=[whole] * 3,
        out_shape=[jax.ShapeDtypeStruct((tokens, width), bf16)] * 3,
        compiler_params=params(),
        cost_estimate=cost(2 * tokens * width * parts * n, 2 * width * parts * n),
        name="qkv",
    )(normed, weight, bias)


def pair_masks(pair, width):
    lane = lax.broadcasted_iota(jnp.int32, (1, LANES), 1)
    inside = lane + pair * LANES < width
    return inside & (lane < HEAD_DIM), inside & (lane >= HEAD_DIM), inside


def attention_forward(bounds, queries, pairs_full, seg_col, seg_row):
    seqs, rows, width = queries.shape
    blocks = pairs_full.shape[0]
    pairs = pl.cdiv(width, LANES)

    def kernel(bounds_ref, q_ref, kv_ref, sc_ref, sr_ref, o_ref, of_ref, lse_ref):
        seq, pair = pl.program_id(0), pl.program_id(1)
        mine, start = bounds_ref[0], bounds_ref[1 + seq]
        low, high, inside = pair_masks(pair, width)
        scaled = q_ref[0] * jnp.asarray(0.125, bf16)
        q_heads = (
            jnp.where(low, scaled, jnp.zeros_like(scaled)),
            jnp.where(high, scaled, jnp.zeros_like(scaled)),
        )
        seg_q = sc_ref[0]

        def block(j, diagonal, carry):
            k = jnp.where(inside, kv_ref[j, 0, 0], jnp.zeros((rows, LANES), bf16))
            v = jnp.where(inside, kv_ref[j, 1, 0], jnp.zeros((rows, LANES), bf16))
            allowed = sr_ref[0, j] == seg_q
            if diagonal:
                at_row = lax.broadcasted_iota(jnp.int32, (rows, rows), 0)
                at_col = lax.broadcasted_iota(jnp.int32, (rows, rows), 1)
                allowed = allowed & (at_col <= at_row)
            out = []
            for head in range(2):
                s = jnp.where(allowed, dot_nt(q_heads[head], k), NEG_FILL)
                top = jnp.max(s, axis=1, keepdims=True)
                if carry is None:
                    p = jnp.exp(s - top)
                    out += [top, jnp.sum(p, axis=1, keepdims=True), dot_nn(p.astype(bf16), v)]
                else:
                    m, l, acc = carry[3 * head : 3 * head + 3]
                    new = jnp.maximum(m, top)
                    scale = jnp.exp(m - new)
                    p = jnp.exp(s - new)
                    out += [
                        new,
                        l * scale + jnp.sum(p, axis=1, keepdims=True),
                        acc * scale + dot_nn(p.astype(bf16), v),
                    ]
            return tuple(out)

        carry = block(mine, True, None)
        carry = lax.fori_loop(start, mine, lambda j, c: block(j, False, c), carry)
        m0, l0, a0, m1, l1, a1 = carry
        result = jnp.where(low, a0 / l0, a1 / l1)
        o_ref[0] = result.astype(bf16)
        of_ref[0] = result
        lse_ref[0] = jnp.where(low, m0 + jnp.log(l0), m1 + jnp.log(l1))

    tile = pl.BlockSpec((1, rows, LANES), lambda s, p, b: (s, 0, p))
    return pl.pallas_call(
        kernel,
        grid_spec=pltpu.PrefetchScalarGridSpec(
            num_scalar_prefetch=1,
            grid=(seqs, pairs),
            in_specs=[
                tile,
                pl.BlockSpec((blocks, 2, 1, rows, LANES), lambda s, p, b: (0, 0, s, 0, p)),
                pl.BlockSpec((1, rows, 1), lambda s, p, b: (s, 0, 0)),
                pl.BlockSpec((1, blocks, 1, rows), lambda s, p, b: (s, 0, 0, 0)),
            ],
            out_specs=[tile, tile, tile],
        ),
        out_shape=[
            jax.ShapeDtypeStruct((seqs, rows, width), bf16),
            jax.ShapeDtypeStruct((seqs, rows, width), f32),
            jax.ShapeDtypeStruct((seqs, rows, width), f32),
        ],
        compiler_params=params(2),
        cost_estimate=cost(
            4 * seqs * rows * rows * blocks * width, 4 * seqs * rows * blocks * width
        ),
        name="attn_fwd",
    )(bounds, queries, pairs_full, seg_col, seg_row)


def attention_backward(
    bounds, queries, pairs_full, seg_col, seg_row, out_grad, out_full, log_total
):
    seqs, rows, width = queries.shape
    blocks = pairs_full.shape[0]
    pairs = pl.cdiv(width, LANES)

    def kernel(bounds_ref, q_ref, kv_ref, sc_ref, sr_ref, g_ref, of_ref, lse_ref, dq_ref, dkv_ref):
        seq, pair = pl.program_id(0), pl.program_id(1)
        mine, start = bounds_ref[0], bounds_ref[1 + seq]
        low, high, inside = pair_masks(pair, width)
        zero = jnp.zeros((rows, LANES), bf16)
        scaled = q_ref[0] * jnp.asarray(0.125, bf16)
        grad = g_ref[0]
        q_heads = (jnp.where(low, scaled, zero), jnp.where(high, scaled, zero))
        g_heads = (jnp.where(low, grad, zero), jnp.where(high, grad, zero))
        product = jnp.where(inside, grad.astype(f32) * of_ref[0], 0.0)
        lse = jnp.where(inside, lse_ref[0], 0.0)
        product_t = product.T
        lse_t = lse.T
        delta = (
            jnp.sum(product_t[:HEAD_DIM], axis=0, keepdims=True),
            jnp.sum(product_t[HEAD_DIM:], axis=0, keepdims=True),
        )
        log_row = (lse_t[0:1], lse_t[HEAD_DIM : HEAD_DIM + 1])
        seg_q = sr_ref[0]
        dkv_ref[...] = jnp.zeros_like(dkv_ref)

        def block(j, diagonal, total):
            k = jnp.where(inside, kv_ref[j, 0, 0], zero)
            v = jnp.where(inside, kv_ref[j, 1, 0], zero)
            allowed = sc_ref[0, j] == seg_q
            if diagonal:
                at_key = lax.broadcasted_iota(jnp.int32, (rows, rows), 0)
                at_query = lax.broadcasted_iota(jnp.int32, (rows, rows), 1)
                allowed = allowed & (at_key <= at_query)
            key_grad, value_grad = None, None
            for head in range(2):
                k_head = jnp.where((low, high)[head], k, zero)
                s = jnp.where(allowed, dot_nt(k, q_heads[head]), NEG_FILL)
                p = jnp.exp(s - log_row[head])
                pushed = dot_nt(v, g_heads[head])
                ds = (p * (pushed - delta[head])).astype(bf16)
                dv = dot_nn(p.astype(bf16), g_heads[head])
                dk = dot_nn(ds, q_heads[head])
                dq = dot_tn(ds, k_head)
                key_grad = dk if key_grad is None else key_grad + dk
                value_grad = dv if value_grad is None else value_grad + dv
                total = dq if total is None else total + dq
            dkv_ref[j, 0, 0] = key_grad.astype(bf16)
            dkv_ref[j, 1, 0] = value_grad.astype(bf16)
            return total

        total = block(mine, True, None)
        total = lax.fori_loop(start, mine, lambda j, c: block(j, False, c), total)
        dq_ref[0] = (total * 0.125).astype(bf16)

    tile = pl.BlockSpec((1, rows, LANES), lambda s, p, b: (s, 0, p))
    many = pl.BlockSpec((blocks, 2, 1, rows, LANES), lambda s, p, b: (0, 0, s, 0, p))
    return pl.pallas_call(
        kernel,
        grid_spec=pltpu.PrefetchScalarGridSpec(
            num_scalar_prefetch=1,
            grid=(seqs, pairs),
            in_specs=[
                tile,
                many,
                pl.BlockSpec((1, blocks, rows, 1), lambda s, p, b: (s, 0, 0, 0)),
                pl.BlockSpec((1, 1, rows), lambda s, p, b: (s, 0, 0)),
                tile,
                tile,
                tile,
            ],
            out_specs=[tile, many],
        ),
        out_shape=[
            jax.ShapeDtypeStruct((seqs, rows, width), bf16),
            jax.ShapeDtypeStruct(pairs_full.shape, bf16),
        ],
        compiler_params=params(2),
        cost_estimate=cost(
            10 * seqs * rows * rows * blocks * width, 8 * seqs * rows * blocks * width
        ),
        name="attn_bwd",
    )(bounds, queries, pairs_full, seg_col, seg_row, out_grad, out_full, log_total)


def feed_in(normed, weight, bias, groups):
    tokens, width = normed.shape
    parts, _, n = weight.shape
    ratio = parts // groups

    def kernel(x_ref, w_ref, b_ref, inner_ref, act_ref):
        place = lax.rem(pl.program_id(0), ratio)
        u = dot_nn(x_ref[...], w_ref[0]) + b_ref[0]
        act = (0.5 * u * (1.0 + jnp.tanh(GELU_C * (u + GELU_A * u * u * u)))).astype(bf16)
        for r in range(ratio):

            @pl.when(place == r)
            def _():
                inner_ref[0, :, r * n : (r + 1) * n] = u
                act_ref[0, :, r * n : (r + 1) * n] = act

    out = pl.BlockSpec((1, tokens, ratio * n), lambda d: (d // ratio, 0, 0))
    return pl.pallas_call(
        kernel,
        grid=(parts,),
        in_specs=[
            pl.BlockSpec((tokens, width), lambda d: (0, 0)),
            pl.BlockSpec((1, width, n), lambda d: (d, 0, 0)),
            pl.BlockSpec((1, 1, n), lambda d: (d, 0, 0)),
        ],
        out_specs=[out, out],
        out_shape=[
            jax.ShapeDtypeStruct((groups, tokens, ratio * n), f32),
            jax.ShapeDtypeStruct((groups, tokens, ratio * n), bf16),
        ],
        compiler_params=params(),
        cost_estimate=cost(2 * tokens * width * parts * n, 2 * width * parts * n),
        name="fc",
    )(normed, weight, bias)


def feed_out(act, weight, hidden, bias):
    groups, tokens, f = act.shape
    width = weight.shape[1]

    def kernel(a_ref, w_ref, h_ref, b_ref, o_ref, acc_ref):
        step = pl.program_id(0)

        @pl.when(step == 0)
        def _():
            acc_ref[...] = h_ref[...] + b_ref[...]

        acc_ref[...] += dot_nt(a_ref[0], w_ref[0])

        @pl.when(step == groups - 1)
        def _():
            o_ref[...] = acc_ref[...].astype(bf16)

    return pl.pallas_call(
        kernel,
        grid=(groups,),
        in_specs=[
            pl.BlockSpec((1, tokens, f), lambda c: (c, 0, 0)),
            pl.BlockSpec((1, width, f), lambda c: (c, 0, 0)),
            pl.BlockSpec((tokens, width), lambda c: (0, 0)),
            pl.BlockSpec((1, width), lambda c: (0, 0)),
        ],
        out_specs=pl.BlockSpec((tokens, width), lambda c: (0, 0)),
        out_shape=jax.ShapeDtypeStruct((tokens, width), bf16),
        scratch_shapes=[pltpu.VMEM((tokens, width), f32)],
        compiler_params=params(),
        cost_estimate=cost(2 * groups * tokens * width * f, 2 * groups * width * f),
        name="proj",
    )(act, weight, hidden, bias)


def feed_back(grad, weight, inner, parts):
    groups, tokens, f = inner.shape
    width = weight.shape[1]
    ratio = parts // groups
    n = f // ratio

    def kernel(g_ref, w_ref, u_ref, o_ref, s_ref):
        u = u_ref[0]
        t = jnp.tanh(GELU_C * (u + GELU_A * u * u * u))
        slope = 0.5 * (1.0 + t) + 0.5 * u * (1.0 - t * t) * (
            GELU_C * (1.0 + 3.0 * GELU_A * u * u)
        )
        out = (dot_nn(g_ref[...], w_ref[0]) * slope).astype(bf16)
        total = jnp.sum(out.astype(f32), axis=0, keepdims=True)
        for r in range(ratio):
            o_ref[r] = out[:, r * n : (r + 1) * n]
            s_ref[r] = total[:, r * n : (r + 1) * n]

    return pl.pallas_call(
        kernel,
        grid=(groups,),
        in_specs=[
            pl.BlockSpec((tokens, width), lambda c: (0, 0)),
            pl.BlockSpec((1, width, f), lambda c: (c, 0, 0)),
            pl.BlockSpec((1, tokens, f), lambda c: (c, 0, 0)),
        ],
        out_specs=[
            pl.BlockSpec((ratio, tokens, n), lambda c: (c, 0, 0)),
            pl.BlockSpec((ratio, 1, n), lambda c: (c, 0, 0)),
        ],
        out_shape=[
            jax.ShapeDtypeStruct((parts, tokens, n), bf16),
            jax.ShapeDtypeStruct((parts, 1, n), f32),
        ],
        compiler_params=params(),
        cost_estimate=cost(2 * groups * tokens * width * f, 6 * groups * width * f),
        name="act_bwd",
    )(grad, weight, inner)


def back_project(grads, weight):
    parts, tokens, n = grads.shape
    width = weight.shape[1]

    def kernel(g_ref, w_ref, o_ref):
        @pl.when(pl.program_id(0) == 0)
        def _():
            o_ref[...] = dot_nt(g_ref[0], w_ref[0])

        @pl.when(pl.program_id(0) > 0)
        def _():
            o_ref[...] += dot_nt(g_ref[0], w_ref[0])

    return pl.pallas_call(
        kernel,
        grid=(parts,),
        in_specs=[
            pl.BlockSpec((1, tokens, n), lambda d: (d, 0, 0)),
            pl.BlockSpec((1, width, n), lambda d: (d, 0, 0)),
        ],
        out_specs=pl.BlockSpec((tokens, width), lambda d: (0, 0)),
        out_shape=jax.ShapeDtypeStruct((tokens, width), f32),
        compiler_params=params(),
        cost_estimate=cost(2 * parts * tokens * width * n, 2 * parts * width * n),
        name="back",
    )(grads, weight)


def weight_grad(left, right, picks, arrived=None):
    rows, tokens = left.shape
    n = right.shape[2]
    count = picks.shape[0]

    def kernel(picks_ref, a_ref, b_ref, *refs):
        y = dot_nn(a_ref[...], b_ref[0])
        if arrived is not None:
            y = y + refs[0][0].astype(f32)
        refs[-1][0] = y.astype(bf16)

    block = pl.BlockSpec((1, rows, n), lambda j, picks: (j, 0, 0))
    return pl.pallas_call(
        kernel,
        grid_spec=pltpu.PrefetchScalarGridSpec(
            num_scalar_prefetch=1,
            grid=(count,),
            in_specs=[
                pl.BlockSpec((rows, tokens), lambda j, picks: (0, 0)),
                pl.BlockSpec((1, tokens, n), lambda j, picks: (picks[j], 0, 0)),
            ]
            + ([block] if arrived is not None else []),
            out_specs=block,
        ),
        out_shape=jax.ShapeDtypeStruct((count, rows, n), bf16),
        compiler_params=params(),
        cost_estimate=cost(2 * count * rows * tokens * n, 2 * count * rows * n),
        name="wgrad",
    )(picks, left, right, *(() if arrived is None else (arrived,)))


MESH = pl.DeviceIdType.MESH


def far_first(k, z, nz):
    low = z < nz // 2
    me = jnp.where(low, z, nz - 1 - z)
    got = jnp.where(k < nz - 1 - me, nz - 1 - k, jnp.where(k == nz - 1, me, nz - 2 - k))
    return jnp.where(low, got, nz - 1 - got)


def summed_grads(grid, collective_id, operands, unit, shape, cut, name):
    rows, n = shape
    ra, rb = cut, rows - cut
    nz = grid.nz
    count = len(operands)

    def kernel(*refs):
        ins, out = refs[:count], refs[count]
        (sa, sb, ga, gb, oa, ob, xa, yb, ta, tb, ya, xb, la, lb, za, zb, ua, ub, da, db, ss, rs, zr) = refs[count + 1 :]
        d, c = lax.axis_index("dp"), lax.axis_index("ctx")
        z, y = d // grid.ny, d % grid.ny
        x, core = c // 2, c % 2
        at_sib = (d, c + 1 - 2 * core)
        at_x = (d, (1 - x) * 2 + core)
        at_y = (z * grid.ny + 1 - y, c)
        at_up = ((z + 1) * grid.ny + y, c)
        at_down = ((z - 1) * grid.ny + y, c)
        has_up, has_down = z < nz - 1, z > 0

        barrier = pltpu.get_barrier_semaphore()
        for target in (at_sib, at_x, at_y):
            pl.semaphore_signal(barrier, inc=1, device_id=target, device_id_type=MESH)

        @pl.when(has_up)
        def _():
            pl.semaphore_signal(barrier, inc=1, device_id=at_up, device_id_type=MESH)

        @pl.when(has_down)
        def _():
            pl.semaphore_signal(barrier, inc=1, device_id=at_down, device_id_type=MESH)

        pl.semaphore_wait(barrier, 3 + has_up.astype(jnp.int32) + has_down.astype(jnp.int32))

        def copy(src, dst, kind, k, target):
            return pltpu.make_async_remote_copy(
                src_ref=src,
                dst_ref=dst,
                send_sem=ss.at[kind, k],
                recv_sem=rs.at[kind, k],
                device_id=target,
                device_id_type=MESH,
            )

        def sib(k):
            s = k % 2
            return copy(sa.at[s], ga.at[k], 0, k, at_sib), copy(sb.at[s], gb.at[k], 1, k, at_sib)

        def first(k):
            s = k % 2
            return (
                copy(oa.at[s, 1 - x], xa.at[k], 2, k, at_x),
                copy(ob.at[s, 1 - y], yb.at[k], 3, k, at_y),
            )

        def second(k):
            s = k % 2
            return copy(ta.at[s], ya.at[k], 4, k, at_y), copy(tb.at[s], xb.at[k], 5, k, at_x)

        def line(k, to, up):
            dst = (ua, ub) if up else (da, db)
            target = at_up if up else at_down
            way = 0 if up else 1
            return [
                pltpu.make_async_remote_copy(
                    src_ref=(za, zb)[h].at[k],
                    dst_ref=dst[h].at[to],
                    send_sem=ss.at[6 + h, k],
                    recv_sem=zr.at[way, h, to],
                    device_id=target,
                    device_id_type=MESH,
                )
                for h in range(2)
            ]

        def step(t, _):
            @pl.when(t < nz)
            def _():
                k, s = t, t % 2
                to = far_first(k, z, nz)

                @pl.when(k >= 2)
                def _():
                    for cp in sib(k - 2):
                        cp.wait_send()
                    for cp in first(k - 2):
                        cp.wait_send()

                def store_sib(y_to, x_to, value):
                    sa[s, x_to, y_to] = value[:ra].astype(bf16)
                    sb[s, y_to, x_to] = value[ra:].astype(bf16)

                unit(ins, 1 - core, to, store_sib)
                for cp in sib(k):
                    cp.start()
                waits = sib(k)
                done = []

                def store_own(y_to, x_to, value):
                    if not done:
                        done.append(True)
                        for cp in waits:
                            cp.wait_recv()
                    oa[s, x_to, y_to] = (value[:ra] + ga[k, x_to, y_to].astype(f32)).astype(bf16)
                    ob[s, y_to, x_to] = (value[ra:] + gb[k, y_to, x_to].astype(f32)).astype(bf16)

                unit(ins, core, to, store_own)
                for cp in first(k):
                    cp.start()

            @pl.when((t >= 1) & (t <= nz))
            def _():
                k, s = t - 1, (t - 1) % 2

                @pl.when(k >= 2)
                def _():
                    for cp in second(k - 2):
                        cp.wait_send()

                one, two = first(k)
                one.wait_recv()
                ta[s] = (oa[s, x, 1 - y].astype(f32) + xa[k, 1 - y].astype(f32)).astype(bf16)
                go_a, go_b = second(k)
                go_a.start()
                la[s] = oa[s, x, y].astype(f32) + xa[k, y].astype(f32)
                two.wait_recv()
                tb[s] = (ob[s, y, 1 - x].astype(f32) + yb[k, 1 - x].astype(f32)).astype(bf16)
                go_b.start()
                lb[s] = ob[s, y, x].astype(f32) + yb[k, x].astype(f32)

            @pl.when(t >= 2)
            def _():
                k, s = t - 2, t % 2
                to = far_first(k, z, nz)
                one, two = second(k)
                one.wait_recv()
                two.wait_recv()
                la[s] = la[s] + ya[k].astype(f32)
                lb[s] = lb[s] + xb[k].astype(f32)
                for up in (True, False):
                    behind = has_down if up else has_up

                    @pl.when(((to > z) if up else (to < z)) & behind)
                    def _():
                        for cp in line(k, to, up):
                            cp.wait_recv()
                        la[s] = la[s] + (ua, da)[0 if up else 1][to].astype(f32)
                        lb[s] = lb[s] + (ub, db)[0 if up else 1][to].astype(f32)

                    @pl.when((to > z) if up else (to < z))
                    def _():
                        za[k] = la[s].astype(bf16)
                        zb[k] = lb[s].astype(bf16)
                        for cp in line(k, to, up):
                            cp.start()

            return 0

        lax.fori_loop(0, nz + 2, step, 0)
        last = (nz - 1) % 2
        for up in (True, False):

            @pl.when(has_down if up else has_up)
            def _():
                for cp in line(nz - 1, z, up):
                    cp.wait_recv()
                la[last] = la[last] + (ua, da)[0 if up else 1][z].astype(f32)
                lb[last] = lb[last] + (ub, db)[0 if up else 1][z].astype(f32)

        out[:ra] = la[last]
        out[ra:] = lb[last]
        for k in range(nz - 2, nz):
            for cp in (*sib(k), *first(k), *second(k)):
                cp.wait_send()
        for k in range(nz - 1):
            for cp in line(k, 0, True):
                cp.wait_send()

    def vm(*dims, dtype=bf16):
        return pltpu.VMEM(dims, dtype)

    halves = [
        *(vm(2, 2, 2, h, n) for h in (ra, rb)),
        *(vm(nz, 2, 2, h, n) for h in (ra, rb)),
        *(vm(2, 2, 2, h, n) for h in (ra, rb)),
        *(vm(nz, 2, h, n) for h in (ra, rb)),
        *(vm(2, h, n) for h in (ra, rb)),
        *(vm(nz, h, n) for h in (ra, rb)),
        *(vm(2, h, n, dtype=f32) for h in (ra, rb)),
        *(vm(nz, h, n) for h in (ra, rb)),
        *(vm(nz, h, n) for h in (ra, rb)),
        *(vm(nz, h, n) for h in (ra, rb)),
    ]
    flops = sum(2 * 2 * 2 * nz * grid.ny * rows * n * 512 for _ in range(1))
    return pl.pallas_call(
        kernel,
        out_shape=jax.ShapeDtypeStruct((rows, n), f32),
        in_specs=[pl.BlockSpec(memory_space=pltpu.VMEM)] * count,
        out_specs=pl.BlockSpec(memory_space=pltpu.VMEM),
        scratch_shapes=[
            *halves,
            pltpu.SemaphoreType.DMA((8, nz)),
            pltpu.SemaphoreType.DMA((6, nz)),
            pltpu.SemaphoreType.DMA((2, 2, nz)),
        ],
        compiler_params=pltpu.CompilerParams(
            collective_id=collective_id, has_side_effects=True, vmem_limit_bytes=VMEM_LIMIT
        ),
        cost_estimate=cost(flops, 100_000_000),
        name=name,
    )(*operands)


def pick(array, index, axis):
    return lax.dynamic_index_in_dim(array, index, axis, keepdims=False)


def add_low(first, second):
    return (first.astype(f32) + second.astype(f32)).astype(bf16)


class Grid:
    def __init__(self, dp, ctx):
        self.dp, self.ctx = dp, ctx
        self.nx = max(ctx // 2, 1)
        self.ny = self.nx
        self.nz = dp // self.ny
        self.paired = self.nx == 2 and ctx == 4 and dp % 2 == 0

    def place(self):
        d, c = lax.axis_index("dp"), lax.axis_index("ctx")
        self.d, self.c = d, c
        self.z, self.y = d // self.ny, d % self.ny
        self.x, self.core = c // 2, c % 2

    def swap_core(self, v):
        return lax.ppermute(v, "ctx", [(i, i ^ 1) for i in range(self.ctx)])


def on_device(grid, *args):
    (
        layer_input,
        grad_out,
        segment_ids,
        qkv_weight,
        q_bias,
        v_bias,
        out_weight,
        out_bias,
        fc_weight,
        fc_bias,
        proj_weight,
        proj_bias,
        ln1_gain,
        ln1_bias,
        ln2_gain,
        ln2_bias,
    ) = args
    seqs, rows, width = layer_input.shape
    tokens = seqs * rows
    parts, groups = grid.dp, grid.ctx
    both = ("dp", "ctx")
    grid.place()

    vectors = (q_bias, v_bias, out_bias, proj_bias, ln1_gain, ln1_bias, ln2_gain, ln2_bias, fc_bias)
    sizes = [v.shape[0] for v in vectors]
    packed = lax.all_gather(jnp.concatenate(vectors), "dp", axis=0)
    spread, at = [], 0
    for size in sizes:
        spread.append(packed[:, at : at + size].astype(f32))
        at += size
    q_all, v_all, ob_all, pb_all, g1, b1, g2, b2 = [v.reshape(-1) for v in spread[:8]]
    fcb = spread[8][:, None, :]

    def gather(block, axes):
        return lax.all_gather(block, axes, axis=0)

    n_qkv, n_out, n_fc = qkv_weight.shape[1], out_weight.shape[1], fc_weight.shape[1]
    slab, hidden_slab = qkv_weight.shape[0], proj_weight.shape[0]
    w_qkv = gather(qkv_weight, both).reshape(parts, width, n_qkv)
    w_out = gather(out_weight, both).reshape(parts, width, n_out)
    w_fc = gather(fc_weight, both).reshape(parts, width, n_fc)
    w_proj = gather(proj_weight.T, ("ctx", "dp")).reshape(groups, width, hidden_slab)
    out_full = w_out.transpose(1, 0, 2).reshape(width, width)

    values = layer_input.reshape(tokens, width).astype(f32)
    normed1 = layer_norm(values, g1, b1).astype(bf16)
    joined = jnp.concatenate([q_all, jnp.zeros((width,), f32), v_all]).reshape(parts, 1, n_qkv)
    queries, key_rows, value_rows = qkv_project(normed1, w_qkv, joined)
    queries = queries.reshape(seqs, rows, width)
    own = jnp.stack([key_rows, value_rows]).reshape(2, seqs, rows, width)
    if grid.paired:
        other = lax.ppermute(own, "ctx", [(0, 2), (1, 3)])
        column = jnp.where(grid.x == 0, jnp.stack([own, own]), jnp.stack([other, own]))
        sibling = grid.swap_core(column)
        even = jnp.where(grid.core == 0, column, sibling)
        odd = jnp.where(grid.core == 0, sibling, column)
        pairs_full = jnp.stack([even, odd], axis=1).reshape(groups, 2, seqs, rows, width)
    else:
        pairs_full = lax.all_gather(own, "ctx", axis=0)

    seg_blocks = segment_ids.reshape(seqs, groups, rows)
    seg_mine = pick(seg_blocks, grid.c, 1)
    needed = seg_blocks[:, :, -1] >= seg_mine[:, :1]
    start = jnp.minimum(jnp.argmax(needed, axis=1).astype(jnp.int32), grid.c)
    bounds = jnp.concatenate([grid.c[None].astype(jnp.int32), start])
    attended, attended_f32, log_total = attention_forward(
        bounds, queries, pairs_full, seg_mine[:, :, None], seg_blocks[:, :, None, :]
    )
    attended = attended.reshape(tokens, width)
    hidden = values + jnp.dot(attended, out_full, preferred_element_type=f32) + ob_all
    normed2 = layer_norm(hidden, g2, b2).astype(bf16)
    inner, activated = feed_in(normed2, w_fc, fcb, groups)
    output = feed_out(activated, w_proj, hidden, pb_all[None])

    mlp_grad = grad_out.reshape(tokens, width)
    cotangent = mlp_grad.astype(f32)
    proj_bias_grad = jnp.sum(cotangent, axis=0)
    inner_grad, fc_bias_grad = feed_back(mlp_grad, w_proj, inner, parts)

    def tall_cut(size):
        return (size // 2 + 15) // 16 * 16

    def by_columns(refs, core, z, store):
        for y_to in range(2):
            for x_to in range(2):
                at = pl.ds(pl.multiple_of((2 * x_to + core) * slab, 16), slab)
                terms = [
                    dot_nn(left[at, :], right[z * grid.ny + y_to])
                    for left, right in zip(refs[::2], refs[1::2])
                ]
                store(y_to, x_to, jnp.concatenate(terms, axis=1) if len(terms) > 1 else terms[0])

    def by_rows(refs, core, z, store):
        left, right = refs
        cols = width // parts
        at = pl.ds(pl.multiple_of(z * (grid.ny * cols), 16), grid.ny * cols)
        for x_to in range(2):
            term = dot_nn(left[at, :], right[2 * x_to + core])
            for y_to in range(2):
                store(y_to, x_to, term[y_to * cols : (y_to + 1) * cols])

    def reduced(pairs, collective_id, name):
        if not grid.paired:
            everything = jnp.arange(parts, dtype=jnp.int32)
            results = []
            for left, right in pairs:
                whole = weight_grad(left.T, right, everything)
                whole = whole.reshape(parts * groups, slab, right.shape[2])
                results.append(lax.psum_scatter(whole, both, scatter_dimension=0).astype(f32))
            return results
        operands, ends = [], [0]
        for left, right in pairs:
            n = right.shape[2]
            full = n if len(ends) == len(pairs) else pl.cdiv(n, LANES) * LANES
            operands += [left.T, jnp.pad(right, ((0, 0), (0, 0), (0, full - n)))]
            ends.append(ends[-1] + full)
        total = summed_grads(
            grid, collective_id, operands, by_columns, (slab, ends[-1]), tall_cut(slab), name
        )
        return [total[:, at : at + pair[1].shape[2]] for at, pair in zip(ends, pairs)]

    def reduced_proj(left, right):
        f = right.shape[2]
        cols = width // parts
        if not grid.paired:
            whole = weight_grad(left.T, right, jnp.arange(groups, dtype=jnp.int32))
            whole = whole.reshape(groups * parts, cols, f)
            return lax.psum_scatter(whole, ("ctx", "dp"), scatter_dimension=0).astype(f32)
        return summed_grads(grid, 1, [left.T, right], by_rows, (cols, f), tall_cut(cols), "rs_proj")

    proj_weight_grad = reduced_proj(mlp_grad, activated).T
    (fc_weight_grad,) = reduced([(normed2, inner_grad)], 2, "rs_fc")

    normed2_grad = back_project(inner_grad, w_fc)
    norm2_out, norm2_pull = jax.vjp(layer_norm, hidden, g2, b2)
    hidden_ln, g2_grad, b2_grad = norm2_pull(normed2_grad)
    hidden_grad = cotangent + hidden_ln
    branch_grad = hidden_grad.astype(bf16)
    out_bias_grad = jnp.sum(branch_grad, axis=0, dtype=f32)
    attended_grad = jnp.einsum(
        "nd,ed->ne", branch_grad, out_full, preferred_element_type=f32
    ).astype(bf16)
    branch_parts = branch_grad.reshape(tokens, parts, n_out).transpose(1, 0, 2)

    query_grad, pairs_grad = attention_backward(
        bounds,
        queries,
        pairs_full,
        seg_blocks[:, :, :, None],
        seg_mine[:, None, :],
        attended_grad.reshape(seqs, rows, width),
        attended_f32,
        log_total,
    )
    if grid.paired:
        by_chip = pairs_grad.reshape(2, 2, 2, seqs, rows, width)
        plane = add_low(
            pick(by_chip, grid.core, 1), grid.swap_core(pick(by_chip, 1 - grid.core, 1))
        )
        came = lax.ppermute(plane[0], "ctx", [(2, 0), (3, 1)])
        pair_grad = add_low(pick(plane, grid.x, 0), came)
    else:
        pair_grad = lax.psum_scatter(pairs_grad, "ctx", scatter_dimension=0)
    pair_grad = pair_grad.reshape(2, tokens, width)
    projected_grad = jnp.concatenate(
        [query_grad.reshape(tokens, width), pair_grad[0], pair_grad[1]], axis=1
    )
    q_bias_grad = jnp.sum(query_grad.reshape(tokens, width), axis=0, dtype=f32)
    v_bias_grad = jnp.sum(pair_grad[1], axis=0, dtype=f32)
    by_part = projected_grad.reshape(tokens, parts, n_qkv).transpose(1, 0, 2)
    out_weight_grad, qkv_weight_grad = reduced(
        [(attended, branch_parts), (normed1, by_part)], 3, "rs_qkv"
    )
    normed1_grad = back_project(by_part, w_qkv)
    norm1_out, norm1_pull = jax.vjp(layer_norm, values, g1, b1)
    values_ln, g1_grad, b1_grad = norm1_pull(normed1_grad)
    input_grad = hidden_grad + values_ln

    sums = [q_bias_grad, v_bias_grad, out_bias_grad, proj_bias_grad, g1_grad, b1_grad, g2_grad, b2_grad]
    stacked = jnp.concatenate(
        [v.reshape(parts, -1) for v in sums] + [fc_bias_grad.reshape(parts, -1)], axis=1
    )
    total = pick(lax.psum(stacked, both), grid.d, 0)
    vec, at = [], 0
    for size in sizes:
        vec.append(total[at : at + size])
        at += size
    return (
        output.reshape(seqs, rows, width),
        input_grad.reshape(seqs, rows, width),
        qkv_weight_grad,
        vec[0],
        vec[1],
        out_weight_grad,
        vec[2],
        fc_weight_grad,
        vec[8],
        proj_weight_grad,
        vec[3],
        vec[4],
        vec[5],
        vec[6],
        vec[7],
    )


def solution(mesh):
    rows3, mat, vec = P("dp", "ctx", None), P("ctx", "dp"), P("dp")
    grid = Grid(mesh.shape["dp"], mesh.shape["ctx"])
    return jax.shard_map(
        functools.partial(on_device, grid),
        mesh=mesh,
        in_specs=(
            rows3,
            rows3,
            P("dp", None),
            mat,
            vec,
            vec,
            mat,
            vec,
            mat,
            vec,
            mat,
            vec,
            vec,
            vec,
            vec,
            vec,
        ),
        out_specs=(
            rows3,
            rows3,
            mat,
            vec,
            vec,
            mat,
            vec,
            mat,
            vec,
            mat,
            vec,
            vec,
            vec,
            vec,
            vec,
        ),
        check_vma=False,
    )
```

time: 3030 us -> 1210 us (0.40)
  waiting for transfers between devices: 2070 us -> 253 us
  Pallas kernels: 0 us -> 602 us
  matrix products: 505 us -> 11.6 us
  blocking collectives: 131 us -> 39.9 us
    all_gather x19 -> x4, waiting for transfers between devices: 1210 us -> 171 us  [gather(): return lax.all_gather(block, axes, axis=0)]
    pallas_call x0 -> x11, Pallas kernels: none -> 602 us  [the longest x3 408 us: summed_grads(): pl.pallas_call(kernel, out_shape=jax.ShapeDtypeStruct((rows, n), f32), in...]
    unnamed x33 -> x5, waiting for transfers between devices: 601 us -> 2.6 us
    dot_general x96 -> x2, matrix products: 505 us -> 11.6 us  [the longest x1 5.84 us: on_device(): jnp.dot(attended, out_full, preferred_element_type=f32)]
    all_to_all x5 -> x0, waiting for transfers between devices: 133 us -> none  [the longest x2 83 us: on_device(): lax.all_to_all(activated, 'ctx', split_axis=1, concat_axis=0, tiled=True)]
    reduce_scatter x4 -> x0, waiting for transfers between devices: 118 us -> none  [the longest x2 60.3 us: on_device(): lax.psum_scatter(key_grad, 'ctx', scatter_dimension=1, tiled=True)]
    ppermute x0 -> x4, waiting for transfers between devices: none -> 79.1 us  [the longest x1 79.1 us: on_device(): other = lax.ppermute(own, 'ctx', [(0, 2), (1, 3)])]
    all_to_all x3 -> x0, blocking collectives: 71.6 us -> none  [the longest x1 24.7 us: on_device(): lax.all_to_all(attended, 'ctx', split_axis=1, concat_axis=0, tiled=True)]
  transfers between devices with their start and end apart: 33 -> 9, of which waited for: 23 -> 4; matrix products, arithmetic and copies ran while one was open for 19% -> 13% of each run, Pallas kernels for 0% -> 43%
where the time goes in v1:
time: 1210 us; the launch traced here: 1190 us
  Pallas kernels  602 us (50%)
  waiting for transfers between devices  253 us (21%)
  local copies, waits for them, and re-layouts  182 us (15%)
  other arithmetic  73.3 us (6%)
  blocking collectives  39.9 us (3%)
  between operations  15.4 us (1%)
  starting transfers between devices  14.4 us (1%)
    pallas_call x3, Pallas kernels, summed_grads(): pl.pallas_call(kernel, out_shape=jax.ShapeDtypeStruct((rows, n), f32), in...  408 us
    all_gather x4, waiting for transfers between devices, gather(): return lax.all_gather(block, axes, axis=0)  171 us
    ppermute x1, waiting for transfers between devices, on_device(): other = lax.ppermute(own, 'ctx', [(0, 2), (1, 3)])  79.1 us
    unnamed x1, blocking collectives  39.9 us
    pallas_call x2, Pallas kernels, back_project(): pl.pallas_call(kernel, grid=(parts,), in_specs=[pl.BlockSpec((1, tokens,...  37.6 us
    pallas_call x1, Pallas kernels, attention_backward(): pl.pallas_call(kernel, grid_spec=pltpu.PrefetchScalarGridSpec(num_scalar_...  30.8 us
    pallas_call x1, Pallas kernels, feed_in(): pl.pallas_call(kernel, grid=(parts,), in_specs=[pl.BlockSpec((tokens, wid...  30.4 us
    pallas_call x1, Pallas kernels, attention_forward(): pl.pallas_call(kernel, grid_spec=pltpu.PrefetchScalarGridSpec(num_scalar_...  29.7 us
  transfers between devices with their start and end apart: 9, of which 4 were waited for; matrix products, arithmetic and copies ran while one was open for 13% of the time, Pallas kernels for 43%

profile of v1, /device:TPU:0, one launch (start us, length us, event | category | flops | bytes accessed | tf_op | source)
XLA Modules:
  0.0 1191.4 jit_solution(1776015557226265491)
XLA Ops:
  11.9 6.1 concatenate.18
  18.4 39.9 %all-reduce.1 = bf16[19200]{0:T(1024)(128)(2,1)S(1)} all-reduce(bf16[19200]{0:T(1024)(128)(2,1)S(1)} %dynamic-update-slice), channel_id=2, replica_groups=mesh['dp'=8,'ctx'=4] {'dp'}, use_global_device_ids=true, to_apply=%add.1 | all-reduce | flops 19200 | bytes 76800
  69.4 57.5 %all-gather.10.cloned.1.call-done = bf16[12800,600]{1,0:T(8,128)(2,1)} async-done(((bf16[400,600]{1,0:T(8,128)(2,1)}), bf16[12800,600]{1,0:T(8,128)(2,1)}) %all-gather.10.cloned.1.call-update) | async-done | bytes 15360016 | tf_op jit(solution)/shard_map/all_gather | solution.py:714
  127.0 19.3 %qkv.1 = (bf16[512,1600]{1,0:T(8,128)(2,1)}, bf16[512,1600]{1,0:T(8,128)(2,1)}, bf16[512,1600]{1,0:T(8,128)(2,1)}) custom-call(bf16[512,1600]{1,0:T(8,128)(2,1)} %copy.94.x_ref, bf16[8,1600,600]{2,1,0:T(8,128)(2,1)} %bitcast.157, f32[8,1,600]{2,1,0:T(1,128)} %reshape.249.b_ref), custom_call_target="tpu_custom_call" | custom-call | flops 7864320000 | bytes 15360000 | tf_op jit(solution)/shard_map/qkv/pallas_call | solution.py:73
  153.4 3.9 pad_maximum_fusion.3
  157.3 5.2 collective-permute-start
  162.5 3.6 copy.96
  169.7 79.1 %collective-permute-done = bf16[2,2,256,1600]{2,3,1,0:T(8,128)(2,1)} collective-permute-done((bf16[2,2,256,1600]{2,3,1,0:T(8,128)(2,1)}, bf16[2,2,256,1600]{2,3,1,0:T(8,128)(2,1)}, u32[]{:S(2)}, u32[]{:S(2)}) %collective-permute-start) | collective-permute-done | bytes 3276832 | tf_op jit(solution)/shard_map/ppermute | solution.py:731
  248.8 7.5 maximum_select_fusion
  263.4 3.6 copy.107.g_ref
  268.6 8.5 copy.103
  277.1 7.5 select_bitcast_fusion.1
  284.6 6.0 pad_maximum_fusion
  290.6 18.4 %copy.99 = bf16[2,2,2,2,256,1600]{5,4,3,2,1,0:T(8,128)(2,1)} copy(bf16[2,2,2,2,256,1600]{4,5,3,2,0,1:T(8,128)(2,1)} %pad_maximum_fusion) | data formatting | bytes 26214400 | tf_op jit(solution)/shard_map/stack | solution.py:736
  309.0 29.7 %attn_fwd.1 = (bf16[2,256,1600]{2,1,0:T(8,128)(2,1)}, f32[2,256,1600]{2,1,0:T(8,128)}, f32[2,256,1600]{2,1,0:T(8,128)}) custom-call(s32[3]{0:T(128)} %pad_add_fusion.bounds_ref, bf16[2,256,1600]{2,1,0:T(8,128)(2,1)} %bitcast.131, bf16[4,2,2,256,1600]{4,3,2,1,0:T(8,128)(2,1)} %bitcast.97, s32[2,256,1]{2,1,0:T(8,128)} %broadcast_in_dim.45.sc_ref, ...), custom_call_target="tpu_custom_call" | custom-call | flops 3355443200 | bytes 13107200 | tf_op jit(solution)/shard_map/attn_fwd/pallas_call | solution.py:147
  338.7 5.8 fusion.13
  351.7 7.3 all-gather.14.cloned.1.call-done
  359.0 30.4 %fc.1 = (f32[4,512,1600]{2,1,0:T(8,128)}, bf16[4,512,1600]{2,1,0:T(8,128)(2,1)}) custom-call(bf16[512,1600]{1,0:T(8,128)(2,1)} %copy.104.x_ref, bf16[8,1600,800]{2,1,0:T(8,128)(2,1)} %bitcast.153, f32[8,1,800]{2,1,0:T(1,128)} %reshape.284.b_ref), custom_call_target="tpu_custom_call" | custom-call | flops 10485760000 | bytes 20480000 | tf_op jit(solution)/shard_map/fc/pallas_call | solution.py:277
  389.4 106.6 %all-gather.16.cloned.1.call-done = bf16[6400,1600]{1,0:T(8,128)(2,1)} async-done(((bf16[200,1600]{1,0:T(8,128)(2,1)}), bf16[6400,1600]{1,0:T(8,128)(2,1)}) %all-gather.16.cloned.1.call-update) | async-done | bytes 20480016 | tf_op jit(solution)/shard_map/all_gather | solution.py:714
  496.0 26.0 %act_bwd.1 = (bf16[8,512,800]{2,1,0:T(8,128)(2,1)}, f32[8,1,800]{2,1,0:T(1,128)}) custom-call(bf16[512,1600]{1,0:T(8,128)(2,1)} %copy.107.g_ref, bf16[4,1600,1600]{2,1,0:T(8,128)(2,1)} %bitcast.155, f32[4,512,1600]{2,1,0:T(8,128)} %get-tuple-element.34.u_ref), custom_call_target="tpu_custom_call" | custom-call | flops 10485760000 | bytes 61440000 | tf_op jit(solution)/shard_map/act_bwd/pallas_call | solution.py:349
  522.0 20.6 %back.2 = f32[512,1600]{1,0:T(8,128)} custom-call(bf16[8,512,800]{2,1,0:T(8,128)(2,1)} %get-tuple-element.35.g_ref.refs_1_, bf16[8,1600,800]{2,1,0:T(8,128)(2,1)} %bitcast.154), custom_call_target="tpu_custom_call" | custom-call | flops 10485760000 | bytes 20480000 | tf_op jit(solution)/shard_map/back/pallas_call | solution.py:384
  542.6 4.8 copy.108
  547.4 4.0 multiply_reduce_fusion
  556.1 5.8 convolution_convert_fusion
  561.9 3.6 copy.109
  565.5 30.8 %attn_bwd.1 = (bf16[2,256,1600]{2,1,0:T(8,128)(2,1)}, bf16[4,2,2,256,1600]{4,3,2,1,0:T(8,128)(2,1)}) custom-call(s32[3]{0:T(128)} %pad_add_fusion.bounds_ref, bf16[2,256,1600]{2,1,0:T(8,128)(2,1)} %bitcast.132, bf16[4,2,2,256,1600]{4,3,2,1,0:T(8,128)(2,1)} %bitcast.98, s32[2,4,256,1]{3,2,1,0:T(8,128)} %broadcast_in_dim_reshape.23.sc_ref, ...), custom_call_target="tpu_custom_call" | custom-call | flops 8388608000 | bytes 26214400 | tf_op jit(solution)/shard_map/attn_bwd/pallas_call | solution.py:232
  596.2 9.8 constant_dynamic-slice_fusion.2
  606.1 9.6 copy.112
  615.7 7.7 collective-permute-start.2
  627.9 9.6 copy.128
  637.5 9.0 fusion
  646.5 4.0 slice_bitcast_fusion
  653.7 4.6 copy.105.h_ref
  658.3 3.6 copy.123
  664.0 19.6 %proj.1 = bf16[512,1600]{1,0:T(8,128)(2,1)} custom-call(bf16[4,512,1600]{2,1,0:T(8,128)(2,1)} %get-tuple-element.33.a_ref.refs_1_, bf16[4,1600,1600]{2,1,0:T(8,128)(2,1)} %bitcast.156, f32[512,1600]{1,0:T(8,128)} %copy.105.h_ref, f32[1,1600]{1,0:T(1,128)} %reshape.285.b_ref), custom_call_target="tpu_custom_call" | custom-call | flops 10485760000 | bytes 20480000 | tf_op jit(solution)/shard_map/proj/pallas_call | solution.py:313
  683.6 3.6 copy.121
  687.2 3.6 copy.115
  690.8 3.7 copy.118
  698.6 163.2 %rs_fc.1 = f32[400,800]{1,0:T(8,128)} custom-call(bf16[1600,512]{1,0:T(8,128)(2,1)} %fusion.18.refs_0_, bf16[8,512,800]{2,1,0:T(8,128)(2,1)} %get-tuple-element.35.g_ref.refs_1_), custom_call_target="tpu_custom_call" | custom-call | flops 10485760000 | bytes 100000000 | tf_op jit(solution)/shard_map/rs_fc/pallas_call | solution.py:633
  861.8 118.4 %rs_proj.1 = f32[200,1600]{1,0:T(8,128)} custom-call(bf16[1600,512]{1,0:T(8,128)(2,1)} %bitcast.100, bf16[4,512,1600]{2,1,0:T(8,128)(2,1)} %get-tuple-element.33.a_ref.refs_1_), custom_call_target="tpu_custom_call" | custom-call | flops 10485760000 | bytes 100000000 | tf_op jit(solution)/shard_map/rs_proj/pallas_call | solution.py:633
  980.2 3.7 fusion.1
  984.4 10.3 copy.114
  995.1 10.0 copy.113
  1008.0 7.7 copy.116
  1015.7 17.0 %back.3 = f32[512,1600]{1,0:T(8,128)} custom-call(bf16[8,512,600]{2,1,0:T(8,128)(2,1)} %bitcast.124, bf16[8,1600,600]{2,1,0:T(8,128)(2,1)} %bitcast.158), custom_call_target="tpu_custom_call" | custom-call | flops 7864320000 | bytes 15360000 | tf_op jit(solution)/shard_map/back/pallas_call | solution.py:384
  1032.7 4.7 copy.117
  1044.9 126.8 %rs_qkv.1 = f32[400,856]{1,0:T(8,128)} custom-call(bf16[1600,512]{1,0:T(8,128)(2,1)} %bitcast.133, bf16[8,512,256]{2,1,0:T(8,128)(2,1)} %pad.4.refs_1_, bf16[1600,512]{1,0:T(8,128)(2,1)} %fusion.19.refs_2_, bf16[8,512,600]{2,1,0:T(8,128)(2,1)} %bitcast.125), custom_call_target="tpu_custom_call" | custom-call | flops 11219763200 | bytes 100000000 | tf_op jit(solution)/shard_map/rs_qkv/pallas_call | solution.py:633
  1171.7 3.8 add_add_fusion.2
  (148 shorter events, 80.5 us)
Async XLA Ops:
  7.2 51.3 %copy-start.8 = (bf16[2,256,1600]{1,2,0:T(8,128)(2,1)S(1)}, bf16[2,256,1600]{1,2,0:T(8,128)(2,1)}, u32[]{:S(2)}) copy-start(bf16[2,256,1600]{1,2,0:T(8,128)(2,1)} %param.16) | copy-start | bytes 4915204
  7.2 119.8 %all-gather.10.cloned.1.call-start = ((), (), s32[]{:S(2)}) async-start(), calls=%async_computation.1 | async-start | bytes 16896000 | tf_op jit(solution)/shard_map/all_gather | solution.py:714
  7.9 260.7 %all-gather.12.cloned.1.call-start = ((), (), s32[]{:S(2)}) async-start(), calls=%async_computation.2 | async-start | bytes 6758400 | tf_op jit(solution)/shard_map/all_gather | solution.py:714
  8.7 350.3 %all-gather.14.cloned.1.call-start = ((), (), s32[]{:S(2)}) async-start(), calls=%async_computation.3 | async-start | bytes 23654400 | tf_op jit(solution)/shard_map/all_gather | solution.py:714
  9.4 486.6 %all-gather.16.cloned.1.call-start = ((), (), s32[]{:S(2)}) async-start(), calls=%async_computation.4 | async-start | bytes 21964800 | tf_op jit(solution)/shard_map/all_gather | solution.py:714
  10.0 1169.3 %all-reduce.4.cloned.1.call-start = ((), (), s32[]{:S(2)}) async-start(), calls=%async_computation | async-start | bytes 155648 | tf_op jit(solution)/shard_map/psum | solution.py:862
  63.0 5.5 copy-start.17
  157.3 91.4 %collective-permute-start = (bf16[2,2,256,1600]{2,3,1,0:T(8,128)(2,1)}, bf16[2,2,256,1600]{2,3,1,0:T(8,128)(2,1)}, u32[]{:S(2)}, u32[]{:S(2)}) collective-permute-start(bf16[2,2,256,1600]{2,3,1,0:T(8,128)(2,1)} %pad_maximum_fusion.3), channel_id=1, source_target_pairs={{0,2},{1,3},{4,6},{5,7},{8,10},{9,11},{12,14},{13,15},{16,18},{17,... | collective-permute-start | bytes 9830408 | tf_op jit(solution)/shard_map/ppermute | solution.py:731
  248.8 7.5 copy-start.15
  256.3 20.9 %collective-permute-start.1 = (bf16[2,2,2,256,1600]{3,4,2,1,0:T(8,128)(2,1)}, bf16[2,2,2,256,1600]{3,4,2,1,0:T(8,128)(2,1)}, u32[]{:S(2)}, u32[]{:S(2)}) collective-permute-start(bf16[2,2,2,256,1600]{3,4,2,1,0:T(8,128)(2,1)} %maximum_select_fusion), channel_id=1, source_target_pairs={{0,1},{1,0},{2,3},{3,2},{4,5},{5,4},{6,7},{7,6},{8,9},{9,8},{10,11... | collective-permute-start | bytes 19660808 | tf_op jit(solution)/shard_map/ppermute | solution.py:675
  259.0 8.1 copy-start.19
  344.5 1.7 copy-start
  547.4 4.1 copy-start.1
  547.4 4.8 copy-start.5
  547.4 8.7 slice-start
  552.2 1.6 copy-start.6
  552.2 3.9 slice-start.1
  553.0 1.9 copy-start.4
  554.9 1.2 copy-start.11
  615.7 21.8 %collective-permute-start.2 = (bf16[2,2,2,256,1600]{3,4,2,1,0:T(8,128)(2,1)}, bf16[2,2,2,256,1600]{3,4,2,1,0:T(8,128)(2,1)}, u32[]{:S(2)}, u32[]{:S(2)}) collective-permute-start(bf16[2,2,2,256,1600]{3,4,2,1,0:T(8,128)(2,1)} %bitcast.116), channel_id=1, source_target_pairs={{0,1},{1,0},{2,3},{3,2},{4,5},{5,4},{6,7},{7,6},{8,9},{9,8},{10,11... | collective-permute-start | bytes 19660808 | tf_op jit(solution)/shard_map/ppermute | solution.py:675
  646.5 5.3 copy-start.2
  650.4 329.8 %collective-permute-start.3 = (bf16[2,2,256,1600]{2,3,1,0:T(8,128)(2,1)}, bf16[2,2,256,1600]{2,3,1,0:T(8,128)(2,1)}, u32[]{:S(2)}, u32[]{:S(2)}) collective-permute-start(bf16[2,2,256,1600]{2,3,1,0:T(8,128)(2,1)} %slice_bitcast_fusion), channel_id=1, source_target_pairs={{2,0},{3,1},{6,4},{7,5},{10,8},{11,9},{14,12},{15,13},{18,16},{19,... | collective-permute-start | bytes 9830408 | tf_op jit(solution)/shard_map/ppermute | solution.py:839
  694.5 3.4 copy-start.9
  694.5 4.1 copy-start.16
  995.1 10.5 copy-start.10
  1039.6 2.6 copy-start.18
  1039.6 2.9 copy-start.3
  1044.9 126.8 %copy-start.7 = (bf16[2,200,8,256]{3,2,0,1:T(8,128)(2,1)S(1)}, bf16[2,200,8,256]{3,2,0,1:T(8,128)(2,1)}, u32[]{:S(2)}) copy-start(bf16[2,200,8,256]{3,2,0,1:T(8,128)(2,1)} %copy.131) | copy-start | bytes 4915204
  1171.7 3.8 copy-start.13
  1177.3 4.9 copy-start.12
  1177.4 6.0 copy-start.14
Sparse Core Ops, SparseCore 0:
  10.9 116.0 all-gather.9
  129.8 68.8 all-gather.11
  201.6 157.3 all-gather.13
  361.7 134.3 all-gather.15
  1045.0 126.8 all-reduce.3

commit v2 on v1

--- a/solution.py
+++ b/solution.py
@@ -255,6 +255,194 @@
         ),
         name="attn_bwd",
     )(bounds, queries, pairs_full, seg_col, seg_row, out_grad, out_full, log_total)
+
+
+def causal(rows, transposed=False):
+    first = lax.broadcasted_iota(jnp.int32, (rows, rows), 0)
+    second = lax.broadcasted_iota(jnp.int32, (rows, rows), 1)
+    return first <= second if transposed else second <= first
+
+
+def pair_forward(extra, q, k, v, sk, sv, seg_q, seg_k, seg_sk, masks):
+    low, high, inside = masks
+    rows = q(0).shape[0]
+    zero = jnp.zeros((rows, LANES), bf16)
+    tri = causal(rows)
+
+    def heads_of(value):
+        scaled = value * jnp.asarray(0.125, bf16)
+        return jnp.where(low, scaled, zero), jnp.where(high, scaled, zero)
+
+    def clean(value):
+        return jnp.where(inside, value, zero)
+
+    def unit(q_heads, keys, values, allowed, state):
+        out = []
+        for head in range(2):
+            s = jnp.where(allowed, dot_nt(q_heads[head], keys), NEG_FILL)
+            top = jnp.max(s, axis=1, keepdims=True)
+            if state is None:
+                p = jnp.exp(s - top)
+                out.append((top, jnp.sum(p, axis=1, keepdims=True), dot_nn(p.astype(bf16), values)))
+            else:
+                m, l, acc = state[head]
+                new = jnp.maximum(m, top)
+                scale = jnp.exp(m - new)
+                p = jnp.exp(s - new)
+                out.append(
+                    (
+                        new,
+                        l * scale + jnp.sum(p, axis=1, keepdims=True),
+                        acc * scale + dot_nn(p.astype(bf16), values),
+                    )
+                )
+        return out
+
+    more = unit(
+        heads_of(q(extra)), clean(sk(extra)), clean(sv(extra)), seg_sk(extra) == seg_q(extra), None
+    )
+    results = []
+    for slot in range(2):
+        here = extra == slot
+        state = [
+            (jnp.where(here, m, NEG_FILL), jnp.where(here, l, 0.0), jnp.where(here, acc, 0.0))
+            for m, l, acc in more
+        ]
+        q_heads = heads_of(q(slot))
+        state = unit(
+            q_heads, clean(k(slot)), clean(v(slot)), (seg_k(slot) == seg_q(slot)) & tri, state
+        )
+        if slot == 1:
+            state = unit(q_heads, clean(k(0)), clean(v(0)), seg_k(0) == seg_q(1), state)
+            state = unit(q_heads, clean(sk(0)), clean(sv(0)), seg_sk(0) == seg_q(1), state)
+        (m0, l0, a0), (m1, l1, a1) = state
+        results.append(
+            (jnp.where(low, a0 / l0, a1 / l1), jnp.where(low, m0 + jnp.log(l0), m1 + jnp.log(l1)))
+        )
+    return results
+
+
+def pair_backward(extra, q, k, v, sk, sv, g, o, lse, seg_q, seg_k, seg_sk, masks):
+    low, high, inside = masks
+    rows = q(0).shape[0]
+    zero = jnp.zeros((rows, LANES), bf16)
+    tri = causal(rows, transposed=True)
+
+    def halves(value):
+        return jnp.where(low, value, zero), jnp.where(high, value, zero)
+
+    def queries(slot):
+        grad = g(slot)
+        product = jnp.where(inside, grad.astype(f32) * o(slot), 0.0).T
+        sums = jnp.where(inside, lse(slot), 0.0).T
+        return (
+            halves(q(slot) * jnp.asarray(0.125, bf16)),
+            halves(grad),
+            (
+                jnp.sum(product[:HEAD_DIM], axis=0, keepdims=True),
+                jnp.sum(product[HEAD_DIM:], axis=0, keepdims=True),
+            ),
+            (sums[0:1], sums[HEAD_DIM : HEAD_DIM + 1]),
+        )
+
+    def unit(side, keys, values, allowed):
+        q_heads, g_heads, delta, logs = side
+        keys, values = jnp.where(inside, keys, zero), jnp.where(inside, values, zero)
+        k_heads = halves(keys)
+        dq = dk = dv = None
+        for head in range(2):
+            s = jnp.where(allowed, dot_nt(keys, q_heads[head]), NEG_FILL)
+            p = jnp.exp(s - logs[head])
+            ds = (p * (dot_nt(values, g_heads[head]) - delta[head])).astype(bf16)
+            terms = (
+                dot_tn(ds, k_heads[head]),
+                dot_nn(ds, q_heads[head]),
+                dot_nn(p.astype(bf16), g_heads[head]),
+            )
+            dq, dk, dv = terms if dq is None else (dq + terms[0], dk + terms[1], dv + terms[2])
+        return dq, dk, dv
+
+    sides = [queries(0), queries(1)]
+    first = unit(sides[0], k(0), v(0), (seg_k(0) == seg_q(0)) & tri)
+    second = unit(sides[1], k(1), v(1), (seg_k(1) == seg_q(1)) & tri)
+    third = unit(sides[1], k(0), v(0), seg_k(0) == seg_q(1))
+    fourth = unit(sides[1], sk(0), sv(0), seg_sk(0) == seg_q(1))
+    fifth = unit(queries(extra), sk(extra), sv(extra), seg_sk(extra) == seg_q(extra))
+    at_one = extra == 1
+
+    def when(flag, value):
+        return jnp.where(flag, value, 0.0)
+
+    dq0 = first[0] + when(~at_one, fifth[0])
+    dq1 = second[0] + third[0] + fourth[0] + when(at_one, fifth[0])
+    own = [(first[1] + third[1], first[2] + third[2]), second[1:]]
+    other = [
+        tuple(fourth[i] + when(~at_one, fifth[i]) for i in (1, 2)),
+        tuple(when(at_one, fifth[i]) for i in (1, 2)),
+    ]
+    return (dq0 * 0.125, dq1 * 0.125), own, other
+
+
+def chip_attention_back(extra, queries, keys, values, other, grad, out, logs, seg_q, seg_k, seg_sk):
+    _, rows, width = grad.shape
+    pairs = pl.cdiv(width, LANES)
+
+    def kernel(
+        extra_ref, q_ref, k_ref, v_ref, s_ref, g_ref, of_ref, lse_ref, rq_ref, ck_ref, cs_ref, dq_ref, own_ref, oth_ref
+    ):
+        masks = pair_masks(pl.program_id(0), width)
+        dq, own, oth = pair_backward(
+            extra_ref[0],
+            lambda i: q_ref[i],
+            lambda i: k_ref[i],
+            lambda i: v_ref[i],
+            lambda i: s_ref[0, i],
+            lambda i: s_ref[1, i],
+            lambda i: g_ref[i],
+            lambda i: of_ref[i],
+            lambda i: lse_ref[i],
+            lambda i: rq_ref[i],
+            lambda i: ck_ref[i],
+            lambda i: cs_ref[i],
+            masks,
+        )
+        for slot in range(2):
+            dq_ref[slot] = dq[slot].astype(bf16)
+            for kind in range(2):
+                own_ref[kind, slot] = own[slot][kind]
+                oth_ref[kind, slot] = oth[slot][kind].astype(bf16)
+
+    tile = pl.BlockSpec((2, rows, LANES), lambda p, e: (0, 0, p))
+    both = pl.BlockSpec((2, 2, rows, LANES), lambda p, e: (0, 0, 0, p))
+    col = pl.BlockSpec((2, rows, 1), lambda p, e: (0, 0, 0))
+    return pl.pallas_call(
+        kernel,
+        grid_spec=pltpu.PrefetchScalarGridSpec(
+            num_scalar_prefetch=1,
+            grid=(pairs,),
+            in_specs=[
+                tile,
+                tile,
+                tile,
+                both,
+                tile,
+                tile,
+                tile,
+                pl.BlockSpec((2, 1, rows), lambda p, e: (0, 0, 0)),
+                col,
+                col,
+            ],
+            out_specs=[tile, both, both],
+        ),
+        out_shape=[
+            jax.ShapeDtypeStruct((2, rows, width), bf16),
+            jax.ShapeDtypeStruct((2, 2, rows, width), f32),
+            jax.ShapeDtypeStruct((2, 2, rows, width), bf16),
+        ],
+        compiler_params=params(),
+        cost_estimate=cost(100 * rows * rows * width, 60 * rows * width),
+        name="chip_attn_back",
+    )(extra, queries, keys, values, other, grad, out, logs, seg_q, seg_k, seg_sk)
 
 
 def feed_in(normed, weight, bias, groups):
@@ -649,6 +837,433 @@
     )(*operands)
 
 
+def near_first(k, z, nz):
+    return far_first(nz - 1 - k, z, nz)
+
+
+def forward_gather(grid, x_in, weights, vectors, seg_col, seg_row, seg_other):
+    _, rows, width = x_in.shape
+    tokens = 2 * rows
+    nz = grid.nz
+    parts, groups = grid.dp, grid.ctx
+    wide = pl.cdiv(width, LANES) * LANES
+    pairs = wide // LANES
+    n_qkv, n_out, n_fc = (w.shape[1] for w in weights[:3])
+    slab = weights[0].shape[0]
+    ff = weights[3].shape[1]
+    n_vec = vectors.shape[1]
+    n_bias = n_out
+    n_slots = 4 * nz
+
+    def kernel(
+        x_ref, wq_in, wo_in, wf_in, wp_in, vec_in, sc_ref, sr_ref, so_ref,
+        gq, go, gf, gp, vec_out, inner_out, act_out, sib_out,
+        n1_ref, q_ref, k_ref, v_ref, att_ref, of_ref, lse_ref, hid_ref, n2_ref,
+        sib, vbuf, rowbuf, jrow, wqkv, wbig, wout, stage_u, stage_a, mq, mo, mf, mp,
+        s_z, r_z, s_p, r_p, s_vz, r_vz, s_vy, r_vy, s_kv, r_kv, s_loc, s_w, s_st,
+    ):
+        d, c = lax.axis_index("dp"), lax.axis_index("ctx")
+        z, y = d // grid.ny, d % grid.ny
+        x, core = c // 2, c % 2
+        extra = 1 - core
+        at_sib = (d, c + 1 - 2 * core)
+        at_x = (d, (1 - x) * 2 + core)
+        at_y = (z * grid.ny + 1 - y, c)
+        at_up = ((z + 1) * grid.ny + y, c)
+        at_down = ((z - 1) * grid.ny + y, c)
+        has_up, has_down = z < nz - 1, z > 0
+        gathered = (gq, go, gf, gp)
+        mine = (mq, mo, mf, mp)
+        cuts = [(w.shape[0] // 2 + 7) // 8 * 8 for w in weights]
+
+        def piece(w, zz, yy, xx, cc, half=None):
+            h = weights[w].shape[0]
+            tail = () if half is None else ((pl.ds(0, cuts[w]) if half == 0 else pl.ds(cuts[w], h - cuts[w])),)
+            index = (zz, yy, xx, cc) if w < 3 else (xx, cc, zz, yy)
+            return gathered[w].at[(*index, *tail)]
+
+        def remote(src, dst, send, recv, target):
+            return pltpu.make_async_remote_copy(
+                src_ref=src, dst_ref=dst, send_sem=send, recv_sem=recv, device_id=target, device_id_type=MESH
+            )
+
+        every = slice(None)
+
+        def part_copy(w, kind, j):
+            zz = near_first(j, z, nz)
+            src, target = (
+                (piece(w, zz, y, x, core, 0), at_y),
+                (piece(w, zz, y, x, core, 1), at_x),
+                (piece(w, zz, every, x, core, 0), at_x),
+                (piece(w, zz, y, every, core, 1), at_y),
+                (piece(w, zz, every, every, core), at_sib),
+            )[kind]
+            return remote(src, src, s_p.at[w, kind, j], r_p.at[w, kind, j], target)
+
+        def z_copy(w, zz, way, j):
+            src = piece(w, zz, y, x, core)
+            return remote(src, src, s_z.at[w, way, j], r_z.at[w, zz], (at_up, at_down)[way])
+
+        def vz_copy(zz, way, j):
+            src = vbuf.at[zz, y]
+            return remote(src, src, s_vz.at[way, j], r_vz.at[zz], (at_up, at_down)[way])
+
+        def vy_copy(j):
+            src = vbuf.at[near_first(j, z, nz), y]
+            return remote(src, src, s_vy.at[j], r_vy.at[j], at_y)
+
+        def passes_on(j):
+            zz = near_first(j, z, nz)
+            return zz, (zz < z) & has_up, (zz > z) & has_down
+
+        def z_arrived(w, j):
+            zz = near_first(j, z, nz)
+            z_copy(w, zz, 0, j).wait_recv()
+            if w == 0:
+                vz_copy(zz, 0, j).wait_recv()
+
+        def z_send(w, zz, way, j):
+            z_copy(w, zz, way, j).start()
+            if w == 0:
+                vz_copy(zz, way, j).start()
+
+        def pass_on(i):
+            w, j = divmod(i, nz)
+            if j == 0:
+
+                @pl.when(has_up)
+                def _():
+                    z_send(w, z, 0, 0)
+
+                @pl.when(has_down)
+                def _():
+                    z_send(w, z, 1, 0)
+
+                return
+            zz, up, down = passes_on(j)
+            for way, flag in ((0, up), (1, down)):
+
+                @pl.when(flag)
+                def _():
+                    z_arrived(w, j)
+                    z_send(w, zz, way, j)
+
+        def tick(i):
+            if i < n_slots:
+                w, j = divmod(i, nz)
+                if j > 0:
+                    _, up, down = passes_on(j)
+
+                    @pl.when(jnp.logical_not(up | down))
+                    def _():
+                        z_arrived(w, j)
+
+                part_copy(w, 0, j).start()
+                part_copy(w, 1, j).start()
+                if w == 0:
+                    vy_copy(j).start()
+            if 0 <= i - 1 < n_slots:
+                w, j = divmod(i - 1, nz)
+                part_copy(w, 0, j).wait_recv()
+                part_copy(w, 2, j).start()
+                part_copy(w, 1, j).wait_recv()
+                part_copy(w, 3, j).start()
+            if 0 <= i - 2 < n_slots:
+                w, j = divmod(i - 2, nz)
+                part_copy(w, 2, j).wait_recv()
+                part_copy(w, 3, j).wait_recv()
+                part_copy(w, 4, j).start()
+            if i + 1 < n_slots:
+                pass_on(i + 1)
+
+        def complete(w):
+            for j in range(nz):
+                part_copy(w, 4, j).wait_recv()
+
+        barrier = pltpu.get_barrier_semaphore()
+        for target in (at_sib, at_x, at_y):
+            pl.semaphore_signal(barrier, inc=1, device_id=target, device_id_type=MESH)
+
+        @pl.when(has_up)
+        def _():
+            pl.semaphore_signal(barrier, inc=1, device_id=at_up, device_id_type=MESH)
+
+        @pl.when(has_down)
+        def _():
+            pl.semaphore_signal(barrier, inc=1, device_id=at_down, device_id_type=MESH)
+
+        sources = (wq_in, wo_in, wf_in, wp_in)
+        into = [pltpu.make_async_copy(src, mine[w], s_loc.at[w]) for w, src in enumerate(sources)]
+        into.append(pltpu.make_async_copy(vec_in, vbuf.at[z, y], s_loc.at[4]))
+        for cp in into:
+            cp.start()
+        for ref in (q_ref, k_ref, v_ref):
+            ref[:, :, wide - LANES :] = jnp.zeros((2, rows, LANES), bf16)
+        jrow[...] = jnp.zeros_like(jrow)
+        for cp in into:
+            cp.wait()
+        local = [
+            pltpu.make_async_copy(mine[w], piece(w, z, y, x, core), s_loc.at[w]) for w in range(4)
+        ]
+        for cp in local:
+            cp.start()
+        for cp in local:
+            cp.wait()
+        pl.semaphore_wait(barrier, 3 + has_up.astype(jnp.int32) + has_down.astype(jnp.int32))
+
+        pass_on(0)
+        for i in range(nz + 1):
+            tick(i)
+        for j in range(nz):
+            vy_copy(j).wait_recv()
+
+        for part in range(parts):
+            line = vbuf[part // grid.ny, part % grid.ny]
+            cols = slice(part * n_bias, (part + 1) * n_bias)
+            for v in range(8):
+                term = line[0:1, n_fc + v * n_bias : n_fc + (v + 1) * n_bias]
+                if v < 2:
+                    jrow[0:1, 2 * v * width + cols.start : 2 * v * width + cols.stop] = term
+                else:
+                    rowbuf[v : v + 1, cols] = term
+        for s in range(2):
+            values = x_ref[s].astype(f32)
+            n1_ref[s] = layer_norm(values, rowbuf[4:5, :], rowbuf[5:6, :]).astype(bf16)
+
+        for i in range(nz + 1, nz + 3):
+            tick(i)
+        complete(0)
+
+        def stream(source, buffer, body, hooks):
+            def load(part):
+                return pltpu.make_async_copy(
+                    source.at[part // grid.ny, part % grid.ny], buffer.at[part % 2], s_w.at[part % 2]
+                )
+
+            load(0).start()
+
+            def step(part, _):
+                load(part).wait()
+
+                @pl.when(part + 1 < parts)
+                def _():
+                    load(part + 1).start()
+
+                body(part, part % 2)
+                for when, todo in hooks.items():
+
+                    @pl.when(part == when)
+                    def _():
+                        for i in todo:
+                            tick(i)
+
+                return 0
+
+            lax.fori_loop(0, parts, step, 0)
+
+        def project(part, slot):
+            left = n1_ref[...].reshape(tokens, width)
+            product = dot_nn(left, wqkv[slot].reshape(width, n_qkv))
+            for p in range(parts):
+
+                @pl.when(part == p)
+                def _():
+                    first, last = p * n_qkv, (p + 1) * n_qkv
+                    out = (product + jrow[0:1, first:last]).astype(bf16).reshape(2, rows, n_qkv)
+                    for g, ref in enumerate((q_ref, k_ref, v_ref)):
+                        lo, hi = max(first, g * width), min(last, (g + 1) * width)
+                        if lo < hi:
+                            ref[:, :, lo - g * width : hi - g * width] = out[:, :, lo - first : hi - first]
+
+        stream(gq, wqkv, project, {0: [nz + 3], 4: [nz + 4]})
+        swaps = [
+            remote(ref, sib.at[kind], s_kv.at[kind], r_kv.at[kind], at_sib)
+            for kind, ref in enumerate((k_ref, v_ref))
+        ]
+        for cp in swaps:
+            cp.start()
+        for cp in swaps:
+            cp.wait_recv()
+        tick(nz + 5)
+
+        def attend(p, _):
+            lanes = pl.ds(pl.multiple_of(p * LANES, LANES), LANES)
+            got = pair_forward(
+                extra,
+                lambda i: q_ref[i, :, lanes],
+                lambda i: k_ref[i, :, lanes],
+                lambda i: v_ref[i, :, lanes],
+                lambda i: sib[0, i, :, lanes],
+                lambda i: sib[1, i, :, lanes],
+                lambda i: sc_ref[i],
+                lambda i: sr_ref[i],
+                lambda i: so_ref[i],
+                pair_masks(p, width),
+            )
+            for slot, (out, logs) in enumerate(got):
+                att_ref[slot, :, lanes] = out.astype(bf16)
+                of_ref[slot, :, lanes] = out
+                lse_ref[slot, :, lanes] = logs
+
+            @pl.when(p == pairs // 2)
+            def _():
+                tick(nz + 6)
+
+            return 0
+
+        lax.fori_loop(0, pairs, attend, 0)
+        keep = pltpu.make_async_copy(sib, sib_out, s_loc.at[0])
+        keep.start()
+        complete(1)
+
+        def branch(part, slot):
+            product = dot_nn(
+                att_ref[:, :, :width].reshape(tokens, width), wout[slot].reshape(width, n_out)
+            ).reshape(2, rows, n_out)
+            for p in range(parts):
+
+                @pl.when(part == p)
+                def _():
+                    hid_ref[:, :, p * n_out : (p + 1) * n_out] = product
+
+        stream(go, wout, branch, {0: [nz + 7]})
+        for s in range(2):
+            hidden = x_ref[s].astype(f32) + hid_ref[s] + rowbuf[2:3, :]
+            hid_ref[s] = hidden
+            n2_ref[s] = layer_norm(hidden, rowbuf[6:7, :], rowbuf[7:8, :]).astype(bf16)
+        tick(nz + 8)
+        tick(nz + 9)
+        complete(2)
+
+        ratio = parts // groups
+
+        def saves(group):
+            slot = group % 2
+            return (
+                pltpu.make_async_copy(stage_u.at[slot], inner_out.at[group], s_st.at[0, slot]),
+                pltpu.make_async_copy(stage_a.at[slot], act_out.at[group], s_st.at[1, slot]),
+            )
+
+        def feed(part, slot):
+            group, place = part // ratio, part % ratio
+
+            @pl.when((place == 0) & (group >= 2))
+            def _():
+                for cp in saves(group - 2):
+                    cp.wait()
+
+            left = n2_ref[...].reshape(tokens, width)
+            u = dot_nn(left, wbig[slot].reshape(width, n_fc))
+            u = u + vbuf[part // grid.ny, part % grid.ny][0:1, :n_fc]
+            act = (0.5 * u * (1.0 + jnp.tanh(GELU_C * (u + GELU_A * u * u * u)))).astype(bf16)
+            for r in range(ratio):
+
+                @pl.when(place == r)
+                def _():
+                    stage_u[group % 2, :, r * n_fc : (r + 1) * n_fc] = u
+                    stage_a[group % 2, :, r * n_fc : (r + 1) * n_fc] = act
+
+            @pl.when(place == ratio - 1)
+            def _():
+                for cp in saves(group):
+                    cp.start()
+
+        stream(gf, wbig, feed, {1: [nz + 10], 5: [nz + 11]})
+        tick(nz + 12)
+        tick(nz + 13)
+        save_vec = pltpu.make_async_copy(vbuf, vec_out, s_loc.at[1])
+        save_vec.start()
+        for group in range(groups - 2, groups):
+            for cp in saves(group):
+                cp.wait()
+        keep.wait()
+        save_vec.wait()
+        complete(3)
+        for cp in swaps:
+            cp.wait_send()
+
+        def finish(j, _):
+            zz, up, down = passes_on(j)
+            up, down = up | ((j == 0) & has_up), down | ((j == 0) & has_down)
+            vy_copy(j).wait_send()
+            for w in range(4):
+                for kind in range(5):
+                    part_copy(w, kind, j).wait_send()
+                for way, flag in ((0, up), (1, down)):
+
+                    @pl.when(flag)
+                    def _():
+                        z_copy(w, zz, way, j).wait_send()
+                        if w == 0:
+                            vz_copy(zz, way, j).wait_send()
+
+            return 0
+
+        lax.fori_loop(0, nz, finish, 0)
+
+    any_, vm = pl.BlockSpec(memory_space=pl.ANY), pl.BlockSpec(memory_space=pltpu.VMEM)
+    dma = pltpu.SemaphoreType.DMA
+    columns = [
+        jax.ShapeDtypeStruct((nz, grid.ny, grid.nx, 2, *w.shape), bf16) for w in weights[:3]
+    ]
+    wide_low = jax.ShapeDtypeStruct((2, rows, wide), bf16)
+    wide_full = jax.ShapeDtypeStruct((2, rows, wide), f32)
+    low = jax.ShapeDtypeStruct((2, rows, width), bf16)
+    out_shape = [
+        *columns,
+        jax.ShapeDtypeStruct((grid.nx, 2, nz, grid.ny, *weights[3].shape), bf16),
+        jax.ShapeDtypeStruct((nz, grid.ny, 8, n_vec), f32),
+        jax.ShapeDtypeStruct((groups, tokens, ff), f32),
+        jax.ShapeDtypeStruct((groups, tokens, ff), bf16),
+        jax.ShapeDtypeStruct((2, 2, rows, wide), bf16),
+        low,
+        wide_low,
+        wide_low,
+        wide_low,
+        wide_low,
+        wide_full,
+        wide_full,
+        jax.ShapeDtypeStruct((2, rows, width), f32),
+        low,
+    ]
+    return pl.pallas_call(
+        kernel,
+        out_shape=out_shape,
+        in_specs=[vm] + [any_] * 4 + [any_] + [vm] * 3,
+        out_specs=[any_] * 8 + [vm] * 9,
+        scratch_shapes=[
+            pltpu.VMEM((2, 2, rows, wide), bf16),
+            pltpu.VMEM((nz, grid.ny, 8, n_vec), f32),
+            pltpu.VMEM((8, width), f32),
+            pltpu.VMEM((8, 3 * width), f32),
+            pltpu.VMEM((2, grid.nx, 2, slab, n_qkv), bf16),
+            pltpu.VMEM((2, grid.nx, 2, slab, n_fc), bf16),
+            pltpu.VMEM((2, grid.nx, 2, slab, n_out), bf16),
+            pltpu.VMEM((2, tokens, ff), f32),
+            pltpu.VMEM((2, tokens, ff), bf16),
+            *(pltpu.VMEM(w.shape, bf16) for w in weights),
+            dma((4, 2, nz)),
+            dma((4, nz)),
+            dma((4, 5, nz)),
+            dma((4, 5, nz)),
+            dma((2, nz)),
+            dma((nz,)),
+            dma((nz,)),
+            dma((nz,)),
+            dma((2,)),
+            dma((2,)),
+            dma((5,)),
+            dma((2,)),
+            dma((2, 2)),
+        ],
+        compiler_params=pltpu.CompilerParams(
+            collective_id=4, has_side_effects=True, vmem_limit_bytes=VMEM_LIMIT
+        ),
+        cost_estimate=cost(30e9, 150e6),
+        name="forward",
+    )(x_in, *weights, vectors, seg_col, seg_row, seg_other)
+
+
 def pick(array, index, axis):
     return lax.dynamic_index_in_dim(array, index, axis, keepdims=False)
 
@@ -673,6 +1288,21 @@
 
     def swap_core(self, v):
         return lax.ppermute(v, "ctx", [(i, i ^ 1) for i in range(self.ctx)])
+
+    ACROSS = ((0, 2), (1, 3), (2, 1), (3, 0))
+    WITHIN = ((2, 3), (3, 2))
+
+    def by_sequence(self, v):
+        first = self.x == 0
+        across = lax.ppermute(pick(v, 1 - self.x, 0), "ctx", self.ACROSS)
+        within = lax.ppermute(v[1], "ctx", self.WITHIN)
+        return jnp.stack([jnp.where(first, v[0], across), jnp.where(first, across, within)])
+
+    def by_position(self, v):
+        first = self.x == 0
+        across = lax.ppermute(pick(v, 1 - self.x, 0), "ctx", [(b, a) for a, b in self.ACROSS])
+        within = lax.ppermute(v[1], "ctx", self.WITHIN)
+        return jnp.stack([jnp.where(first, v[0], across), jnp.where(first, across, within)])
 
 
 def on_device(grid, *args):
@@ -700,55 +1330,77 @@
     both = ("dp", "ctx")
     grid.place()
 
-    vectors = (q_bias, v_bias, out_bias, proj_bias, ln1_gain, ln1_bias, ln2_gain, ln2_bias, fc_bias)
-    sizes = [v.shape[0] for v in vectors]
-    packed = lax.all_gather(jnp.concatenate(vectors), "dp", axis=0)
-    spread, at = [], 0
-    for size in sizes:
-        spread.append(packed[:, at : at + size].astype(f32))
-        at += size
-    q_all, v_all, ob_all, pb_all, g1, b1, g2, b2 = [v.reshape(-1) for v in spread[:8]]
-    fcb = spread[8][:, None, :]
-
-    def gather(block, axes):
-        return lax.all_gather(block, axes, axis=0)
-
     n_qkv, n_out, n_fc = qkv_weight.shape[1], out_weight.shape[1], fc_weight.shape[1]
     slab, hidden_slab = qkv_weight.shape[0], proj_weight.shape[0]
-    w_qkv = gather(qkv_weight, both).reshape(parts, width, n_qkv)
-    w_out = gather(out_weight, both).reshape(parts, width, n_out)
-    w_fc = gather(fc_weight, both).reshape(parts, width, n_fc)
-    w_proj = gather(proj_weight.T, ("ctx", "dp")).reshape(groups, width, hidden_slab)
-    out_full = w_out.transpose(1, 0, 2).reshape(width, width)
-
-    values = layer_input.reshape(tokens, width).astype(f32)
-    normed1 = layer_norm(values, g1, b1).astype(bf16)
-    joined = jnp.concatenate([q_all, jnp.zeros((width,), f32), v_all]).reshape(parts, 1, n_qkv)
-    queries, key_rows, value_rows = qkv_project(normed1, w_qkv, joined)
-    queries = queries.reshape(seqs, rows, width)
-    own = jnp.stack([key_rows, value_rows]).reshape(2, seqs, rows, width)
-    if grid.paired:
-        other = lax.ppermute(own, "ctx", [(0, 2), (1, 3)])
-        column = jnp.where(grid.x == 0, jnp.stack([own, own]), jnp.stack([other, own]))
-        sibling = grid.swap_core(column)
-        even = jnp.where(grid.core == 0, column, sibling)
-        odd = jnp.where(grid.core == 0, sibling, column)
-        pairs_full = jnp.stack([even, odd], axis=1).reshape(groups, 2, seqs, rows, width)
+    paired = grid.paired and seqs == 2
+    seg_blocks = segment_ids.reshape(seqs, groups, rows)
+    vectors = (fc_bias, q_bias, v_bias, out_bias, proj_bias, ln1_gain, ln1_bias, ln2_gain, ln2_bias)
+    sizes = [v.shape[0] for v in vectors]
+
+    def unpack(packed):
+        spread, at = [], 0
+        for size in sizes:
+            spread.append(packed[:, at : at + size].astype(f32))
+            at += size
+        return [v.reshape(-1) for v in spread]
+
+    if paired:
+        layer_input, grad_out = grid.by_sequence(layer_input), grid.by_sequence(grad_out)
+        extra = 1 - grid.core
+        chip_seg = pick(seg_blocks, grid.x, 0)
+        seg_own = jnp.stack([pick(chip_seg, grid.core, 0), pick(chip_seg, 3 - grid.core, 0)])
+        seg_other = jnp.stack([pick(chip_seg, extra, 0), pick(chip_seg, 3 - extra, 0)])
+        packed = jnp.concatenate(vectors).astype(f32)[None]
+        (
+            w_qkv, w_out, w_fc, w_proj, packed, inner, activated, other,
+            normed1, queries, keys, vals, attended, attended_f32, log_total, hidden, normed2,
+        ) = forward_gather(
+            grid,
+            layer_input,
+            (qkv_weight, out_weight, fc_weight, proj_weight.T),
+            jnp.broadcast_to(packed, (8, packed.shape[1])),
+            seg_own[:, :, None],
+            seg_own[:, None, :],
+            seg_other[:, None, :],
+        )
+        _, _, _, _, pb_all, g1, b1, g2, b2 = unpack(packed[:, :, 0].reshape(parts, -1))
+        w_qkv = w_qkv.reshape(parts, width, n_qkv)
+        w_fc = w_fc.reshape(parts, width, n_fc)
+        w_proj = w_proj.reshape(groups, width, hidden_slab)
+        out_full = w_out.reshape(parts, width, n_out).transpose(1, 0, 2).reshape(width, width)
+        normed1, normed2, hidden = (v.reshape(tokens, width) for v in (normed1, normed2, hidden))
+        attended = attended[:, :, :width].reshape(tokens, width)
+        values = layer_input.reshape(tokens, width).astype(f32)
     else:
+        packed = lax.all_gather(jnp.concatenate(vectors), "dp", axis=0)
+        fcb, q_all, v_all, ob_all, pb_all, g1, b1, g2, b2 = unpack(packed)
+
+        def gather(block, axes):
+            return lax.all_gather(block, axes, axis=0)
+
+        w_qkv = gather(qkv_weight, both).reshape(parts, width, n_qkv)
+        w_out = gather(out_weight, both).reshape(parts, width, n_out)
+        w_fc = gather(fc_weight, both).reshape(parts, width, n_fc)
+        w_proj = gather(proj_weight.T, ("ctx", "dp")).reshape(groups, width, hidden_slab)
+        out_full = w_out.transpose(1, 0, 2).reshape(width, width)
+        values = layer_input.reshape(tokens, width).astype(f32)
+        normed1 = layer_norm(values, g1, b1).astype(bf16)
+        joined = jnp.concatenate([q_all, jnp.zeros((width,), f32), v_all])
+        queries, key_rows, value_rows = qkv_project(normed1, w_qkv, joined.reshape(parts, 1, n_qkv))
+        queries = queries.reshape(seqs, rows, width)
+        own = jnp.stack([key_rows, value_rows]).reshape(2, seqs, rows, width)
         pairs_full = lax.all_gather(own, "ctx", axis=0)
-
-    seg_blocks = segment_ids.reshape(seqs, groups, rows)
-    seg_mine = pick(seg_blocks, grid.c, 1)
-    needed = seg_blocks[:, :, -1] >= seg_mine[:, :1]
-    start = jnp.minimum(jnp.argmax(needed, axis=1).astype(jnp.int32), grid.c)
-    bounds = jnp.concatenate([grid.c[None].astype(jnp.int32), start])
-    attended, attended_f32, log_total = attention_forward(
-        bounds, queries, pairs_full, seg_mine[:, :, None], seg_blocks[:, :, None, :]
-    )
-    attended = attended.reshape(tokens, width)
-    hidden = values + jnp.dot(attended, out_full, preferred_element_type=f32) + ob_all
-    normed2 = layer_norm(hidden, g2, b2).astype(bf16)
-    inner, activated = feed_in(normed2, w_fc, fcb, groups)
+        seg_mine = pick(seg_blocks, grid.c, 1)
+        needed = seg_blocks[:, :, -1] >= seg_mine[:, :1]
+        start = jnp.minimum(jnp.argmax(needed, axis=1).astype(jnp.int32), grid.c)
+        bounds = jnp.concatenate([grid.c[None].astype(jnp.int32), start])
+        attended, attended_f32, log_total = attention_forward(
+            bounds, queries, pairs_full, seg_mine[:, :, None], seg_blocks[:, :, None, :]
+        )
+        attended = attended.reshape(tokens, width)
+        hidden = values + jnp.dot(attended, out_full, preferred_element_type=f32) + ob_all
+        normed2 = layer_norm(hidden, g2, b2).astype(bf16)
+        inner, activated = feed_in(normed2, w_fc, fcb.reshape(parts, 1, n_fc), groups)
     output = feed_out(activated, w_proj, hidden, pb_all[None])
 
     mlp_grad = grad_out.reshape(tokens, width)
@@ -779,7 +1431,7 @@
                 store(y_to, x_to, term[y_to * cols : (y_to + 1) * cols])
 
     def reduced(pairs, collective_id, name):
-        if not grid.paired:
+        if not paired:
             everything = jnp.arange(parts, dtype=jnp.int32)
             results = []
             for left, right in pairs:
@@ -801,7 +1453,7 @@
     def reduced_proj(left, right):
         f = right.shape[2]
         cols = width // parts
-        if not grid.paired:
+        if not paired:
             whole = weight_grad(left.T, right, jnp.arange(groups, dtype=jnp.int32))
             whole = whole.reshape(groups * parts, cols, f)
             return lax.psum_scatter(whole, ("ctx", "dp"), scatter_dimension=0).astype(f32)
@@ -821,24 +1473,33 @@
     ).astype(bf16)
     branch_parts = branch_grad.reshape(tokens, parts, n_out).transpose(1, 0, 2)
 
-    query_grad, pairs_grad = attention_backward(
-        bounds,
-        queries,
-        pairs_full,
-        seg_blocks[:, :, :, None],
-        seg_mine[:, None, :],
-        attended_grad.reshape(seqs, rows, width),
-        attended_f32,
-        log_total,
-    )
-    if grid.paired:
-        by_chip = pairs_grad.reshape(2, 2, 2, seqs, rows, width)
-        plane = add_low(
-            pick(by_chip, grid.core, 1), grid.swap_core(pick(by_chip, 1 - grid.core, 1))
+    attended_grad = attended_grad.reshape(seqs, rows, width)
+    if paired:
+        query_grad, own_grad, other_grad = chip_attention_back(
+            extra.astype(jnp.int32)[None],
+            queries,
+            keys,
+            vals,
+            other,
+            attended_grad,
+            attended_f32,
+            log_total,
+            seg_own[:, None, :],
+            seg_own[:, :, None],
+            seg_other[:, :, None],
         )
-        came = lax.ppermute(plane[0], "ctx", [(2, 0), (3, 1)])
-        pair_grad = add_low(pick(plane, grid.x, 0), came)
+        pair_grad = add_low(own_grad, grid.swap_core(other_grad))
     else:
+        query_grad, pairs_grad = attention_backward(
+            bounds,
+            queries,
+            pairs_full,
+            seg_blocks[:, :, :, None],
+            seg_mine[:, None, :],
+            attended_grad,
+            attended_f32,
+            log_total,
+        )
         pair_grad = lax.psum_scatter(pairs_grad, "ctx", scatter_dimension=0)
     pair_grad = pair_grad.reshape(2, tokens, width)
     projected_grad = jnp.concatenate(
@@ -855,31 +1516,43 @@
     values_ln, g1_grad, b1_grad = norm1_pull(normed1_grad)
     input_grad = hidden_grad + values_ln
 
-    sums = [q_bias_grad, v_bias_grad, out_bias_grad, proj_bias_grad, g1_grad, b1_grad, g2_grad, b2_grad]
-    stacked = jnp.concatenate(
-        [v.reshape(parts, -1) for v in sums] + [fc_bias_grad.reshape(parts, -1)], axis=1
-    )
+    output, input_grad = (v.reshape(seqs, rows, width) for v in (output, input_grad))
+    if paired:
+        output, input_grad = grid.by_position(output), grid.by_position(input_grad)
+
+    sums = [
+        fc_bias_grad,
+        q_bias_grad,
+        v_bias_grad,
+        out_bias_grad,
+        proj_bias_grad,
+        g1_grad,
+        b1_grad,
+        g2_grad,
+        b2_grad,
+    ]
+    stacked = jnp.concatenate([v.reshape(parts, -1) for v in sums], axis=1)
     total = pick(lax.psum(stacked, both), grid.d, 0)
     vec, at = [], 0
     for size in sizes:
         vec.append(total[at : at + size])
         at += size
     return (
-        output.reshape(seqs, rows, width),
-        input_grad.reshape(seqs, rows, width),
+        output,
+        input_grad,
         qkv_weight_grad,
+        vec[1],
+        vec[2],
+        out_weight_grad,
+        vec[3],
+        fc_weight_grad,
         vec[0],
-        vec[1],
-        out_weight_grad,
-        vec[2],
-        fc_weight_grad,
-        vec[8],
         proj_weight_grad,
-        vec[3],
         vec[4],
         vec[5],
         vec[6],
         vec[7],
+        vec[8],
     )
 
 

time: 1210 us -> 1070 us (0.88)
  Pallas kernels: 602 us -> 829 us
  waiting for transfers between devices: 253 us -> 29.8 us
  local copies, waits for them, and re-layouts: 182 us -> 128 us
  blocking collectives: 39.9 us -> 0 us
  other arithmetic: 73.3 us -> 44.4 us
    pallas_call x4 -> x2, Pallas kernels: 110 us -> 349 us  [the longest x1 310 us: forward_gather(): pl.pallas_call(kernel, out_shape=out_shape, in_specs=[vm] + [any_] * 4 +...]
    all_gather x4 -> x0, waiting for transfers between devices: 171 us -> none  [gather(): return lax.all_gather(block, axes, axis=0)]
    ppermute x2 -> x8, waiting for transfers between devices: 79.1 us -> 29.8 us  [the longest x2 29.8 us: by_sequence(): across = lax.ppermute(pick(v, 1 - self.x, 0), 'ctx', self.ACROSS)]
    unnamed x1 -> x0, blocking collectives: 39.9 us -> none
    another operation x7 -> x2, local copies, waits for them, and re-layouts: 35.3 us -> 3.14 us  [the longest x1 2.45 us: by_sequence(): jnp.stack([jnp.where(first, v[0], across), jnp.where(first, across, withi...]
    reshape x13 -> x14, local copies, waits for them, and re-layouts: 7.01 us -> 27.6 us  [the longest x3 10.1 us: on_device(): v.reshape(tokens, width)]
    dynamic_slice x3, local copies, waits for them, and re-layouts: 19.5 us -> 3.61 us  [pick(): return lax.dynamic_index_in_dim(array, index, axis, keepdims=False)]
  transfers between devices with their start and end apart: 9 -> 10, of which waited for: 4 -> 2; matrix products, arithmetic and copies ran while one was open for 13% -> 10% of each run, Pallas kernels for 43% -> 41%
where the time goes in v2:
time: 1070 us; the launch traced here: 1060 us
  Pallas kernels  829 us (77%)
  local copies, waits for them, and re-layouts  128 us (12%)
  other arithmetic  44.4 us (4%)
  waiting for transfers between devices  29.8 us (3%)
  between operations  15.2 us (1%)
  starting transfers between devices  13.7 us (1%)
    pallas_call x3, Pallas kernels, summed_grads(): pl.pallas_call(kernel, out_shape=jax.ShapeDtypeStruct((rows, n), f32), in...  397 us
    pallas_call x1, Pallas kernels, forward_gather(): pl.pallas_call(kernel, out_shape=out_shape, in_specs=[vm] + [any_] * 4 +...  310 us
    pallas_call x1, Pallas kernels, chip_attention_back(): pl.pallas_call(kernel, grid_spec=pltpu.PrefetchScalarGridSpec(num_scalar_...  39.3 us
    pallas_call x2, Pallas kernels, back_project(): pl.pallas_call(kernel, grid=(parts,), in_specs=[pl.BlockSpec((1, tokens,...  37.7 us
    ppermute x2, waiting for transfers between devices, by_sequence(): across = lax.ppermute(pick(v, 1 - self.x, 0), 'ctx', self.ACROSS)  29.8 us
    pallas_call x1, Pallas kernels, feed_back(): pl.pallas_call(kernel, grid=(groups,), in_specs=[pl.BlockSpec((tokens, wi...  25.9 us
  transfers between devices with their start and end apart: 10, of which 2 were waited for; matrix products, arithmetic and copies ran while one was open for 10% of the time, Pallas kernels for 41%

profile of v2, /device:TPU:0, one launch (start us, length us, event | category | flops | bytes accessed | tf_op | source)
XLA Modules:
  0.0 1062.8 jit_solution(10146016984641905821)
XLA Ops:
  7.4 2.8 slice_bitcast_fusion.1
  11.7 3.3 collective-permute-start
  21.9 12.2 %collective-permute-done = bf16[256,1600]{0,1:T(8,128)(2,1)} collective-permute-done((bf16[256,1600]{0,1:T(8,128)(2,1)}, bf16[256,1600]{0,1:T(8,128)(2,1)}, u32[]{:S(2)}, u32[]{:S(2)}) %collective-permute-start) | collective-permute-done | bytes 819232 | tf_op jit(solution)/shard_map/ppermute | solution.py:1297
  34.1 17.6 %collective-permute-done.4 = bf16[256,1600]{0,1:T(8,128)(2,1)} collective-permute-done((bf16[256,1600]{0,1:T(8,128)(2,1)}, bf16[256,1600]{0,1:T(8,128)(2,1)}, u32[]{:S(2)}, u32[]{:S(2)}) %collective-permute-start.4) | collective-permute-done | bytes 819232 | tf_op jit(solution)/shard_map/ppermute | solution.py:1297
  53.7 2.5 fusion.14
  56.5 2.4 copy.88.g_ref
  58.9 2.5 copy.80.x_ref
  62.0 309.5 %forward.1 = (bf16[4,2,2,2,400,600]{5,4,3,2,1,0:T(8,128)(2,1)}, bf16[4,2,2,2,400,200]{5,4,3,2,1,0:T(8,128)(2,1)}, bf16[4,2,2,2,400,800]{5,4,3,2,1,0:T(8,128)(2,1...) custom-call(bf16[2,256,1600]{2,1,0:T(8,128)(2,1)} %copy.80.x_ref, ...), custom_call_target="tpu_custom_call" | custom-call | flops 30000001024 | bytes 150000000 | tf_op jit(solution)/shard_map/forward/pallas_call | solution.py:1229
  371.5 25.9 %act_bwd.1 = (bf16[8,512,800]{2,1,0:T(8,128)(2,1)}, f32[8,1,800]{2,1,0:T(1,128)}) custom-call(bf16[512,1600]{1,0:T(8,128)(2,1)} %copy.88.g_ref, bf16[4,1600,1600]{2,1,0:T(8,128)(2,1)} %bitcast.154, f32[4,512,1600]{2,1,0:T(8,128)} %get-tuple-element.41.u_ref), custom_call_target="tpu_custom_call" | custom-call | flops 10485760000 | bytes 61440000 | tf_op jit(solution)/shard_map/act_bwd/pallas_call | solution.py:537
  397.4 20.7 %back.2 = f32[512,1600]{1,0:T(8,128)} custom-call(bf16[8,512,800]{2,1,0:T(8,128)(2,1)} %get-tuple-element.42.g_ref.refs_1_, bf16[8,1600,800]{2,1,0:T(8,128)(2,1)} %bitcast.153), custom_call_target="tpu_custom_call" | custom-call | flops 10485760000 | bytes 20480000 | tf_op jit(solution)/shard_map/back/pallas_call | solution.py:572
  418.1 4.7 copy.89
  422.8 2.3 reduce_sum.167
  429.4 2.9 copy.110
  432.4 4.1 multiply_reduce_fusion.1
  438.1 9.4 copy.90
  447.5 2.2 convert_reduce_fusion.3
  450.9 3.2 convolution_convert_fusion
  454.1 2.4 copy.91
  456.5 39.3 %chip_attn_back.1 = (bf16[2,256,1600]{2,1,0:T(8,128)(2,1)}, f32[2,2,256,1600]{3,2,1,0:T(8,128)}, bf16[2,2,256,1600]{3,2,1,0:T(8,128)(2,1)}) custom-call(s32[1]{0:T(128)} %bitcast.23.extra_ref, bf16[2,256,1664]{2,1,0:T(8,128)(2,1)} %get-tuple-element.44.q_ref, bf16[2,256,1664]{2,1,0:T(8,128)(2,1)} %get-tuple-element.45.k_ref, ...), custom_call_target="tpu_custom_call" | custom-call | flops 10485760000 | bytes 24576000 | tf_op jit(solution)/shard_map/chip_attn_back/pallas_call | solution.py:418
  495.9 5.7 copy.94
  502.5 4.7 copy.101
  507.1 3.5 copy.102
  511.5 122.3 %rs_proj.1 = f32[200,1600]{1,0:T(8,128)} custom-call(bf16[1600,512]{1,0:T(8,128)(2,1)} %bitcast.112, bf16[4,512,1600]{2,1,0:T(8,128)(2,1)} %get-tuple-element.37.a_ref.refs_1_), custom_call_target="tpu_custom_call" | custom-call | flops 10485760000 | bytes 100000000 | tf_op jit(solution)/shard_map/rs_proj/pallas_call | solution.py:821
  633.9 19.7 %proj.1 = bf16[512,1600]{1,0:T(8,128)(2,1)} custom-call(bf16[4,512,1600]{2,1,0:T(8,128)(2,1)} %get-tuple-element.37.a_ref.refs_1_, bf16[4,1600,1600]{2,1,0:T(8,128)(2,1)} %bitcast.155, f32[512,1600]{1,0:T(8,128)} %bitcast.108, f32[1,1600]{1,0:T(1,128)} %broadcast_in_dim_reshape.2.b_ref), custom_call_target="tpu_custom_call" | custom-call | flops 10485760000 | bytes 20480000 | tf_op jit(solution)/shard_map/proj/pallas_call | solution.py:501
  653.5 2.1 constant_dynamic-slice_fusion.1
  655.7 2.1 copy.117
  659.4 3.6 copy.111
  662.9 3.6 copy.112
  666.5 3.6 copy.113
  670.1 2.7 fusion.18
  672.9 2.2 copy.118
  676.6 3.8 copy.96
  680.4 5.5 copy.95
  685.9 4.6 add_convert_fusion
  693.3 3.6 copy.97
  696.8 3.6 copy.98
  700.4 4.9 pad_maximum_fusion
  705.3 7.7 copy.99
  713.1 17.0 %back.3 = f32[512,1600]{1,0:T(8,128)} custom-call(bf16[8,512,600]{2,1,0:T(8,128)(2,1)} %bitcast.123, bf16[8,1600,600]{2,1,0:T(8,128)(2,1)} %bitcast.156), custom_call_target="tpu_custom_call" | custom-call | flops 7864320000 | bytes 15360000 | tf_op jit(solution)/shard_map/back/pallas_call | solution.py:572
  730.1 4.7 copy.100
  734.8 2.6 multiply_reduce_fusion.3
  740.1 2.8 add_add_fusion.2
  742.9 3.9 reshape.318
  750.8 146.7 %rs_fc.1 = f32[400,800]{1,0:T(8,128)} custom-call(bf16[1600,512]{1,0:T(8,128)(2,1)} %bitcast.132, bf16[8,512,800]{2,1,0:T(8,128)(2,1)} %get-tuple-element.42.g_ref.refs_1_), custom_call_target="tpu_custom_call" | custom-call | flops 10485760000 | bytes 100000000 | tf_op jit(solution)/shard_map/rs_fc/pallas_call | solution.py:821
  898.3 2.8 copy.105
  911.1 2.5 reduce_sum.162
  915.0 127.8 %rs_qkv.1 = f32[400,856]{1,0:T(8,128)} custom-call(bf16[1600,512]{1,0:T(8,128)(2,1)} %bitcast.130, bf16[8,512,256]{2,1,0:T(8,128)(2,1)} %pad.4.refs_1_, bf16[1600,512]{1,0:T(8,128)(2,1)} %bitcast.131, bf16[8,512,600]{2,1,0:T(8,128)(2,1)} %bitcast.124), custom_call_target="tpu_custom_call" | custom-call | flops 11219763200 | bytes 100000000 | tf_op jit(solution)/shard_map/rs_qkv/pallas_call | solution.py:821
  1044.5 2.4 slice.127
  (160 shorter events, 55.3 us)
Async XLA Ops:
  7.2 7.9 copy-start.22
  7.2 1039.7 %all-reduce.3.cloned.1.call-start = ((), (), s32[]{:S(2)}) async-start(), calls=%async_computation | async-start | bytes 155648 | tf_op jit(solution)/shard_map/psum | solution.py:1535
  7.3 11.6 %copy-start.28 = (s32[2,1024]{1,0:T(2,128)S(1)}, s32[2,1024]{1,0:T(2,128)}, u32[]{:S(2)}) copy-start(s32[2,1024]{1,0:T(2,128)} %param.18) | copy-start | bytes 24580
  7.3 14.5 %copy-start.29 = (bf16[800]{0:T(1024)(128)(2,1)S(1)}, bf16[800]{0:T(1024)(128)(2,1)}, u32[]{:S(2)}) copy-start(bf16[800]{0:T(1024)(128)(2,1)} %param.25) | copy-start | bytes 4804
  7.3 14.5 %copy-start.30 = (bf16[200]{0:T(256)(128)(2,1)S(1)}, bf16[200]{0:T(256)(128)(2,1)}, u32[]{:S(2)}) copy-start(bf16[200]{0:T(256)(128)(2,1)} %param.20) | copy-start | bytes 1204
  7.3 14.5 %copy-start.31 = (bf16[200]{0:T(256)(128)(2,1)S(1)}, bf16[200]{0:T(256)(128)(2,1)}, u32[]{:S(2)}) copy-start(bf16[200]{0:T(256)(128)(2,1)} %param.21) | copy-start | bytes 1204
  7.3 14.4 %copy-start.32 = (bf16[200]{0:T(256)(128)(2,1)S(1)}, bf16[200]{0:T(256)(128)(2,1)}, u32[]{:S(2)}) copy-start(bf16[200]{0:T(256)(128)(2,1)} %param.23) | copy-start | bytes 1204
  7.3 14.4 %copy-start.33 = (bf16[200]{0:T(256)(128)(2,1)S(1)}, bf16[200]{0:T(256)(128)(2,1)}, u32[]{:S(2)}) copy-start(bf16[200]{0:T(256)(128)(2,1)} %param.27) | copy-start | bytes 1204
  7.3 14.4 %copy-start.34 = (bf16[200]{0:T(256)(128)(2,1)S(1)}, bf16[200]{0:T(256)(128)(2,1)}, u32[]{:S(2)}) copy-start(bf16[200]{0:T(256)(128)(2,1)} %param.28) | copy-start | bytes 1204
  7.3 14.4 %copy-start.35 = (bf16[200]{0:T(256)(128)(2,1)S(1)}, bf16[200]{0:T(256)(128)(2,1)}, u32[]{:S(2)}) copy-start(bf16[200]{0:T(256)(128)(2,1)} %param.29) | copy-start | bytes 1204
  7.3 14.4 %copy-start.36 = (bf16[200]{0:T(256)(128)(2,1)S(1)}, bf16[200]{0:T(256)(128)(2,1)}, u32[]{:S(2)}) copy-start(bf16[200]{0:T(256)(128)(2,1)} %param.30) | copy-start | bytes 1204
  7.3 14.4 %copy-start.37 = (bf16[200]{0:T(256)(128)(2,1)S(1)}, bf16[200]{0:T(256)(128)(2,1)}, u32[]{:S(2)}) copy-start(bf16[200]{0:T(256)(128)(2,1)} %param.31) | copy-start | bytes 1204
  7.4 44.3 %copy-start.23 = (bf16[2,256,1600]{1,2,0:T(8,128)(2,1)S(1)}, bf16[2,256,1600]{1,2,0:T(8,128)(2,1)}, u32[]{:S(2)}) copy-start(bf16[2,256,1600]{1,2,0:T(8,128)(2,1)} %param.16) | copy-start | bytes 4915204
  10.2 11.7 %collective-permute-start.1 = (bf16[256,1600]{0,1:T(8,128)(2,1)}, bf16[256,1600]{0,1:T(8,128)(2,1)}, u32[]{:S(2)}, u32[]{:S(2)}) collective-permute-start(bf16[256,1600]{0,1:T(8,128)(2,1)} %get-tuple-element.77), channel_id=1, source_target_pairs={{2,3},{3,2},{6,7},{7,6},{10,11},{11,10},{14,15},{15,14},{18,19},{1... | collective-permute-start | bytes 2457608 | tf_op jit(solution)/shard_map/ppermute | solution.py:1298
  11.7 22.4 %collective-permute-start = (bf16[256,1600]{0,1:T(8,128)(2,1)}, bf16[256,1600]{0,1:T(8,128)(2,1)}, u32[]{:S(2)}, u32[]{:S(2)}) collective-permute-start(bf16[256,1600]{0,1:T(8,128)(2,1)} %get-tuple-element.78), channel_id=1, source_target_pairs={{0,2},{1,3},{2,1},{3,0},{4,6},{5,7},{6,5},{7,4},{8,10},{9,11},{10,... | collective-permute-start | bytes 2457608 | tf_op jit(solution)/shard_map/ppermute | solution.py:1297
  16.4 17.8 %collective-permute-start.5 = (bf16[256,1600]{0,1:T(8,128)(2,1)}, bf16[256,1600]{0,1:T(8,128)(2,1)}, u32[]{:S(2)}, u32[]{:S(2)}) collective-permute-start(bf16[256,1600]{0,1:T(8,128)(2,1)} %get-tuple-element.75), channel_id=1, source_target_pairs={{2,3},{3,2},{6,7},{7,6},{10,11},{11,10},{14,15},{15,14},{18,19},{1... | collective-permute-start | bytes 2457608 | tf_op jit(solution)/shard_map/ppermute | solution.py:1298
  17.9 33.7 %collective-permute-start.4 = (bf16[256,1600]{0,1:T(8,128)(2,1)}, bf16[256,1600]{0,1:T(8,128)(2,1)}, u32[]{:S(2)}, u32[]{:S(2)}) collective-permute-start(bf16[256,1600]{0,1:T(8,128)(2,1)} %get-tuple-element.76), channel_id=1, source_target_pairs={{0,2},{1,3},{2,1},{3,0},{4,6},{5,7},{6,5},{7,4},{8,10},{9,11},{10,... | collective-permute-start | bytes 2457608 | tf_op jit(solution)/shard_map/ppermute | solution.py:1297
  53.3 2.8 copy-start.11
  53.4 2.8 copy-start.13
  53.4 2.8 copy-start.15
  53.4 2.8 copy-start.17
  56.5 4.9 copy-start.7
  422.8 3.0 copy-start.1
  432.4 4.1 copy-start.5
  432.4 4.8 copy-start.6
  438.1 9.4 copy-start.2
  447.5 3.4 copy-start.21
  449.7 1.2 copy-start.19
  495.8 5.7 copy-start.12
  495.8 5.7 copy-start.14
  495.9 6.2 copy-start.16
  495.9 6.2 copy-start.18
  501.6 178.9 %collective-permute-start.6 = (bf16[2,2,256,1600]{2,3,1,0:T(8,128)(2,1)}, bf16[2,2,256,1600]{2,3,1,0:T(8,128)(2,1)}, u32[]{:S(2)}, u32[]{:S(2)}) collective-permute-start(bf16[2,2,256,1600]{2,3,1,0:T(8,128)(2,1)} %copy.94), channel_id=1, source_target_pairs={{0,1},{1,0},{2,3},{3,2},{4,5},{5,4},{6,7},{7,6},{8,9},{9,8},{10,11... | collective-permute-start | bytes 9830408 | tf_op jit(solution)/shard_map/ppermute | solution.py:1290
  507.1 3.5 copy-start.27
  657.8 246.8 %collective-permute-start.2 = (bf16[256,1600]{0,1:T(8,128)(2,1)}, bf16[256,1600]{0,1:T(8,128)(2,1)}, u32[]{:S(2)}, u32[]{:S(2)}) collective-permute-start(bf16[256,1600]{0,1:T(8,128)(2,1)} %bitcast.134), channel_id=1, source_target_pairs={{2,0},{3,1},{1,2},{0,3},{6,4},{7,5},{5,6},{4,7},{10,8},{11,9},{9,1... | collective-permute-start | bytes 2457608 | tf_op jit(solution)/shard_map/ppermute | solution.py:1303
  675.0 229.5 %collective-permute-start.3 = (bf16[256,1600]{0,1:T(8,128)(2,1)}, bf16[256,1600]{0,1:T(8,128)(2,1)}, u32[]{:S(2)}, u32[]{:S(2)}) collective-permute-start(bf16[256,1600]{0,1:T(8,128)(2,1)} %copy.118), channel_id=1, source_target_pairs={{2,3},{3,2},{6,7},{7,6},{10,11},{11,10},{14,15},{15,14},{18,19},{1... | collective-permute-start | bytes 2457608 | tf_op jit(solution)/shard_map/ppermute | solution.py:1304
  690.5 2.8 copy-start.9
  734.8 2.9 copy-start
  737.7 1.9 copy-start.3
  737.7 2.4 copy-start.8
  749.6 156.4 %collective-permute-start.7 = (f32[256,1600]{0,1:T(8,128)}, f32[256,1600]{0,1:T(8,128)}, u32[]{:S(2)}, u32[]{:S(2)}) collective-permute-start(f32[256,1600]{0,1:T(8,128)} %bitcast.105), channel_id=1, source_target_pairs={{2,0},{3,1},{1,2},{0,3},{6,4},{7,5},{5,6},{4,7},{10,8},{11,9},{9,1... | collective-permute-start | bytes 4915208 | tf_op jit(solution)/shard_map/ppermute | solution.py:1303
  750.8 146.8 %copy-start.24 = (bf16[256,1600]{1,0:T(8,128)(2,1)S(1)}, bf16[256,1600]{1,0:T(8,128)(2,1)}, u32[]{:S(2)}) copy-start(bf16[256,1600]{1,0:T(8,128)(2,1)} %get-tuple-element.71) | copy-start | bytes 2457604
  902.9 3.1 copy-start.4
  908.0 141.8 %collective-permute-start.8 = (f32[256,1600]{0,1:T(8,128)}, f32[256,1600]{0,1:T(8,128)}, u32[]{:S(2)}, u32[]{:S(2)}) collective-permute-start(f32[256,1600]{0,1:T(8,128)} %get-tuple-element.70), channel_id=1, source_target_pairs={{2,3},{3,2},{6,7},{7,6},{10,11},{11,10},{14,15},{15,14},{18,19},{1... | collective-permute-start | bytes 4915208 | tf_op jit(solution)/shard_map/ppermute | solution.py:1304
  909.8 3.8 copy-start.10
  1044.5 6.9 copy-start.20
  1051.4 1.9 copy-start.25
  1051.4 3.1 copy-start.26
Sparse Core Ops, SparseCore 0:
  915.1 122.9 all-reduce.2

commit v3 on v2

--- a/solution.py
+++ b/solution.py
@@ -381,68 +381,6 @@
         tuple(when(at_one, fifth[i]) for i in (1, 2)),
     ]
     return (dq0 * 0.125, dq1 * 0.125), own, other
-
-
-def chip_attention_back(extra, queries, keys, values, other, grad, out, logs, seg_q, seg_k, seg_sk):
-    _, rows, width = grad.shape
-    pairs = pl.cdiv(width, LANES)
-
-    def kernel(
-        extra_ref, q_ref, k_ref, v_ref, s_ref, g_ref, of_ref, lse_ref, rq_ref, ck_ref, cs_ref, dq_ref, own_ref, oth_ref
-    ):
-        masks = pair_masks(pl.program_id(0), width)
-        dq, own, oth = pair_backward(
-            extra_ref[0],
-            lambda i: q_ref[i],
-            lambda i: k_ref[i],
-            lambda i: v_ref[i],
-            lambda i: s_ref[0, i],
-            lambda i: s_ref[1, i],
-            lambda i: g_ref[i],
-            lambda i: of_ref[i],
-            lambda i: lse_ref[i],
-            lambda i: rq_ref[i],
-            lambda i: ck_ref[i],
-            lambda i: cs_ref[i],
-            masks,
-        )
-        for slot in range(2):
-            dq_ref[slot] = dq[slot].astype(bf16)
-            for kind in range(2):
-                own_ref[kind, slot] = own[slot][kind]
-                oth_ref[kind, slot] = oth[slot][kind].astype(bf16)
-
-    tile = pl.BlockSpec((2, rows, LANES), lambda p, e: (0, 0, p))
-    both = pl.BlockSpec((2, 2, rows, LANES), lambda p, e: (0, 0, 0, p))
-    col = pl.BlockSpec((2, rows, 1), lambda p, e: (0, 0, 0))
-    return pl.pallas_call(
-        kernel,
-        grid_spec=pltpu.PrefetchScalarGridSpec(
-            num_scalar_prefetch=1,
-            grid=(pairs,),
-            in_specs=[
-                tile,
-                tile,
-                tile,
-                both,
-                tile,
-                tile,
-                tile,
-                pl.BlockSpec((2, 1, rows), lambda p, e: (0, 0, 0)),
-                col,
-                col,
-            ],
-            out_specs=[tile, both, both],
-        ),
-        out_shape=[
-            jax.ShapeDtypeStruct((2, rows, width), bf16),
-            jax.ShapeDtypeStruct((2, 2, rows, width), f32),
-            jax.ShapeDtypeStruct((2, 2, rows, width), bf16),
-        ],
-        compiler_params=params(),
-        cost_estimate=cost(100 * rows * rows * width, 60 * rows * width),
-        name="chip_attn_back",
-    )(extra, queries, keys, values, other, grad, out, logs, seg_q, seg_k, seg_sk)
 
 
 def feed_in(normed, weight, bias, groups):
@@ -841,7 +779,7 @@
     return far_first(nz - 1 - k, z, nz)
 
 
-def forward_gather(grid, x_in, weights, vectors, seg_col, seg_row, seg_other):
+def forward_gather(grid, x_in, g_in, weights, vectors, seg_col, seg_row, seg_other):
     _, rows, width = x_in.shape
     tokens = 2 * rows
     nz = grid.nz
@@ -856,11 +794,11 @@
     n_slots = 4 * nz
 
     def kernel(
-        x_ref, wq_in, wo_in, wf_in, wp_in, vec_in, sc_ref, sr_ref, so_ref,
-        gq, go, gf, gp, vec_out, inner_out, act_out, sib_out,
-        n1_ref, q_ref, k_ref, v_ref, att_ref, of_ref, lse_ref, hid_ref, n2_ref,
-        sib, vbuf, rowbuf, jrow, wqkv, wbig, wout, stage_u, stage_a, mq, mo, mf, mp,
-        s_z, r_z, s_p, r_p, s_vz, r_vz, s_vy, r_vy, s_kv, r_kv, s_loc, s_w, s_st,
+        x_own, g_own, wq_in, wo_in, wf_in, wp_in, vec_in, sc_ref, sr_ref, so_ref,
+        gq, go, gf, gp, vec_out, slope_out, act_out, sib_out, x_out, g_out, n1t_out, n2t_out, att_out, dw_out,
+        q_out, k_out, v_out, of_out, lse_out, hid_out,
+        q_ref, k_ref, v_ref, of_ref, lse_ref, hid_ref, x_ref, n1_ref, att_ref, flip, sib, vbuf, rowbuf, jrow, wqkv, wbig, wout, stage_u, stage_a, stage_w, mq, mo, mf, mp,
+        s_z, r_z, s_p, r_p, s_vz, r_vz, s_vy, r_vy, s_kv, r_kv, s_loc, s_w, s_st, s_sh, r_sh, s_fl, s_out, s_dw,
     ):
         d, c = lax.axis_index("dp"), lax.axis_index("ctx")
         z, y = d // grid.ny, d % grid.ny
@@ -874,7 +812,9 @@
         has_up, has_down = z < nz - 1, z > 0
         gathered = (gq, go, gf, gp)
         mine = (mq, mo, mf, mp)
-        cuts = [(w.shape[0] // 2 + 7) // 8 * 8 for w in weights]
+        cuts = [(w.shape[0] * 2 // 5 + 7) // 8 * 8 for w in weights]
+        at_cross = (d, (1 - x) * 2 + 1 - core)
+        n2_ref = n1_ref
 
         def piece(w, zz, yy, xx, cc, half=None):
             h = weights[w].shape[0]
@@ -947,6 +887,54 @@
                 def _():
                     z_arrived(w, j)
                     z_send(w, zz, way, j)
+
+        def across(kind, p, target):
+            src, dst = moved[kind]
+            at = pl.ds(p * (rows // nz), rows // nz)
+            return remote(src.at[1 - x, at], dst.at[x, at], s_sh.at[kind, p], r_sh.at[kind, p], target)
+
+        def within(kind):
+            src, dst = moved[kind]
+            return remote(src.at[1], dst.at[1], s_sh.at[kind, nz], r_sh.at[kind, nz], at_sib)
+
+        def stays(kind):
+            src, dst = moved[kind]
+            return pltpu.make_async_copy(src.at[0], dst.at[0], s_sh.at[kind, nz])
+
+        moved = ((x_own, x_ref), (g_own, g_out))
+
+        def move(kind, p):
+            @pl.when(x == 0)
+            def _():
+                across(kind, p, at_x).start()
+                if p == 0:
+                    stays(kind).start()
+
+            @pl.when(x == 1)
+            def _():
+                across(kind, p, at_cross).start()
+                if p == 0:
+                    within(kind).start()
+
+        def moved_in(kind):
+            for p in range(nz):
+                across(kind, p, at_x).wait_recv()
+
+            @pl.when(x == 0)
+            def _():
+                stays(kind).wait()
+
+            @pl.when(x == 1)
+            def _():
+                within(kind).wait_recv()
+
+        def moved_out(kind):
+            for p in range(nz):
+                across(kind, p, at_x).wait_send()
+
+            @pl.when(x == 1)
+            def _():
+                within(kind).wait_send()
 
         def tick(i):
             if i < n_slots:
@@ -973,15 +961,19 @@
                 part_copy(w, 2, j).wait_recv()
                 part_copy(w, 3, j).wait_recv()
                 part_copy(w, 4, j).start()
-            if i + 1 < n_slots:
+            if i + 1 < n_slots and (i + 1) % nz != 0:
                 pass_on(i + 1)
+            if i % nz == 1 and i + nz - 1 < n_slots:
+                pass_on(i + nz - 1)
+            if i // nz in (0, 2):
+                move(i // nz // 2, i % nz)
 
         def complete(w):
             for j in range(nz):
                 part_copy(w, 4, j).wait_recv()
 
         barrier = pltpu.get_barrier_semaphore()
-        for target in (at_sib, at_x, at_y):
+        for target in (at_sib, at_x, at_y, at_cross):
             pl.semaphore_signal(barrier, inc=1, device_id=target, device_id_type=MESH)
 
         @pl.when(has_up)
@@ -1009,11 +1001,14 @@
             cp.start()
         for cp in local:
             cp.wait()
-        pl.semaphore_wait(barrier, 3 + has_up.astype(jnp.int32) + has_down.astype(jnp.int32))
+        pl.semaphore_wait(barrier, 4 + has_up.astype(jnp.int32) + has_down.astype(jnp.int32))
 
         pass_on(0)
         for i in range(nz + 1):
             tick(i)
+        moved_in(0)
+        keep_x = pltpu.make_async_copy(x_ref, x_out, s_loc.at[2])
+        keep_x.start()
         for j in range(nz):
             vy_copy(j).wait_recv()
 
@@ -1032,6 +1027,17 @@
 
         for i in range(nz + 1, nz + 3):
             tick(i)
+
+        def flipped(dst):
+            return pltpu.make_async_copy(flip, dst, s_fl.at[0])
+
+        def turn(value, dst, before):
+            if before is not None:
+                flipped(before).wait()
+            flip[...] = value.T
+            flipped(dst).start()
+
+        turn(n1_ref[...].reshape(tokens, width), n1t_out, None)
         complete(0)
 
         def stream(source, buffer, body, hooks):
@@ -1080,7 +1086,11 @@
             remote(ref, sib.at[kind], s_kv.at[kind], r_kv.at[kind], at_sib)
             for kind, ref in enumerate((k_ref, v_ref))
         ]
-        for cp in swaps:
+        results = (
+            (q_ref, q_out), (k_ref, k_out), (v_ref, v_out), (of_ref, of_out), (lse_ref, lse_out), (hid_ref, hid_out)
+        )
+        saved = [pltpu.make_async_copy(src, dst, s_out.at[i]) for i, (src, dst) in enumerate(results)]
+        for cp in (*swaps, *saved[:3]):
             cp.start()
         for cp in swaps:
             cp.wait_recv()
@@ -1113,8 +1123,10 @@
 
         lax.fori_loop(0, pairs, attend, 0)
         keep = pltpu.make_async_copy(sib, sib_out, s_loc.at[0])
-        keep.start()
+        for cp in (keep, *saved[3:5]):
+            cp.start()
         complete(1)
+        turn(att_ref[:, :, :width].reshape(tokens, width), att_out, n1t_out)
 
         def branch(part, slot):
             product = dot_nn(
@@ -1131,16 +1143,46 @@
             hidden = x_ref[s].astype(f32) + hid_ref[s] + rowbuf[2:3, :]
             hid_ref[s] = hidden
             n2_ref[s] = layer_norm(hidden, rowbuf[6:7, :], rowbuf[7:8, :]).astype(bf16)
+        saved[5].start()
         tick(nz + 8)
+        turn(n2_ref[...].reshape(tokens, width), n2t_out, att_out)
         tick(nz + 9)
+        moved_in(1)
+        for half in range(2):
+            fetch = pltpu.make_async_copy(
+                g_out.at[half], stage_a.at[0, pl.ds(half * rows, rows)], s_loc.at[3]
+            )
+            fetch.start()
+            fetch.wait()
+        flipped(n2t_out).wait()
+        flip[...] = stage_a[0].T
         complete(2)
+        band = width // nz
+
+        def save_w(i):
+            return pltpu.make_async_copy(
+                stage_w.at[i % 2], dw_out.at[i // nz, pl.ds(pl.multiple_of(i % nz * band, 16), band)], s_dw.at[i % 2]
+            )
+
+        def proj_terms(group):
+            def body(i, _):
+                @pl.when(i >= 2)
+                def _():
+                    save_w(i - 2).wait()
+
+                at = pl.ds(pl.multiple_of(i % nz * band, 16), band)
+                stage_w[i % 2] = dot_nn(flip[at, :], stage_a[group % 2]).astype(bf16)
+                save_w(i).start()
+                return 0
+
+            lax.fori_loop(group * nz, (group + 1) * nz, body, 0)
 
         ratio = parts // groups
 
         def saves(group):
             slot = group % 2
             return (
-                pltpu.make_async_copy(stage_u.at[slot], inner_out.at[group], s_st.at[0, slot]),
+                pltpu.make_async_copy(stage_u.at[slot], slope_out.at[group], s_st.at[0, slot]),
                 pltpu.make_async_copy(stage_a.at[slot], act_out.at[group], s_st.at[1, slot]),
             )
 
@@ -1155,30 +1197,38 @@
             left = n2_ref[...].reshape(tokens, width)
             u = dot_nn(left, wbig[slot].reshape(width, n_fc))
             u = u + vbuf[part // grid.ny, part % grid.ny][0:1, :n_fc]
-            act = (0.5 * u * (1.0 + jnp.tanh(GELU_C * (u + GELU_A * u * u * u)))).astype(bf16)
+            t = jnp.tanh(GELU_C * (u + GELU_A * u * u * u))
+            act = (0.5 * u * (1.0 + t)).astype(bf16)
+            slope = 0.5 * (1.0 + t) + 0.5 * u * (1.0 - t * t) * (GELU_C * (1.0 + 3.0 * GELU_A * u * u))
+            slope = slope.astype(bf16)
             for r in range(ratio):
 
                 @pl.when(place == r)
                 def _():
-                    stage_u[group % 2, :, r * n_fc : (r + 1) * n_fc] = u
+                    stage_u[group % 2, :, r * n_fc : (r + 1) * n_fc] = slope
                     stage_a[group % 2, :, r * n_fc : (r + 1) * n_fc] = act
 
             @pl.when(place == ratio - 1)
             def _():
                 for cp in saves(group):
                     cp.start()
-
-        stream(gf, wbig, feed, {1: [nz + 10], 5: [nz + 11]})
-        tick(nz + 12)
+                proj_terms(group)
+
+        stream(gf, wbig, feed, {0: [nz + 10], 3: [nz + 11], 6: [nz + 12]})
         tick(nz + 13)
         save_vec = pltpu.make_async_copy(vbuf, vec_out, s_loc.at[1])
         save_vec.start()
         for group in range(groups - 2, groups):
             for cp in saves(group):
                 cp.wait()
-        keep.wait()
+        for i in range(groups * nz - 2, groups * nz):
+            save_w(i).wait()
+        for cp in (keep, keep_x, *saved):
+            cp.wait()
         save_vec.wait()
         complete(3)
+        for kind in range(2):
+            moved_out(kind)
         for cp in swaps:
             cp.wait_send()
 
@@ -1213,25 +1263,33 @@
         *columns,
         jax.ShapeDtypeStruct((grid.nx, 2, nz, grid.ny, *weights[3].shape), bf16),
         jax.ShapeDtypeStruct((nz, grid.ny, 8, n_vec), f32),
-        jax.ShapeDtypeStruct((groups, tokens, ff), f32),
+        jax.ShapeDtypeStruct((groups, tokens, ff), bf16),
         jax.ShapeDtypeStruct((groups, tokens, ff), bf16),
         jax.ShapeDtypeStruct((2, 2, rows, wide), bf16),
         low,
-        wide_low,
+        low,
+        *[jax.ShapeDtypeStruct((width, tokens), bf16)] * 3,
+        jax.ShapeDtypeStruct((groups, width, ff), bf16),
         wide_low,
         wide_low,
         wide_low,
         wide_full,
         wide_full,
         jax.ShapeDtypeStruct((2, rows, width), f32),
-        low,
     ]
     return pl.pallas_call(
         kernel,
         out_shape=out_shape,
-        in_specs=[vm] + [any_] * 4 + [any_] + [vm] * 3,
-        out_specs=[any_] * 8 + [vm] * 9,
+        in_specs=[any_] * 7 + [vm] * 3,
+        out_specs=[any_] * 20,
         scratch_shapes=[
+            *[pltpu.VMEM((2, rows, wide), bf16)] * 3,
+            *[pltpu.VMEM((2, rows, wide), f32)] * 2,
+            pltpu.VMEM((2, rows, width), f32),
+            pltpu.VMEM((2, rows, width), bf16),
+            pltpu.VMEM((2, rows, width), bf16),
+            pltpu.VMEM((2, rows, wide), bf16),
+            pltpu.VMEM((width, tokens), bf16),
             pltpu.VMEM((2, 2, rows, wide), bf16),
             pltpu.VMEM((nz, grid.ny, 8, n_vec), f32),
             pltpu.VMEM((8, width), f32),
@@ -1239,8 +1297,9 @@
             pltpu.VMEM((2, grid.nx, 2, slab, n_qkv), bf16),
             pltpu.VMEM((2, grid.nx, 2, slab, n_fc), bf16),
             pltpu.VMEM((2, grid.nx, 2, slab, n_out), bf16),
-            pltpu.VMEM((2, tokens, ff), f32),
             pltpu.VMEM((2, tokens, ff), bf16),
+            pltpu.VMEM((2, tokens, ff), bf16),
+            pltpu.VMEM((2, width // nz, ff), bf16),
             *(pltpu.VMEM(w.shape, bf16) for w in weights),
             dma((4, 2, nz)),
             dma((4, nz)),
@@ -1255,13 +1314,840 @@
             dma((5,)),
             dma((2,)),
             dma((2, 2)),
+            dma((2, nz + 1)),
+            dma((2, nz + 1)),
+            dma((1,)),
+            dma((6,)),
+            dma((2,)),
         ],
         compiler_params=pltpu.CompilerParams(
             collective_id=4, has_side_effects=True, vmem_limit_bytes=VMEM_LIMIT
         ),
         cost_estimate=cost(30e9, 150e6),
         name="forward",
-    )(x_in, *weights, vectors, seg_col, seg_row, seg_other)
+    )(x_in, g_in, *weights, vectors, seg_col, seg_row, seg_other)
+
+
+def backward_sums(
+    grid, grad, proj_terms, act, slope, w_proj, hidden, normed_t, w_fc, w_out, queries, keys, values, other,
+    att_full, logs, x_in, first_t, att_t, w_qkv, vec_rows, seg_row, seg_col, seg_other,
+):
+    tokens, width = grad.shape
+    rows = tokens // 2
+    nz, parts, groups = grid.nz, grid.dp, grid.ctx
+    wide = queries.shape[2]
+    pairs = wide // LANES
+    ff, n_fc, n_out = act.shape[2], w_fc.shape[2], w_out.shape[2]
+    n_qkv = 3 * width // parts
+    slab = width // groups
+    cols = width // parts
+    ratio = parts // groups
+    h, n = cols * 2 // 5 // 16 * 16, ff
+    low_half = slab // 2
+    v_rows = 8 + parts
+    chunk = min(rows, 64)
+    units = 3 * nz
+
+    def kernel(
+        g_in, dw_in, act_in, u_in, wp_in, hid_in, nt_in, wf_in, wo_in, q_in, k_in, v_in, s_in, of_in, lse_in,
+        x_in, n1t_in, at_in, wq_in, vr_ref, rq_ref, ck_ref, cs_ref,
+        gp_out, gf_out, gq_out, sum_ref, y_out, di_out, dx_out, hg_out, bg_out, pg_out, ig_out,
+        sa, sb, ga, gb, oa, ob, xa, yb, ta, tb, ya, xb, la, lb, za, zb, ra, rb, swap, v_send, v_got,
+        ss, rs, zss, zrs, s_ld, s_st, s_tile, s_kv, s_vec, r_vec, s_back, r_back, s_out, s_dw,
+    ):
+        d, c = lax.axis_index("dp"), lax.axis_index("ctx")
+        z, y = d // grid.ny, d % grid.ny
+        x, core = c // 2, c % 2
+        extra = 1 - core
+        at_sib = (d, c + 1 - 2 * core)
+        at_x = (d, (1 - x) * 2 + core)
+        at_y = (z * grid.ny + 1 - y, c)
+        at_cross = (d, (1 - x) * 2 + 1 - core)
+        at_up = ((z + 1) * grid.ny + y, c)
+        at_down = ((z - 1) * grid.ny + y, c)
+        has_up, has_down = z < nz - 1, z > 0
+
+        def remote(src, dst, send, recv, target):
+            return pltpu.make_async_remote_copy(
+                src_ref=src, dst_ref=dst, send_sem=send, recv_sem=recv, device_id=target, device_id_type=MESH
+            )
+
+        def copy(src, dst, kind, u, target):
+            return remote(src, dst, ss.at[kind, u], rs.at[kind, u], target)
+
+        def sib(u):
+            return copy(sa, ga.at[u % 2], 0, u, at_sib), copy(sb, gb.at[u % 2], 1, u, at_sib)
+
+        def first(u):
+            return copy(oa.at[1 - x], xa.at[u % 2], 2, u, at_x), copy(ob.at[1 - y], yb.at[u % 2], 3, u, at_y)
+
+        def second(u):
+            return copy(ta, ya.at[u % 3], 4, u, at_y), copy(tb, xb.at[u % 3], 5, u, at_x)
+
+        def line(u, to, up, place):
+            group, k = divmod(u, nz)
+            target = at_up if up else at_down
+            return [
+                remote(
+                    (za, zb)[i].at[min(k, nz - 2)],
+                    (ra, rb)[i].at[group % 2, place],
+                    zss.at[i, u],
+                    zrs.at[i, group, place],
+                    target,
+                )
+                for i in range(2)
+            ]
+
+        def add_arrived(u, place):
+            for cp in line(u, 0, True, place):
+                cp.wait_recv()
+            la[u % 2] += ra[u // nz % 2, place].astype(f32)
+            lb[u % 2] += rb[u // nz % 2, place].astype(f32)
+
+        def target_z(u):
+            return far_first(u % nz, z, nz)
+
+        def finish(u):
+            at_end = jnp.logical_not(has_up & has_down)
+
+            @pl.when(jnp.logical_not(at_end))
+            def _():
+                finish_unit(u)
+
+            @pl.when(at_end)
+            def _():
+                if u % nz == nz - 1:
+                    finish_unit(u)
+                if (u + 1) % nz != nz - 1:
+                    finish_unit(u + 1)
+
+        def finish_unit(u):
+            if 0 <= u < units:
+                to = target_z(u)
+                for cp in second(u):
+                    cp.wait_recv()
+                la[u % 2] += ya[u % 3].astype(f32)
+                lb[u % 2] += xb[u % 3].astype(f32)
+                if u % nz == nz - 1:
+
+                    @pl.when(has_down)
+                    def _():
+                        add_arrived(u, z)
+
+                    @pl.when(has_up)
+                    def _():
+                        add_arrived(u, nz)
+
+                    out = (gp_out, gf_out, gq_out)[u // nz]
+                    done = [
+                        pltpu.make_async_copy(src, out.at[at], s_out.at[i])
+                        for i, (src, at) in enumerate(
+                            ((la.at[u % 2], pl.ds(0, h)), (lb.at[u % 2], pl.ds(h, cols - h)))
+                        )
+                    ]
+                    for cp in done:
+                        cp.start()
+                    for cp in done:
+                        cp.wait()
+                else:
+                    for up in (True, False):
+                        going = (to > z) if up else (to < z)
+
+                        @pl.when(going & (has_down if up else has_up))
+                        def _():
+                            add_arrived(u, to)
+
+                        @pl.when(going)
+                        def _():
+                            if u >= nz:
+                                for cp in line(u - nz, 0, up, 0):
+                                    cp.wait_send()
+                            za[u % nz] = la[u % 2].astype(bf16)
+                            zb[u % nz] = lb[u % 2].astype(bf16)
+                            place = to if up else jnp.where(to == z - 1, nz, to)
+                            for cp in line(u, to, up, place):
+                                cp.start()
+
+        def second_stage(u):
+            if 0 <= u < units:
+                if u >= 1:
+                    for cp in second(u - 1):
+                        cp.wait_send()
+                for cp in first(u):
+                    cp.wait_recv()
+                s = u % 2
+                go_a, go_b = second(u)
+                ta[...] = oa[x, 1 - y] + xa[s, 1 - y]
+                go_a.start()
+                tb[...] = ob[y, 1 - x] + yb[s, 1 - x]
+                go_b.start()
+                la[s] = oa[x, y].astype(f32) + xa[s, y].astype(f32)
+                lb[s] = ob[y, x].astype(f32) + yb[s, x].astype(f32)
+        def give(u, unit):
+            if u >= 1:
+                for cp in sib(u - 1):
+                    cp.wait_send()
+
+            def store(y_to, x_to, value):
+                sa[x_to, y_to] = value[:h].astype(bf16)
+                sb[y_to, x_to] = value[h:].astype(bf16)
+
+            if u < nz:
+                take_terms(u, 1 - core, sa, sb)
+            else:
+                unit(target_z(u), 1 - core, store)
+            for cp in sib(u):
+                cp.start()
+
+        def take_terms(u, plane, to_a, to_b):
+            loads = []
+            for y_to in range(2):
+                first_row = pl.multiple_of((target_z(u) * grid.ny + y_to) * cols, 8)
+                for x_to in range(2):
+                    src = dw_in.at[2 * x_to + plane]
+                    loads += [
+                        pltpu.make_async_copy(
+                            src.at[pl.ds(first_row, h)], to_a.at[x_to, y_to], s_dw.at[0, y_to, x_to]
+                        ),
+                        pltpu.make_async_copy(
+                            src.at[pl.ds(pl.multiple_of(first_row + h, 8), cols - h)],
+                            to_b.at[y_to, x_to],
+                            s_dw.at[1, y_to, x_to],
+                        ),
+                    ]
+            for cp in loads:
+                cp.start()
+            for cp in loads:
+                cp.wait()
+
+        def begin_unit(u, unit):
+            if u < units:
+                s = u % 2
+                if u % nz == 0:
+                    give(u, unit)
+                if u >= 1:
+                    for cp in first(u - 1):
+                        cp.wait_send()
+                if u < nz:
+                    take_terms(u, core, oa, ob)
+                for cp in sib(u):
+                    cp.wait_recv()
+
+                def store(y_to, x_to, value):
+                    oa[x_to, y_to] = (value[:h] + ga[s, x_to, y_to].astype(f32)).astype(bf16)
+                    ob[y_to, x_to] = (value[h:] + gb[s, y_to, x_to].astype(f32)).astype(bf16)
+
+                if u < nz:
+                    oa[...] = oa[...] + ga[s]
+                    ob[...] = ob[...] + gb[s]
+                else:
+                    unit(target_z(u), core, store)
+                for cp in first(u):
+                    cp.start()
+                if (u + 1) % nz != 0:
+                    give(u + 1, unit)
+
+        def tick(t, unit=None):
+            finish(t - 3)
+            second_stage(t - 1)
+            begin_unit(t, unit)
+
+        def beside(term):
+            return jnp.concatenate([term[:low_half], term[low_half:]], axis=1)
+
+        barrier = pltpu.get_barrier_semaphore()
+        for target in (at_sib, at_x, at_y, at_cross):
+            pl.semaphore_signal(barrier, inc=1, device_id=target, device_id_type=MESH)
+
+        @pl.when(has_up)
+        def _():
+            pl.semaphore_signal(barrier, inc=1, device_id=at_up, device_id_type=MESH)
+
+        @pl.when(has_down)
+        def _():
+            pl.semaphore_signal(barrier, inc=1, device_id=at_down, device_id_type=MESH)
+
+        pl.semaphore_wait(barrier, 4 + has_up.astype(jnp.int32) + has_down.astype(jnp.int32))
+
+        def back_far(kind, src, dst, target):
+            return remote(src.at[1 - x], dst.at[x], s_back.at[kind, 0], r_back.at[kind, 0], target)
+
+        def back_near(kind, src, dst):
+            return remote(src.at[1], dst.at[1], s_back.at[kind, 1], r_back.at[kind, 1], at_sib)
+
+        def back_stay(kind, src, dst):
+            return pltpu.make_async_copy(src.at[0], dst.at[0], s_back.at[kind, 1])
+
+        def give_back(kind, src, dst):
+            @pl.when(x == 0)
+            def _():
+                back_far(kind, src, dst, at_cross).start()
+                back_stay(kind, src, dst).start()
+
+            @pl.when(x == 1)
+            def _():
+                back_far(kind, src, dst, at_x).start()
+                back_near(kind, src, dst).start()
+
+        def given_back(kind, src, dst):
+            back_far(kind, src, dst, at_x).wait_send()
+
+            @pl.when(x == 0)
+            def _():
+                back_stay(kind, src, dst).wait()
+
+            @pl.when(x == 1)
+            def _():
+                back_near(kind, src, dst).wait_send()
+
+        def got_back(kind, src, dst):
+            back_far(kind, src, dst, at_x).wait_recv()
+
+            @pl.when(x == 1)
+            def _():
+                back_near(kind, src, dst).wait_recv()
+
+        def vec_copy(i, target):
+            return remote(v_send.at[i], v_got.at[i], s_vec.at[i], r_vec.at[i], target)
+
+        def vec_step(i):
+            targets = (at_sib, at_x, at_y)
+            if 1 <= i <= 3:
+                vec_copy(i - 1, targets[i - 1]).wait()
+                sum_ref[...] += v_got[i - 1]
+            if i < 3:
+                v_send[i] = sum_ref[...]
+                vec_copy(i, targets[i]).start()
+                return
+            if i == 3:
+                ways = ((3, has_up, has_down, at_up), (4, has_down, has_up, at_down))
+                for slot, going, behind, target in ways:
+                    v_send[slot] = sum_ref[...]
+
+                    @pl.when(going & jnp.logical_not(behind))
+                    def _():
+                        vec_copy(slot, target).start()
+
+                for slot, going, behind, target in ways:
+
+                    @pl.when(behind)
+                    def _():
+                        vec_copy(slot, target).wait_recv()
+                        v_send[slot] += v_got[slot]
+
+                    @pl.when(going & behind)
+                    def _():
+                        vec_copy(slot, target).start()
+
+                return
+            for slot, going, behind, target in ((3, has_up, has_down, at_up), (4, has_down, has_up, at_down)):
+
+                @pl.when(behind)
+                def _():
+                    sum_ref[...] += v_got[slot]
+
+                @pl.when(going)
+                def _():
+                    vec_copy(slot, target).wait_send()
+
+        def load(src, dst, sem):
+            return pltpu.make_async_copy(src, dst, s_ld.at[sem])
+
+        def first_phase(g, acts, w, u, ig_st, total):
+            begin = load(g_in, g, 3)
+            begin.start()
+            tick(0)
+
+            def fetch(group):
+                return load(wp_in.at[group], w, 4), load(u_in.at[group], u, 5)
+
+            for cp in fetch(0):
+                cp.start()
+            begin.wait()
+            sum_ref[0:1, :] = jnp.sum(g[...].astype(f32), axis=0, keepdims=True)
+            hid = load(hid_in, total, 6)
+            hid.start()
+            hid.wait()
+
+            def save(group):
+                return pltpu.make_async_copy(ig_st, ig_out.at[pl.ds(group * ratio, ratio)], s_st.at[0])
+
+            def body(group, _):
+                for cp in fetch(group):
+                    cp.wait()
+                act_load = load(act_in.at[group], acts, 0)
+                act_load.start()
+
+                @pl.when(group > 0)
+                def _():
+                    save(group - 1).wait()
+
+                out = (dot_nn(g[...], w[...]) * u[...].astype(f32)).astype(bf16)
+                sums = jnp.sum(out.astype(f32), axis=0, keepdims=True)
+                for r in range(ratio):
+                    ig_st[r] = out[:, r * n_fc : (r + 1) * n_fc]
+                    sum_ref[pl.ds(8 + group * ratio + r, 1), :n_fc] = sums[:, r * n_fc : (r + 1) * n_fc]
+                save(group).start()
+                act_load.wait()
+                total[...] += dot_nt(acts[...], w[...])
+
+                @pl.when(group + 1 < groups)
+                def _():
+                    for cp in fetch(group + 1):
+                        cp.start()
+
+                for i in range(nz - 1):
+
+                    @pl.when(group == i)
+                    def _():
+                        tick(1 + i)
+
+                return 0
+
+            lax.fori_loop(0, groups, body, 0)
+            save(groups - 1).wait()
+            result = (total[...] + vr_ref[0:1, :]).astype(bf16)
+            swap[0, :, :, :width] = result.reshape(2, rows, width)
+            give_back(0, swap.at[0], y_out)
+
+        low_rows = pltpu.VMEM((tokens, width), bf16)
+        full_rows = pltpu.VMEM((tokens, width), f32)
+        pl.run_scoped(
+            first_phase,
+            low_rows,
+            pltpu.VMEM((tokens, ff), bf16),
+            pltpu.VMEM((width, ff), bf16),
+            pltpu.VMEM((tokens, ff), bf16),
+            pltpu.VMEM((ratio, tokens, n_fc), bf16),
+            full_rows,
+        )
+
+        def second_phase(nt, igs):
+            def fc_unit(to, plane, store):
+                loads = [load(ig_out.at[to * grid.ny + y_to], igs.at[y_to], y_to) for y_to in range(2)]
+                for cp in loads:
+                    cp.start()
+                for cp in loads:
+                    cp.wait()
+
+                def body(i, _):
+                    y_to, x_to = i // 2, i % 2
+                    at = pl.ds(pl.multiple_of((2 * x_to + plane) * slab, 16), slab)
+                    store(y_to, x_to, beside(dot_nn(nt[at, :], igs[y_to])))
+                    return 0
+
+                lax.fori_loop(0, 4, body, 0)
+
+            begin = load(nt_in, nt, 2)
+            begin.start()
+            begin.wait()
+            tick(nz, fc_unit)
+
+            def second_norm(dn, hid):
+                hid_load = load(hid_in, hid, 7)
+                hid_load.start()
+                dn[...] = jnp.zeros_like(dn)
+                pl.run_scoped(
+                    functools.partial(back_feed, dn),
+                    pltpu.VMEM((2, width, n_fc), bf16),
+                    pltpu.VMEM((2, tokens, n_fc), bf16),
+                )
+                finish_norm(dn, hid, hid_load)
+
+            def back_feed(dn, w, ig2):
+                def fetch(part):
+                    s = part % 2
+                    return load(wf_in.at[part], w.at[s], 3 + s), load(ig_out.at[part], ig2.at[s], 5 + s)
+
+                for cp in fetch(0):
+                    cp.start()
+
+                def body(part, _):
+                    for cp in fetch(part):
+                        cp.wait()
+
+                    @pl.when(part + 1 < parts)
+                    def _():
+                        for cp in fetch(part + 1):
+                            cp.start()
+
+                    dn[...] += dot_nt(ig2[part % 2], w[part % 2])
+
+                    @pl.when(part == parts // 2)
+                    def _():
+                        tick(nz + 1, fc_unit)
+
+                    return 0
+
+                lax.fori_loop(0, parts, body, 0)
+
+            def finish_norm(dn, hid, hid_load):
+                hid_load.wait()
+                for v in (1, 2, 3):
+                    sum_ref[v : v + 1, :] = jnp.zeros((1, width), f32)
+
+                def norm(i, _):
+                    at = pl.ds(pl.multiple_of(i * chunk, chunk), chunk)
+                    values = hid[at, :]
+                    grads = dn[at, :]
+                    center = values - jnp.mean(values, axis=-1, keepdims=True)
+                    factor = lax.rsqrt(jnp.mean(center * center, axis=-1, keepdims=True) + EPS)
+                    xhat = center * factor
+                    sum_ref[2:3, :] += jnp.sum(grads * xhat, axis=0, keepdims=True)
+                    sum_ref[3:4, :] += jnp.sum(grads, axis=0, keepdims=True)
+                    scaled = grads * vr_ref[1:2, :]
+                    back = factor * (
+                        scaled
+                        - jnp.mean(scaled, axis=-1, keepdims=True)
+                        - xhat * jnp.mean(scaled * xhat, axis=-1, keepdims=True)
+                    )
+                    hid[at, :] = back
+                    return 0
+
+                lax.fori_loop(0, tokens // chunk, norm, 0)
+
+                def branch(bg, gl):
+                    grad_load = load(g_in, gl, 3)
+                    grad_load.start()
+                    grad_load.wait()
+                    hid[...] += gl[...].astype(f32)
+                    low_grad = hid[...].astype(bf16)
+                    sum_ref[1:2, :] = jnp.sum(low_grad.astype(f32), axis=0, keepdims=True)
+                    for part in range(parts):
+                        bg[part] = low_grad[:, part * n_out : (part + 1) * n_out]
+                    outs = [
+                        pltpu.make_async_copy(hid, hg_out, s_st.at[0]),
+                        pltpu.make_async_copy(bg, bg_out, s_st.at[1]),
+                    ]
+                    for cp in outs:
+                        cp.start()
+                    for cp in outs:
+                        cp.wait()
+
+                pl.run_scoped(branch, pltpu.VMEM((parts, tokens, n_out), bf16), low_rows)
+
+            pl.run_scoped(second_norm, full_rows, full_rows)
+            given_back(0, swap.at[0], y_out)
+            tick(nz + 2, fc_unit)
+
+            def attention(ag):
+                def back_out(acc, w, bgs):
+                    def fetch(part):
+                        s = part % 2
+                        return load(wo_in.at[part], w.at[s], 3 + s), load(bg_out.at[part], bgs.at[s], 5 + s)
+
+                    for cp in fetch(0):
+                        cp.start()
+                    acc[...] = jnp.zeros_like(acc)
+
+                    def body(part, _):
+                        for cp in fetch(part):
+                            cp.wait()
+
+                        @pl.when(part + 1 < parts)
+                        def _():
+                            for cp in fetch(part + 1):
+                                cp.start()
+
+                        acc[...] += dot_nt(bgs[part % 2], w[part % 2])
+                        return 0
+
+                    lax.fori_loop(0, parts, body, 0)
+                    ag[:, :, wide - LANES :] = jnp.zeros((2, rows, LANES), bf16)
+                    ag[:, :, :width] = acc[...].astype(bf16).reshape(2, rows, width)
+
+                pl.run_scoped(
+                    back_out,
+                    full_rows,
+                    pltpu.VMEM((2, width, n_out), bf16),
+                    pltpu.VMEM((2, tokens, n_out), bf16),
+                )
+
+                pl.run_scoped(
+                    functools.partial(attend_back, ag),
+                    wide_low,
+                    pltpu.VMEM((2, 2, rows, wide), f32),
+                    pltpu.VMEM((2, 2, rows, wide), bf16),
+                )
+
+            def attend_back(ag, dq, own, oth):
+                def heads(tq, tk, tv, ts, tof, tls):
+                    def tiles(p):
+                        s = p % 2
+                        lanes = pl.ds(pl.multiple_of(p * LANES, LANES), LANES)
+                        return [
+                            pltpu.make_async_copy(src.at[:, :, lanes], dst.at[s], s_tile.at[i, s])
+                            for i, (src, dst) in enumerate(
+                                ((q_in, tq), (k_in, tk), (v_in, tv), (of_in, tof), (lse_in, tls))
+                            )
+                        ] + [pltpu.make_async_copy(s_in.at[:, :, :, lanes], ts.at[s], s_tile.at[5, s])]
+
+                    for cp in tiles(0):
+                        cp.start()
+
+                    def body(p, _):
+                        s = p % 2
+                        for cp in tiles(p):
+                            cp.wait()
+
+                        @pl.when(p + 1 < pairs)
+                        def _():
+                            for cp in tiles(p + 1):
+                                cp.start()
+
+                        lanes = pl.ds(pl.multiple_of(p * LANES, LANES), LANES)
+                        got_q, got_own, got_oth = pair_backward(
+                            extra,
+                            lambda i: tq[s, i],
+                            lambda i: tk[s, i],
+                            lambda i: tv[s, i],
+                            lambda i: ts[s, 0, i],
+                            lambda i: ts[s, 1, i],
+                            lambda i: ag[i, :, lanes],
+                            lambda i: tof[s, i],
+                            lambda i: tls[s, i],
+                            lambda i: rq_ref[i],
+                            lambda i: ck_ref[i],
+                            lambda i: cs_ref[i],
+                            pair_masks(p, width),
+                        )
+                        for slot in range(2):
+                            dq[slot, :, lanes] = got_q[slot].astype(bf16)
+                            for kind in range(2):
+                                own[kind, slot, :, lanes] = got_own[slot][kind]
+                                oth[kind, slot, :, lanes] = got_oth[slot][kind].astype(bf16)
+                        @pl.when(p == 3)
+                        def _():
+                            tick(nz + 3, fc_unit)
+
+                        @pl.when(p == 8)
+                        def _():
+                            finish(2 * nz - 3)
+                            second_stage(2 * nz - 1)
+
+                        return 0
+
+                    lax.fori_loop(0, pairs, body, 0)
+
+                low_tile, full_tile = pltpu.VMEM((2, 2, rows, LANES), bf16), pltpu.VMEM((2, 2, rows, LANES), f32)
+                pl.run_scoped(
+                    heads, low_tile, low_tile, low_tile, pltpu.VMEM((2, 2, 2, rows, LANES), bf16), full_tile, full_tile
+                )
+                give = remote(oth, swap, s_kv.at[0], s_kv.at[1], at_sib)
+                give.start()
+                give.wait_recv()
+                give.wait_send()
+                for kind in range(2):
+                    oth[kind] = (own[kind] + swap[kind].astype(f32)).astype(bf16)
+                sum_ref[4:5, :] = jnp.sum(dq[...].astype(f32), axis=(0, 1))[None, :width]
+                sum_ref[5:6, :] = jnp.sum(oth[1].astype(f32), axis=(0, 1))[None, :width]
+
+                def spread(st):
+                    def save(part):
+                        return pltpu.make_async_copy(st.at[part % 2], pg_out.at[part], s_st.at[part % 2])
+
+                    for part in range(parts):
+                        if part >= 2:
+                            save(part - 2).wait()
+                        lo_part, hi_part = part * n_qkv, (part + 1) * n_qkv
+                        for g in range(3):
+                            lo, hi = max(lo_part, g * width), min(hi_part, (g + 1) * width)
+                            if lo < hi:
+                                a, b = lo - g * width, hi - g * width
+                                piece = dq[:, :, a:b] if g == 0 else oth[g - 1, :, :, a:b]
+                                st[part % 2, :, lo - lo_part : hi - lo_part] = piece.reshape(tokens, b - a)
+                        save(part).start()
+                    for part in range(parts - 2, parts):
+                        save(part).wait()
+
+                pl.run_scoped(spread, pltpu.VMEM((2, tokens, n_qkv), bf16))
+
+            wide_low = pltpu.VMEM((2, rows, wide), bf16)
+            pl.run_scoped(attention, wide_low)
+
+        pl.run_scoped(
+            second_phase,
+            pltpu.VMEM((width, tokens), bf16),
+            pltpu.VMEM((2, tokens, n_fc), bf16),
+        )
+
+        def third_phase(nt, at_t, pgs, bgs, dn, w, pg2, xs, hg):
+            def qkv_unit(to, plane, store):
+                loads = [
+                    load(src.at[to * grid.ny + y_to], dst.at[y_to], sem + y_to)
+                    for src, dst, sem in ((pg_out, pgs, 0), (bg_out, bgs, 6))
+                    for y_to in range(2)
+                ]
+                for cp in loads:
+                    cp.start()
+                for cp in loads:
+                    cp.wait()
+
+                def body(i, _):
+                    y_to, x_to = i // 2, i % 2
+                    at = pl.ds(pl.multiple_of((2 * x_to + plane) * slab, 16), slab)
+                    term = jnp.concatenate(
+                        [dot_nn(nt[at, :], pgs[y_to]), dot_nn(at_t[at, :], bgs[y_to])], axis=1
+                    )
+                    store(y_to, x_to, beside(term))
+                    return 0
+
+                lax.fori_loop(0, 4, body, 0)
+
+            begin = [load(n1t_in, nt, 2), load(at_in, at_t, 3)]
+            for cp in begin:
+                cp.start()
+            for cp in begin:
+                cp.wait()
+            finish(2 * nz - 2)
+            begin_unit(2 * nz, qkv_unit)
+
+            def fetch(part):
+                s = part % 2
+                return load(wq_in.at[part], w.at[s], 2 + s), load(pg_out.at[part], pg2.at[s], 4 + s)
+
+            late = [pltpu.make_async_copy(x_in, xs, s_st.at[0]), pltpu.make_async_copy(hg_out, hg, s_st.at[1])]
+            for cp in (*late, *fetch(0)):
+                cp.start()
+            dn[...] = jnp.zeros_like(dn)
+
+            def body(part, _):
+                for cp in fetch(part):
+                    cp.wait()
+
+                @pl.when(part + 1 < parts)
+                def _():
+                    for cp in fetch(part + 1):
+                        cp.start()
+
+                dn[...] += dot_nt(pg2[part % 2], w[part % 2])
+
+                @pl.when(part == parts // 2)
+                def _():
+                    second_stage(2 * nz)
+                    begin_unit(2 * nz + 1, qkv_unit)
+
+                return 0
+
+            lax.fori_loop(0, parts, body, 0)
+            for cp in late:
+                cp.wait()
+            sum_ref[6:8, :] = jnp.zeros((2, width), f32)
+
+            def norm(i, _):
+                at = pl.ds(pl.multiple_of(i * chunk, chunk), chunk)
+                values = xs[at, :].astype(f32)
+                grads = dn[at, :]
+                center = values - jnp.mean(values, axis=-1, keepdims=True)
+                factor = lax.rsqrt(jnp.mean(center * center, axis=-1, keepdims=True) + EPS)
+                xhat = center * factor
+                sum_ref[6:7, :] += jnp.sum(grads * xhat, axis=0, keepdims=True)
+                sum_ref[7:8, :] += jnp.sum(grads, axis=0, keepdims=True)
+                scaled = grads * vr_ref[2:3, :]
+                back = factor * (
+                    scaled
+                    - jnp.mean(scaled, axis=-1, keepdims=True)
+                    - xhat * jnp.mean(scaled * xhat, axis=-1, keepdims=True)
+                )
+                total = hg[at, :] + back
+                hg[at, :] = total
+                per = rows // chunk
+                inside = pl.ds(pl.multiple_of(i % per * chunk, chunk), chunk)
+                swap[1, i // per, inside, :width] = total.astype(bf16)
+                return 0
+
+            lax.fori_loop(0, tokens // chunk, norm, 0)
+            give_back(1, swap.at[1], di_out)
+            keep = pltpu.make_async_copy(hg, dx_out, s_st.at[1])
+            keep.start()
+            vec_step(0)
+            tick(2 * nz + 2, qkv_unit)
+            vec_step(1)
+            tick(2 * nz + 3, qkv_unit)
+            vec_step(2)
+            finish(units - 3)
+            finish(units - 2)
+            vec_step(3)
+            keep.wait()
+
+        pl.run_scoped(
+            third_phase,
+            pltpu.VMEM((width, tokens), bf16),
+            pltpu.VMEM((width, tokens), bf16),
+            pltpu.VMEM((2, tokens, n_qkv), bf16),
+            pltpu.VMEM((2, tokens, n_out), bf16),
+            full_rows,
+            pltpu.VMEM((2, width, n_qkv), bf16),
+            pltpu.VMEM((2, tokens, n_qkv), bf16),
+            low_rows,
+            full_rows,
+        )
+        second_stage(units - 1)
+        vec_step(4)
+        finish(units - 1)
+        given_back(1, swap.at[1], di_out)
+        for kind, out in ((0, y_out), (1, di_out)):
+            got_back(kind, swap.at[kind], out)
+        for cp in (*sib(units - 1), *first(units - 1), *second(units - 1)):
+            cp.wait_send()
+        for u in range(units - nz, units - 1):
+            for cp in line(u, 0, True, 0):
+                cp.wait_send()
+
+    any_, vm = pl.BlockSpec(memory_space=pl.ANY), pl.BlockSpec(memory_space=pltpu.VMEM)
+    dma = pltpu.SemaphoreType.DMA
+    halves = (h, n), (cols - h, n)
+    scratch = []
+    for dims in ((2, 2), (2, 2, 2), (2, 2), (2, 2), (), (3,)):
+        scratch += [pltpu.VMEM((*dims, *half), bf16) for half in halves]
+    scratch += [pltpu.VMEM((2, *half), f32) for half in halves]
+    scratch += [pltpu.VMEM((nz - 1, *half), bf16) for half in halves]
+    scratch += [pltpu.VMEM((2, nz + 1, *half), bf16) for half in halves]
+    scratch += [
+        pltpu.VMEM((2, 2, rows, wide), bf16),
+        pltpu.VMEM((5, v_rows, width), f32),
+        pltpu.VMEM((5, v_rows, width), f32),
+        dma((6, units)),
+        dma((6, units)),
+        dma((2, units)),
+        dma((2, 3, nz + 1)),
+        dma((8,)),
+        dma((2,)),
+        dma((6, 2)),
+        dma((2,)),
+        dma((5,)),
+        dma((5,)),
+        dma((2, 2)),
+        dma((2, 2)),
+        dma((2,)),
+        dma((2, 2, 2)),
+    ]
+    shape = jax.ShapeDtypeStruct
+    return pl.pallas_call(
+        kernel,
+        out_shape=[
+            *[shape((cols, n), f32)] * 3,
+            shape((v_rows, width), f32),
+            shape((2, rows, wide), bf16),
+            shape((2, rows, wide), bf16),
+            shape((tokens, width), f32),
+            shape((tokens, width), f32),
+            shape((parts, tokens, n_out), bf16),
+            shape((parts, tokens, n_qkv), bf16),
+            shape((parts, tokens, n_fc), bf16),
+        ],
+        in_specs=[any_] * 19 + [vm] * 4,
+        out_specs=[any_] * 3 + [vm] + [any_] * 7,
+        scratch_shapes=scratch,
+        compiler_params=pltpu.CompilerParams(
+            collective_id=5, has_side_effects=True, vmem_limit_bytes=60 * 1024 * 1024
+        ),
+        cost_estimate=cost(60e9, 200e6),
+        name="backward",
+    )(
+        grad, proj_terms, act, slope, w_proj, hidden, normed_t, w_fc, w_out, queries, keys, values, other,
+        att_full, logs, x_in, first_t, att_t, w_qkv, vec_rows, seg_row, seg_col, seg_other,
+    )
 
 
 def pick(array, index, axis):
@@ -1345,18 +2231,18 @@
         return [v.reshape(-1) for v in spread]
 
     if paired:
-        layer_input, grad_out = grid.by_sequence(layer_input), grid.by_sequence(grad_out)
         extra = 1 - grid.core
         chip_seg = pick(seg_blocks, grid.x, 0)
         seg_own = jnp.stack([pick(chip_seg, grid.core, 0), pick(chip_seg, 3 - grid.core, 0)])
         seg_other = jnp.stack([pick(chip_seg, extra, 0), pick(chip_seg, 3 - extra, 0)])
         packed = jnp.concatenate(vectors).astype(f32)[None]
         (
-            w_qkv, w_out, w_fc, w_proj, packed, inner, activated, other,
-            normed1, queries, keys, vals, attended, attended_f32, log_total, hidden, normed2,
+            w_qkv, w_out, w_fc, w_proj, packed, slope, activated, other, x_seq, grad_seq, normed1_t, normed2_t, attended_t,
+            proj_terms, queries, keys, vals, attended_f32, log_total, hidden,
         ) = forward_gather(
             grid,
             layer_input,
+            grad_out,
             (qkv_weight, out_weight, fc_weight, proj_weight.T),
             jnp.broadcast_to(packed, (8, packed.shape[1])),
             seg_own[:, :, None],
@@ -1367,10 +2253,6 @@
         w_qkv = w_qkv.reshape(parts, width, n_qkv)
         w_fc = w_fc.reshape(parts, width, n_fc)
         w_proj = w_proj.reshape(groups, width, hidden_slab)
-        out_full = w_out.reshape(parts, width, n_out).transpose(1, 0, 2).reshape(width, width)
-        normed1, normed2, hidden = (v.reshape(tokens, width) for v in (normed1, normed2, hidden))
-        attended = attended[:, :, :width].reshape(tokens, width)
-        values = layer_input.reshape(tokens, width).astype(f32)
     else:
         packed = lax.all_gather(jnp.concatenate(vectors), "dp", axis=0)
         fcb, q_all, v_all, ob_all, pb_all, g1, b1, g2, b2 = unpack(packed)
@@ -1401,12 +2283,6 @@
         hidden = values + jnp.dot(attended, out_full, preferred_element_type=f32) + ob_all
         normed2 = layer_norm(hidden, g2, b2).astype(bf16)
         inner, activated = feed_in(normed2, w_fc, fcb.reshape(parts, 1, n_fc), groups)
-    output = feed_out(activated, w_proj, hidden, pb_all[None])
-
-    mlp_grad = grad_out.reshape(tokens, width)
-    cotangent = mlp_grad.astype(f32)
-    proj_bias_grad = jnp.sum(cotangent, axis=0)
-    inner_grad, fc_bias_grad = feed_back(mlp_grad, w_proj, inner, parts)
 
     def tall_cut(size):
         return (size // 2 + 15) // 16 * 16
@@ -1459,55 +2335,96 @@
             return lax.psum_scatter(whole, ("ctx", "dp"), scatter_dimension=0).astype(f32)
         return summed_grads(grid, 1, [left.T, right], by_rows, (cols, f), tall_cut(cols), "rs_proj")
 
-    proj_weight_grad = reduced_proj(mlp_grad, activated).T
-    (fc_weight_grad,) = reduced([(normed2, inner_grad)], 2, "rs_fc")
-
-    normed2_grad = back_project(inner_grad, w_fc)
-    norm2_out, norm2_pull = jax.vjp(layer_norm, hidden, g2, b2)
-    hidden_ln, g2_grad, b2_grad = norm2_pull(normed2_grad)
-    hidden_grad = cotangent + hidden_ln
-    branch_grad = hidden_grad.astype(bf16)
-    out_bias_grad = jnp.sum(branch_grad, axis=0, dtype=f32)
-    attended_grad = jnp.einsum(
-        "nd,ed->ne", branch_grad, out_full, preferred_element_type=f32
-    ).astype(bf16)
-    branch_parts = branch_grad.reshape(tokens, parts, n_out).transpose(1, 0, 2)
-
-    attended_grad = attended_grad.reshape(seqs, rows, width)
     if paired:
-        query_grad, own_grad, other_grad = chip_attention_back(
-            extra.astype(jnp.int32)[None],
+        proj_halves, fc_halves, last_halves, sums, output, far, near, *_ = backward_sums(
+            grid,
+            grad_seq.reshape(tokens, width),
+            proj_terms,
+            activated,
+            slope,
+            w_proj,
+            hidden.reshape(tokens, width),
+            normed2_t,
+            w_fc,
+            w_out.reshape(parts, width, n_out),
             queries,
             keys,
             vals,
             other,
-            attended_grad,
             attended_f32,
             log_total,
+            x_seq.reshape(tokens, width),
+            normed1_t,
+            attended_t,
+            w_qkv,
+            jnp.stack([pb_all, g2, g1] + [jnp.zeros_like(g1)] * 5),
             seg_own[:, None, :],
             seg_own[:, :, None],
             seg_other[:, :, None],
         )
-        pair_grad = add_low(own_grad, grid.swap_core(other_grad))
+        proj_weight_grad = proj_halves.T
+        fc_weight_grad = jnp.concatenate([fc_halves[:, :n_fc], fc_halves[:, n_fc:]], axis=0)
+        last = jnp.concatenate([last_halves[:, :n_fc], last_halves[:, n_fc:]], axis=0)
+        qkv_weight_grad, out_weight_grad = last[:, :n_qkv], last[:, n_qkv:]
+        far = far[:, :, :width].astype(f32)
+        near = near.reshape(2, rows, width)
+        stays = (grid.x == 0) & (jnp.arange(2) == 0)
+        input_grad = jnp.where(stays[:, None, None], near, far)
+        own = pick(sums[:8].reshape(8, parts, n_out), grid.d, 1)
+        fc_own = pick(sums[8:, :n_fc], grid.d, 0)
+        return (
+            output[:, :, :width],
+            input_grad,
+            qkv_weight_grad,
+            own[4],
+            own[5],
+            out_weight_grad,
+            own[1],
+            fc_weight_grad,
+            fc_own,
+            proj_weight_grad,
+            own[0],
+            own[6],
+            own[7],
+            own[2],
+            own[3],
+        )
     else:
+        mlp_grad = grad_out.reshape(tokens, width)
+        cotangent = mlp_grad.astype(f32)
+        output = feed_out(activated, w_proj, hidden, pb_all[None])
+        proj_bias_grad = jnp.sum(cotangent, axis=0)
+        inner_grad, fc_bias_grad = feed_back(mlp_grad, w_proj, inner, parts)
+        proj_weight_grad = reduced_proj(mlp_grad, activated).T
+        (fc_weight_grad,) = reduced([(normed2, inner_grad)], 2, "rs_fc")
+        normed2_grad = back_project(inner_grad, w_fc)
+        norm2_out, norm2_pull = jax.vjp(layer_norm, hidden, g2, b2)
+        hidden_ln, g2_grad, b2_grad = norm2_pull(normed2_grad)
+        hidden_grad = cotangent + hidden_ln
+        branch_grad = hidden_grad.astype(bf16)
+        out_bias_grad = jnp.sum(branch_grad, axis=0, dtype=f32)
+        attended_grad = jnp.einsum(
+            "nd,ed->ne", branch_grad, out_full, preferred_element_type=f32
+        ).astype(bf16)
+        branch_parts = branch_grad.reshape(tokens, parts, n_out).transpose(1, 0, 2)
         query_grad, pairs_grad = attention_backward(
             bounds,
             queries,
             pairs_full,
             seg_blocks[:, :, :, None],
             seg_mine[:, None, :],
-            attended_grad,
+            attended_grad.reshape(seqs, rows, width),
             attended_f32,
             log_total,
         )
         pair_grad = lax.psum_scatter(pairs_grad, "ctx", scatter_dimension=0)
-    pair_grad = pair_grad.reshape(2, tokens, width)
-    projected_grad = jnp.concatenate(
-        [query_grad.reshape(tokens, width), pair_grad[0], pair_grad[1]], axis=1
-    )
-    q_bias_grad = jnp.sum(query_grad.reshape(tokens, width), axis=0, dtype=f32)
-    v_bias_grad = jnp.sum(pair_grad[1], axis=0, dtype=f32)
-    by_part = projected_grad.reshape(tokens, parts, n_qkv).transpose(1, 0, 2)
+        pair_grad = pair_grad.reshape(2, tokens, width)
+        projected_grad = jnp.concatenate(
+            [query_grad.reshape(tokens, width), pair_grad[0], pair_grad[1]], axis=1
+        )
+        q_bias_grad = jnp.sum(query_grad.reshape(tokens, width), axis=0, dtype=f32)
+        v_bias_grad = jnp.sum(pair_grad[1], axis=0, dtype=f32)
+        by_part = projected_grad.reshape(tokens, parts, n_qkv).transpose(1, 0, 2)
     out_weight_grad, qkv_weight_grad = reduced(
         [(attended, branch_parts), (normed1, by_part)], 3, "rs_qkv"
     )
@@ -1517,9 +2434,6 @@
     input_grad = hidden_grad + values_ln
 
     output, input_grad = (v.reshape(seqs, rows, width) for v in (output, input_grad))
-    if paired:
-        output, input_grad = grid.by_position(output), grid.by_position(input_grad)
-
     sums = [
         fc_bias_grad,
         q_bias_grad,

time: 1070 us -> 761 us (0.71)
  Pallas kernels: 829 us -> 719 us
  local copies, waits for them, and re-layouts: 128 us -> 24.4 us
  other arithmetic: 44.4 us -> 5.99 us
  waiting for transfers between devices: 29.8 us -> 0 us
  between operations: 15.2 us -> 1.35 us
  starting transfers between devices: 13.7 us -> 0 us
    pallas_call x9 -> x2, Pallas kernels: 829 us -> 719 us  [the longest x1 385 us: backward_sums(): pl.pallas_call(kernel, out_shape=[*[shape((cols, n), f32)] * 3, shape((v_...]
    reshape x19 -> x1, local copies, waits for them, and re-layouts: 44.4 us -> 0.09 us  [on_device(): own = pick(sums[:8].reshape(8, parts, n_out), grid.d, 1)]
    ppermute x9 -> x0, waiting for transfers between devices: 29.8 us -> none  [the longest x2 29.8 us: by_sequence(): across = lax.ppermute(pick(v, 1 - self.x, 0), 'ctx', self.ACROSS)]
    reduce_sum x14 -> x0, other arithmetic: 19.6 us -> none  [the longest x5 12.8 us: layer_norm(): return center * factor * gain + shift]
    pallas_call x3 -> x0, local copies, waits for them, and re-layouts: 15.1 us -> none  [the longest x2 9.39 us: back_project(): pl.pallas_call(kernel, grid=(parts,), in_specs=[pl.BlockSpec((1, tokens,...]
    ppermute x9 -> x0, starting transfers between devices: 13.7 us -> none  [the longest x2 4.26 us: by_sequence(): across = lax.ppermute(pick(v, 1 - self.x, 0), 'ctx', self.ACROSS)]
    squeeze x4 -> x0, local copies, waits for them, and re-layouts: 11.3 us -> none  [the longest x2 4.08 us: by_sequence(): within = lax.ppermute(v[1], 'ctx', self.WITHIN)]
  transfers between devices with their start and end apart: 10 -> 0, of which waited for: 2 -> 0; matrix products, arithmetic and copies ran while one was open for 10% -> 0% of each run, Pallas kernels for 41% -> 0%
where the time goes in v3:
time: 761 us; the launch traced here: 750 us
  Pallas kernels  719 us (94%)
  local copies, waits for them, and re-layouts  24.4 us (3%)
    pallas_call x1, Pallas kernels, backward_sums(): pl.pallas_call(kernel, out_shape=[*[shape((cols, n), f32)] * 3, shape((v_...  385 us
    pallas_call x1, Pallas kernels, forward_gather(): pl.pallas_call(kernel, out_shape=out_shape, in_specs=[any_] * 7 + [vm] *...  334 us

profile of v3, /device:TPU:0, one launch (start us, length us, event | category | flops | bytes accessed | tf_op | source)
XLA Modules:
  0.0 750.2 jit_solution(15345456138952154969)
XLA Ops:
  0.7 0.7 reshape.149
  1.4 0.9 copy.40.sc_ref.ck_ref
  2.3 0.6 broadcast_in_dim.31.sr_ref.rq_ref
  2.9 0.6 broadcast_in_dim.32.so_ref
  3.5 3.5 copy.38.x_own
  7.0 0.0 copy-done
  7.0 0.0 copy-start.6
  7.0 0.0 copy-start.7
  7.0 0.0 copy-start.8
  7.1 0.0 copy-start.9
  7.1 0.0 copy-start.10
  7.1 0.0 copy-start.11
  7.1 0.0 copy-start.12
  7.1 2.5 copy.39.g_own
  9.6 0.0 copy-done.4
  9.6 0.0 copy-done.5
  9.6 0.0 copy-done.6
  9.6 0.0 copy-done.7
  9.6 0.0 copy-done.8
  9.7 0.0 copy-done.9
  9.7 0.0 copy-done.10
  9.7 0.0 copy-done.11
  9.7 0.0 copy-done.12
  9.7 0.1 concatenate.13
  9.8 0.6 broadcast_in_dim.29.vec_in
  10.4 333.5 %forward.1 = (bf16[4,2,2,2,400,600]{5,4,3,2,1,0:T(8,128)(2,1)}, bf16[4,2,2,2,400,200]{5,4,3,2,1,0:T(8,128)(2,1)}, bf16[4,2,2,2,400,800]{5,4,3,2,1,0:T(8,128)(2,1...) custom-call(bf16[2,256,1600]{2,1,0:T(8,128)(2,1)} %copy.38.x_own, ...), custom_call_target="tpu_custom_call" | custom-call | flops 30000001024 | bytes 150000000 | tf_op jit(solution)/shard_map/forward/pallas_call | solution.py:1280
  344.0 1.3 slice_reduce_fusion
  345.3 0.1 reshape_squeeze.3
  345.4 0.1 fusion.9
  345.4 0.1 stack_reshape.10
  345.5 0.1 stack_reshape.11
  345.6 0.1 stack_reshape.9
  345.8 0.7 stack.19.vr_ref
  346.4 0.9 copy.42.cs_ref
  347.3 385.0 %backward.1 = (f32[200,1600]{1,0:T(8,128)}, f32[200,1600]{1,0:T(8,128)}, f32[200,1600]{1,0:T(8,128)}, f32[16,1600]{1,0:T(8,128)}, bf16[2,256,1664]{2,1,0:T(8,128...) custom-call(bf16[512,1600]{1,0:T(8,128)(2,1)} %bitcast.49, ...), custom_call_target="tpu_custom_call" | custom-call | flops 60000002048 | bytes 200000000 | tf_op jit(solution)/shard_map/backward/pallas_call | solution.py:2126
  732.3 1.6 fusion.7
  733.9 1.2 pad_maximum_fusion
  735.1 0.6 copy-done.1
  735.7 0.2 fusion.8
  735.9 0.9 pad_maximum_fusion.1
  736.9 1.0 fusion
  737.9 2.8 convert_select_fusion
  740.7 2.9 copy.44
  743.7 3.7 copy.43
  747.4 0.1 reshape.158
  747.5 0.6 constant_dynamic-slice_fusion.7
  748.1 0.6 dynamic-slice_reduce_fusion
  748.7 1.1 copy.47
  (15 shorter events, 0.1 us)
Async XLA Ops:
  2.3 4.7 copy-start
  7.0 2.6 copy-start.4
  7.0 2.6 copy-start.5
  7.0 2.6 copy-start.6
  7.0 2.6 copy-start.7
  7.0 2.6 copy-start.8
  7.1 2.6 copy-start.9
  7.1 2.6 copy-start.10
  7.1 2.6 copy-start.11
  7.1 2.6 copy-start.12
  733.9 1.8 copy-start.1
  743.7 3.7 copy-start.3
  743.7 5.0 copy-start.2

commit v4 on v3

--- a/solution.py
+++ b/solution.py
@@ -1773,7 +1773,7 @@
 
                     dn[...] += dot_nt(ig2[part % 2], w[part % 2])
 
-                    @pl.when(part == parts // 2)
+                    @pl.when(part == parts * 3 // 4)
                     def _():
                         tick(nz + 1, fc_unit)
 
@@ -1916,11 +1916,11 @@
                             for kind in range(2):
                                 own[kind, slot, :, lanes] = got_own[slot][kind]
                                 oth[kind, slot, :, lanes] = got_oth[slot][kind].astype(bf16)
-                        @pl.when(p == 3)
+                        @pl.when(p == 5)
                         def _():
                             tick(nz + 3, fc_unit)
 
-                        @pl.when(p == 8)
+                        @pl.when(p == 10)
                         def _():
                             finish(2 * nz - 3)
                             second_stage(2 * nz - 1)

time: 761 us -> 764 us (level)
  no operation moved by 1% of the time
where the time goes in v4:
time: 764 us; the launch traced here: 753 us
  Pallas kernels  721 us (94%)
  local copies, waits for them, and re-layouts  24.4 us (3%)
    pallas_call x1, Pallas kernels, backward_sums(): pl.pallas_call(kernel, out_shape=[*[shape((cols, n), f32)] * 3, shape((v_...  388 us
    pallas_call x1, Pallas kernels, forward_gather(): pl.pallas_call(kernel, out_shape=out_shape, in_specs=[any_] * 7 + [vm] *...  334 us

profile of v4, /device:TPU:0, one launch (start us, length us, event | category | flops | bytes accessed | tf_op | source)
XLA Modules:
  0.0 753.1 jit_solution(6841694000637122630)
XLA Ops:
  0.7 0.7 reshape.149
  1.4 0.9 copy.40.sc_ref.ck_ref
  2.3 0.6 broadcast_in_dim.31.sr_ref.rq_ref
  2.9 0.6 broadcast_in_dim.32.so_ref
  3.5 3.5 copy.38.x_own
  7.0 0.0 copy-done
  7.0 0.0 copy-start.6
  7.0 0.0 copy-start.7
  7.0 0.0 copy-start.8
  7.1 0.0 copy-start.9
  7.1 0.0 copy-start.10
  7.1 0.0 copy-start.11
  7.1 0.0 copy-start.12
  7.1 2.5 copy.39.g_own
  9.6 0.0 copy-done.4
  9.6 0.0 copy-done.5
  9.6 0.0 copy-done.6
  9.6 0.0 copy-done.7
  9.6 0.0 copy-done.8
  9.7 0.0 copy-done.9
  9.7 0.0 copy-done.10
  9.7 0.0 copy-done.11
  9.7 0.0 copy-done.12
  9.7 0.1 concatenate.13
  9.8 0.6 broadcast_in_dim.29.vec_in
  10.4 333.5 %forward.1 = (bf16[4,2,2,2,400,600]{5,4,3,2,1,0:T(8,128)(2,1)}, bf16[4,2,2,2,400,200]{5,4,3,2,1,0:T(8,128)(2,1)}, bf16[4,2,2,2,400,800]{5,4,3,2,1,0:T(8,128)(2,1...) custom-call(bf16[2,256,1600]{2,1,0:T(8,128)(2,1)} %copy.38.x_own, ...), custom_call_target="tpu_custom_call" | custom-call | flops 30000001024 | bytes 150000000 | tf_op jit(solution)/shard_map/forward/pallas_call | solution.py:1280
  344.0 1.3 slice_reduce_fusion
  345.3 0.1 reshape_squeeze.3
  345.4 0.1 fusion.9
  345.4 0.1 stack_reshape.10
  345.5 0.1 stack_reshape.11
  345.6 0.1 stack_reshape.9
  345.8 0.7 stack.19.vr_ref
  346.4 0.9 copy.42.cs_ref
  347.3 387.9 %backward.1 = (f32[200,1600]{1,0:T(8,128)}, f32[200,1600]{1,0:T(8,128)}, f32[200,1600]{1,0:T(8,128)}, f32[16,1600]{1,0:T(8,128)}, bf16[2,256,1664]{2,1,0:T(8,128...) custom-call(bf16[512,1600]{1,0:T(8,128)(2,1)} %bitcast.49, ...), custom_call_target="tpu_custom_call" | custom-call | flops 60000002048 | bytes 200000000 | tf_op jit(solution)/shard_map/backward/pallas_call | solution.py:2126
  735.2 1.6 fusion.7
  736.8 1.2 pad_maximum_fusion
  738.0 0.6 copy-done.1
  738.6 0.2 fusion.8
  738.9 0.9 pad_maximum_fusion.1
  739.8 1.0 fusion
  740.8 2.8 convert_select_fusion
  743.6 2.9 copy.44
  746.6 3.7 copy.43
  750.3 0.1 reshape.158
  750.4 0.6 constant_dynamic-slice_fusion.7
  751.0 0.6 dynamic-slice_reduce_fusion
  751.6 1.1 copy.47
  (15 shorter events, 0.1 us)
Async XLA Ops:
  2.3 4.7 copy-start
  7.0 2.6 copy-start.4
  7.0 2.6 copy-start.5
  7.0 2.6 copy-start.6
  7.0 2.6 copy-start.7
  7.0 2.6 copy-start.8
  7.1 2.6 copy-start.9
  7.1 2.6 copy-start.10
  7.1 2.6 copy-start.11
  7.1 2.6 copy-start.12
  736.8 1.8 copy-start.1
  746.6 3.7 copy-start.3
  746.6 5.0 copy-start.2
